TPU v7x, 128 devices: a whole 4x4x4 slice. The times are simulated.
128 devices in a mesh: dp: 2 (over core), expert: 64 (over y, x, z).
Axes of the slice: x: 4, y: 4, z: 4, core: 2. Of those that a mesh axis runs over, the one named last changes fastest.
Arguments:
- tokens: bfloat16 [16384, 2048], P(('dp', 'expert')), may hold values from -6 to 6
- cotangent: bfloat16 [16384, 2048], P(('dp', 'expert')), may hold values from -6 to 6
- routes: int32 [16384, 2], P(('dp', 'expert')), may hold values from 0 to 15, all different within a row; in each aligned block of 128 rows (0 to 127, 128 to 255, ...) at most 24 rows name the same one
- gates: float32 [16384, 2], P(('dp', 'expert')), may hold values from 0.1 to 1
- capacity: int32 [16], replicated, may hold values from 13 to 24, as said below
- layout: int32 [64], replicated, may hold values from 0 to 63, each once
- partner: int32 [64], replicated, may hold values from 0 to 63, as said below
- w_in: float32 [64, 2048, 256], P('expert'), may hold values from -0.125 to 0.125
- w_out: float32 [64, 256, 2048], P('expert'), may hold values from -0.1875 to 0.1875
- m_in: bfloat16 [64, 2048, 256], P('expert'), may hold values from -5 to 5
- v_in: bfloat16 [64, 2048, 256], P('expert'), may hold values from 0.099609375 to 4
- m_out: bfloat16 [64, 256, 2048], P('expert'), may hold values from -5 to 5
- v_out: bfloat16 [64, 256, 2048], P('expert'), may hold values from 0.099609375 to 4
Outputs:
- mixed: bfloat16 [16384, 2048], P(('dp', 'expert'))
- token_grad: bfloat16 [16384, 2048], P(('dp', 'expert'))
- new_w_in: float32 [64, 2048, 256], P('expert')
- new_w_out: float32 [64, 256, 2048], P('expert')
- new_m_in: bfloat16 [64, 2048, 256], P('expert')
- new_v_in: bfloat16 [64, 2048, 256], P('expert')
- new_m_out: bfloat16 [64, 256, 2048], P('expert')
- new_v_out: bfloat16 [64, 256, 2048], P('expert')
Inputs may be any that keep to these rules, and one draw needn't show every extreme that they name: `routes`: in the rows of one device no expert is named by more than 24 pairs, a bound that some block reaches; each token names 2 different experts. `capacity`: some expert has exactly 24 and some other exactly that minimum. `layout`: A permutation. partner[d] is d or the index half the expert axis away, and partner[partner[d]] = d; both kinds occur.
All inputs are finite; a program needn't handle non-finite values.
Results may differ from a plain program's by a relative error of at most 0.0079.
Values may be sent and summed in bfloat16 or wider, within the bound.
A program may use at most 128 MiB of HBM per device.

v0:
```python
import jax
import jax.numpy as jnp
from jax import lax
from jax.sharding import PartitionSpec as P

GROUP = 4


def from_partner(block, axis, bit):
    count = lax.axis_size(axis)
    route = []
    for low in range(count):
        high = low | 1 << bit
        if high != low and high < count:
            route += [(low, high), (high, low)]
    return lax.ppermute(block, axis, route)


def gelu_tanh(value):
    return jax.nn.gelu(value, approximate=True)


def adamw(weight, first, second, grad):
    first_f = 0.9 * first.astype(jnp.float32) + 0.1 * grad
    second_f = 0.999 * second.astype(jnp.float32) + 0.001 * grad * grad
    corrected = first_f / (1.0 - 0.9**10) / (jnp.sqrt(second_f / (1.0 - 0.999**10)) + 1e-08)
    updated = weight - 0.01 * (corrected + 0.1 * weight)
    return (updated, first_f.astype(jnp.bfloat16), second_f.astype(jnp.bfloat16))


def local(
    tokens,
    cotangent,
    routes,
    gates,
    capacity,
    layout,
    partner,
    w_in,
    w_out,
    m_in,
    v_in,
    m_out,
    v_out,
):
    width = tokens.shape[1]
    count = tokens.shape[0]
    topk = routes.shape[1]
    experts = capacity.shape[0]
    slots = 3 * count * topk // (2 * experts)
    nexp = lax.axis_size("expert")
    here = lax.axis_index("expert")
    far_bit = (nexp // 2).bit_length() - 1
    moved = jnp.take(partner, here) != here
    flat_routes = routes.reshape(-1)
    onehot = (flat_routes[:, None] == jnp.arange(experts, dtype=jnp.int32)[None, :]).astype(
        jnp.int32
    )
    position = jnp.sum((jnp.cumsum(onehot, 0) - 1) * onehot, 1)
    limit = jnp.sum(onehot * capacity[None, :], 1)
    slot = jnp.where(position < limit, flat_routes * slots + position, experts * slots)
    x_rows = jnp.repeat(tokens, topk, axis=0)
    scaled = (
        gates.reshape(-1)[:, None] * jnp.repeat(cotangent, topk, axis=0).astype(jnp.float32)
    ).astype(jnp.bfloat16)

    def build(rows):
        filled = jnp.zeros((experts * slots + 1, width), jnp.bfloat16).at[slot].set(rows)
        return filled[:-1].reshape(experts, slots, width)

    x_buf = build(x_rows)
    g_buf = build(scaled)
    weight_in, weight_out = (w_in[0], w_out[0])
    first_in, second_in, first_out, second_out = (m_in[0], v_in[0], m_out[0], v_out[0])
    held = jnp.take(layout, partner, axis=0)
    other_w = (
        from_partner(weight_in.astype(jnp.bfloat16), "expert", far_bit).astype(weight_in.dtype),
        from_partner(weight_out.astype(jnp.bfloat16), "expert", far_bit).astype(weight_out.dtype),
    )
    other_m = from_partner((first_in, second_in, first_out, second_out), "expert", far_bit)
    weight_in = jnp.where(moved, other_w[0], weight_in)
    weight_out = jnp.where(moved, other_w[1], weight_out)
    first_in = jnp.where(moved, other_m[0], first_in)
    second_in = jnp.where(moved, other_m[1], second_in)
    first_out = jnp.where(moved, other_m[2], first_out)
    second_out = jnp.where(moved, other_m[3], second_out)
    target_expert = held // GROUP
    send_x = jnp.take(x_buf, target_expert, axis=0)
    send_g = jnp.take(g_buf, target_expert, axis=0)
    recv_x, recv_g = (
        lax.all_to_all(send_x, "expert", split_axis=0, concat_axis=0, tiled=True),
        lax.all_to_all(send_g, "expert", split_axis=0, concat_axis=0, tiled=True),
    )
    rows = recv_x.reshape(-1, width)
    grows = recv_g.reshape(-1, width)
    wb_in = weight_in.astype(jnp.bfloat16)
    wb_out = weight_out.astype(jnp.bfloat16)
    pre = jnp.dot(rows, wb_in, preferred_element_type=jnp.float32)
    hidden, pull = jax.vjp(gelu_tanh, pre)
    hidden = hidden.astype(jnp.bfloat16)
    part = jnp.dot(hidden, wb_out, preferred_element_type=jnp.float32).astype(jnp.bfloat16)
    dhid = lax.dot_general(
        grows, wb_out, (((1,), (1,)), ((), ())), preferred_element_type=jnp.float32
    )
    dpre = pull(dhid)[0].astype(jnp.bfloat16)
    xpart = lax.dot_general(
        dpre, wb_in, (((1,), (1,)), ((), ())), preferred_element_type=jnp.float32
    ).astype(jnp.bfloat16)
    grad_in = lax.dot_general(
        rows, dpre, (((0,), (0,)), ((), ())), preferred_element_type=jnp.float32
    )
    grad_out = lax.dot_general(
        hidden, grows, (((0,), (0,)), ((), ())), preferred_element_type=jnp.float32
    )
    back_part, back_dx = (
        lax.all_to_all(
            part.reshape(nexp, slots, width), "expert", split_axis=0, concat_axis=0, tiled=True
        ),
        lax.all_to_all(
            xpart.reshape(nexp, slots, width), "expert", split_axis=0, concat_axis=0, tiled=True
        ),
    )
    grad_in, grad_out = lax.psum((grad_in, grad_out), "dp")
    new_w_in, new_m_in, new_v_in = adamw(weight_in, first_in, second_in, grad_in)
    new_w_out, new_m_out, new_v_out = adamw(weight_out, first_out, second_out, grad_out)
    owners = (target_expert[:, None] == jnp.arange(experts, dtype=jnp.int32)[None, :]).astype(
        jnp.bfloat16
    )
    out_sum = jnp.einsum("je,jcd->ecd", owners, back_part, preferred_element_type=jnp.float32)
    dx_sum = jnp.einsum("je,jcd->ecd", owners, back_dx, preferred_element_type=jnp.float32)
    blank = jnp.zeros((1, width), jnp.float32)
    out_vals = jnp.take(jnp.concatenate([out_sum.reshape(-1, width), blank]), slot, axis=0)
    dx_vals = jnp.take(jnp.concatenate([dx_sum.reshape(-1, width), blank]), slot, axis=0)
    mixed = jnp.sum(out_vals.reshape(count, topk, width) * gates[:, :, None], axis=1).astype(
        jnp.bfloat16
    )
    token_grad = jnp.sum(dx_vals.reshape(count, topk, width), axis=1).astype(jnp.bfloat16)
    return (
        mixed,
        token_grad,
        new_w_in[None],
        new_w_out[None],
        new_m_in[None],
        new_v_in[None],
        new_m_out[None],
        new_v_out[None],
    )


def solution(mesh):
    in_specs = (
        P(("dp", "expert"), None),
        P(("dp", "expert"), None),
        P(("dp", "expert"), None),
        P(("dp", "expert"), None),
        P(),
        P(),
        P(),
        P("expert", None, None),
        P("expert", None, None),
        P("expert", None, None),
        P("expert", None, None),
        P("expert", None, None),
        P("expert", None, None),
    )
    out_specs = (
        P(("dp", "expert"), None),
        P(("dp", "expert"), None),
        P("expert", None, None),
        P("expert", None, None),
        P("expert", None, None),
        P("expert", None, None),
        P("expert", None, None),
        P("expert", None, None),
    )
    return jax.shard_map(local, mesh=mesh, in_specs=in_specs, out_specs=out_specs, check_vma=False)
```

profile of v0, /device:TPU:76, one launch (start us, length us, event | category | flops | bytes accessed | tf_op | source)
XLA Modules:
  0.0 615.1 jit_solution(6039829521313351921)
XLA Ops:
  10.9 2.1 broadcast_in_dim.74
  13.1 2.4 convert_element_type.87
  15.6 3.7 scatter_custom_fusion.1
  22.8 4.2 scatter_custom_fusion
  27.0 1.5 slice.32
  28.5 3.5 gather_fusion.3
  32.1 3.6 gather_fusion.1
  35.7 8.4 %broadcast_select_fusion = (bf16[64,24,2048]{2,1,0:T(8,128)(2,1)}, bf16[64,24,2048]{2,1,0:T(8,128)(2,1)S(1)}) fusion(bf16[64,24,2048]{2,1,0:T(8,128)(2,1)} %gather_fusion.3, pred[64]{0:T(512)(128)(4,1)S(1)} %get-tuple-element.27, bf16[64,24,2048]{2,1,0:T(8,128)(2,1)} %gather_fusion.1), kind=kLoop, calls=%fused_computation.13 | loop fusion | flops 6291456 | bytes 25165888 | tf_op jit(solution)/shard_map/jit(_take)/select_n | solution.py:89
  44.1 80.8 %all_to_all.20 = bf16[64,24,2048]{2,1,0:T(8,128)(2,1)} all-to-all(bf16[64,24,2048]{2,1,0:T(8,128)(2,1)S(1)} %get-tuple-element.38), channel_id=1, replica_groups=mesh['dp'=2,'expert'=64] {'expert'}, dimensions={0} | all-to-all | bytes 12582912 | tf_op jit(solution)/shard_map/all_to_all | solution.py:91
  124.9 9.9 %all-to-all-start.2 = ((bf16[64,24,2048]{2,1,0:T(8,128)(2,1)}), bf16[64,24,2048]{2,1,0:T(8,128)(2,1)}, u32[]{:S(2)}, u32[]{:S(2)}) async-start(bf16[64,24,2048]{2,1,0:T(8,128)(2,1)} %get-tuple-element.37), calls=%async_computation.2 | async-start | bytes 12582912 | tf_op jit(solution)/shard_map/all_to_all | solution.py:92
  134.8 2.8 bitcast_convert_fusion.1
  137.6 2.3 collective-permute-start
  141.1 1.5 collective-permute-start.1
  143.8 92.0 %collective-permute-done = bf16[2048,256]{1,0:T(8,128)(2,1)S(1)} collective-permute-done((bf16[2048,256]{1,0:T(8,128)(2,1)}, bf16[2048,256]{1,0:T(8,128)(2,1)S(1)}, u32[]{:S(2)}, u32[]{:S(2)}) %collective-permute-start) | collective-permute-done | bytes 1048608 | tf_op jit(solution)/shard_map/ppermute | solution.py:16
  235.8 2.3 fusion.13
  238.1 18.5 %collective-permute-done.1 = bf16[256,2048]{1,0:T(8,128)(2,1)} collective-permute-done((bf16[256,2048]{1,0:T(8,128)(2,1)}, bf16[256,2048]{1,0:T(8,128)(2,1)}, u32[]{:S(2)}, u32[]{:S(2)}) %collective-permute-start.1) | collective-permute-done | bytes 1048608 | tf_op jit(solution)/shard_map/ppermute | solution.py:16
  256.6 1.5 fusion.14
  258.2 5.8 fusion.37
  264.0 6.0 fusion.12
  270.0 4.4 convolution_convert_fusion
  274.4 9.5 %all-to-all-start.3 = ((bf16[64,24,2048]{2,1,0:T(8,128)(2,1)}), bf16[64,24,2048]{2,1,0:T(8,128)(2,1)}, u32[]{:S(2)}, u32[]{:S(2)}) async-start(bf16[64,24,2048]{2,1,0:T(8,128)(2,1)} %bitcast.83), calls=%async_computation.3 | async-start | bytes 12582912 | tf_op jit(solution)/shard_map/all_to_all | solution.py:119
  284.4 6.6 %fusion.36 = f32[256,2048]{1,0:T(8,128)} fusion(bf16[1536,2048]{1,0:T(8,128)(2,1)} %bitcast.14, f32[1536,256]{1,0:T(8,128)} %fusion.37), kind=kOutput, calls=%fused_computation.90 | convolution fusion | flops 1614151680 | bytes 9961472 | tf_op jit(solution)/shard_map/dot_general | solution.py:112
  291.0 6.0 fusion.38
  297.0 6.0 convolution_convert_fusion.1
  303.0 61.0 %all-to-all-done.3 = bf16[64,24,2048]{2,1,0:T(8,128)(2,1)} async-done(((bf16[64,24,2048]{2,1,0:T(8,128)(2,1)}), bf16[64,24,2048]{2,1,0:T(8,128)(2,1)}, u32[]{:S(2)}, u32[]{:S(2)}) %all-to-all-start.3) | async-done | bytes 6291488 | tf_op jit(solution)/shard_map/all_to_all | solution.py:119
  364.1 17.3 %all-to-all-start.1 = ((bf16[64,24,2048]{2,1,0:T(8,128)(2,1)}), bf16[64,24,2048]{2,1,0:T(8,128)(2,1)}, u32[]{:S(2)}, u32[]{:S(2)}) async-start(bf16[64,24,2048]{2,1,0:T(8,128)(2,1)} %bitcast.82), calls=%async_computation.1 | async-start | bytes 12582912 | tf_op jit(solution)/shard_map/all_to_all | solution.py:116
  381.4 2.4 collective-permute-start.4
  383.8 1.2 collective-permute-start.5
  385.0 2.3 collective-permute-start.2
  387.3 1.4 collective-permute-start.3
  388.7 95.7 %collective-permute-done.4 = bf16[256,2048]{1,0:T(8,128)(2,1)} collective-permute-done((bf16[256,2048]{1,0:T(8,128)(2,1)}, bf16[256,2048]{1,0:T(8,128)(2,1)}, u32[]{:S(2)}, u32[]{:S(2)}) %collective-permute-start.4) | collective-permute-done | bytes 1048608 | tf_op jit(solution)/shard_map/ppermute | solution.py:16
  484.4 22.5 %collective-permute-done.5 = bf16[256,2048]{1,0:T(8,128)(2,1)} collective-permute-done((bf16[256,2048]{1,0:T(8,128)(2,1)S(1)}, bf16[256,2048]{1,0:T(8,128)(2,1)}, u32[]{:S(2)}, u32[]{:S(2)}) %collective-permute-start.5) | collective-permute-done | bytes 1048608 | tf_op jit(solution)/shard_map/ppermute | solution.py:16
  506.9 7.5 %fusion.20 = (bf16[1,256,2048]{2,1,0:T(8,128)(2,1)}, f32[1,256,2048]{2,1,0:T(8,128)}, bf16[1,256,2048]{2,1,0:T(8,128)(2,1)}) fusion(f32[256,2048]{1,0:T(8,128)} %get-tuple-element.24, bf16[256,2048]{1,0:T(8,128)(2,1)} %collective-permute-done.5, pred[]{:T(512)S(6)} %ne.24, bf16[1,256,2048]{2,1,0:T(8,128)(2,1)S(1)} %copy-done.12, ...), kind=kLoop, calls=%fused_computation.46 | loop fusion | flops 12058624 | bytes 13631489 | tf_op jit(solution)/shard_map/broadcast_in_dim | solution.py:146
  514.4 15.0 %collective-permute-done.2 = bf16[2048,256]{1,0:T(8,128)(2,1)} collective-permute-done((bf16[2048,256]{1,0:T(8,128)(2,1)}, bf16[2048,256]{1,0:T(8,128)(2,1)}, u32[]{:S(2)}, u32[]{:S(2)}) %collective-permute-start.2) | collective-permute-done | bytes 1048608 | tf_op jit(solution)/shard_map/ppermute | solution.py:16
  529.4 20.7 %collective-permute-done.3 = bf16[2048,256]{1,0:T(8,128)(2,1)} collective-permute-done((bf16[2048,256]{1,0:T(8,128)(2,1)}, bf16[2048,256]{1,0:T(8,128)(2,1)}, u32[]{:S(2)}, u32[]{:S(2)}) %collective-permute-start.3) | collective-permute-done | bytes 1048608 | tf_op jit(solution)/shard_map/ppermute | solution.py:16
  550.1 6.2 %fusion.19 = (bf16[1,2048,256]{2,1,0:T(8,128)(2,1)}, f32[1,2048,256]{2,1,0:T(8,128)}, bf16[1,2048,256]{2,1,0:T(8,128)(2,1)}) fusion(f32[2048,256]{1,0:T(8,128)S(1)} %copy-done.9, bf16[2048,256]{1,0:T(8,128)(2,1)} %collective-permute-done.3, pred[]{:T(512)S(6)} %ne.24, bf16[1,2048,256]{2,1,0:T(8,128)(2,1)S(1)} %copy-done.13, ...), kind=kLoop, calls=%fused_computation.45 | loop fusion | flops 12058624 | bytes 13631489 | tf_op jit(solution)/shard_map/broadcast_in_dim | solution.py:144
  556.3 9.7 %fusion = f32[16,24,2048]{2,0,1:T(8,128)S(1)} fusion(bf16[64,24,2048]{2,1,0:T(8,128)(2,1)} %all-to-all-done.3, s32[64]{0:T(128)S(1)} %get-tuple-element.28), kind=kOutput, calls=%fused_computation.9 | convolution fusion | flops 100664320 | bytes 9437440 | tf_op jit(solution)/shard_map/je,jcd->ecd/dot_general | solution.py:130
  566.0 1.8 copy.43
  567.9 9.5 %fusion.2 = f32[16,24,2048]{2,0,1:T(8,128)S(1)} fusion(bf16[64,24,2048]{2,1,0:T(8,128)(2,1)} %all-to-all-done.1, s32[64]{0:T(128)S(1)} %get-tuple-element.28), kind=kOutput, calls=%fused_computation.11 | convolution fusion | flops 100664320 | bytes 9437440 | tf_op jit(solution)/shard_map/je,jcd->ecd/dot_general | solution.py:129
  577.4 1.8 copy.39
  579.2 1.9 concatenate.7
  581.7 5.5 gather_fusion.4
  587.3 2.7 gather_fusion.2
  590.0 5.0 broadcast_select_fusion.2
  595.0 2.5 reshape.152
  597.5 4.0 multiply_reduce_fusion
  601.5 2.5 reshape.157
  604.0 3.9 reduce_sum.45
  (71 shorter events, 10.0 us)
Async XLA Ops:
  7.2 12.9 %copy-start = (s32[64]{0:T(128)S(1)}, s32[64]{0:T(128)}, u32[]{:S(2)}) copy-start(s32[64]{0:T(128)} %param.22) | copy-start | bytes 772
  13.0 2.5 copy-start.17
  19.3 2.2 copy-start.2
  19.4 0.7 copy-start.16
  19.4 1.5 copy-start.15
  22.8 5.7 slice-start
  124.9 139.1 %all-to-all-start.2 = ((bf16[64,24,2048]{2,1,0:T(8,128)(2,1)}), bf16[64,24,2048]{2,1,0:T(8,128)(2,1)}, u32[]{:S(2)}, u32[]{:S(2)}) async-start(bf16[64,24,2048]{2,1,0:T(8,128)(2,1)} %get-tuple-element.37), calls=%async_computation.2 | async-start | bytes 12582912 | tf_op jit(solution)/shard_map/all_to_all | solution.py:92
  134.8 5.1 copy-start.3
  137.6 98.2 %collective-permute-start = (bf16[2048,256]{1,0:T(8,128)(2,1)}, bf16[2048,256]{1,0:T(8,128)(2,1)S(1)}, u32[]{:S(2)}, u32[]{:S(2)}) collective-permute-start(bf16[2048,256]{1,0:T(8,128)(2,1)} %bitcast_convert_fusion.1), channel_id=1, source_target_pairs={{0,32},{32,0},{1,33},{33,1},{2,34},{34,2},{3,35},{35,3},{4,36},{36... | collective-permute-start | bytes 3145736 | tf_op jit(solution)/shard_map/ppermute | solution.py:16
  141.1 115.6 %collective-permute-start.1 = (bf16[256,2048]{1,0:T(8,128)(2,1)}, bf16[256,2048]{1,0:T(8,128)(2,1)}, u32[]{:S(2)}, u32[]{:S(2)}) collective-permute-start(bf16[256,2048]{1,0:T(8,128)(2,1)} %bitcast_convert_fusion), channel_id=1, source_target_pairs={{0,32},{32,0},{1,33},{33,1},{2,34},{34,2},{3,35},{35,3},{4,36},{36... | collective-permute-start | bytes 3145736 | tf_op jit(solution)/shard_map/ppermute | solution.py:16
  235.8 2.3 copy-start.7
  238.1 20.1 %copy-start.5 = (bf16[2048,256]{1,0:T(8,128)(2,1)}, bf16[2048,256]{1,0:T(8,128)(2,1)S(1)}, u32[]{:S(2)}) copy-start(bf16[2048,256]{1,0:T(8,128)(2,1)S(1)} %fusion.13) | copy-start | bytes 3145732
  264.0 6.0 copy-start.6
  270.0 4.4 copy-start.10
  274.4 89.7 %all-to-all-start.3 = ((bf16[64,24,2048]{2,1,0:T(8,128)(2,1)}), bf16[64,24,2048]{2,1,0:T(8,128)(2,1)}, u32[]{:S(2)}, u32[]{:S(2)}) async-start(bf16[64,24,2048]{2,1,0:T(8,128)(2,1)} %bitcast.83), calls=%async_computation.3 | async-start | bytes 12582912 | tf_op jit(solution)/shard_map/all_to_all | solution.py:119
  284.0 222.9 %all-reduce.5.cloned.1.call-start = ((), (), s32[]{:S(2)}) async-start(), calls=%async_computation.4 | async-start | bytes 8388608 | tf_op jit(solution)/shard_map/psum | solution.py:123
  284.4 6.6 %copy-start.11 = (bf16[1536,256]{1,0:T(8,128)(2,1)S(1)}, bf16[1536,256]{1,0:T(8,128)(2,1)}, u32[]{:S(2)}) copy-start(bf16[1536,256]{1,0:T(8,128)(2,1)} %copy-done.10) | copy-start | bytes 2359300
  364.1 19.7 %copy-start.12 = (bf16[1,256,2048]{2,1,0:T(8,128)(2,1)S(1)}, bf16[1,256,2048]{2,1,0:T(8,128)(2,1)}, u32[]{:S(2)}) copy-start(bf16[1,256,2048]{2,1,0:T(8,128)(2,1)} %param.29) | copy-start | bytes 3145732
  364.1 203.8 %all-to-all-start.1 = ((bf16[64,24,2048]{2,1,0:T(8,128)(2,1)}), bf16[64,24,2048]{2,1,0:T(8,128)(2,1)}, u32[]{:S(2)}, u32[]{:S(2)}) async-start(bf16[64,24,2048]{2,1,0:T(8,128)(2,1)} %bitcast.82), calls=%async_computation.1 | async-start | bytes 12582912 | tf_op jit(solution)/shard_map/all_to_all | solution.py:116
  381.4 103.0 %collective-permute-start.4 = (bf16[256,2048]{1,0:T(8,128)(2,1)}, bf16[256,2048]{1,0:T(8,128)(2,1)}, u32[]{:S(2)}, u32[]{:S(2)}) collective-permute-start(bf16[256,2048]{1,0:T(8,128)(2,1)} %bitcast.89), channel_id=1, source_target_pairs={{0,32},{32,0},{1,33},{33,1},{2,34},{34,2},{3,35},{35,3},{4,36},{36... | collective-permute-start | bytes 3145736 | tf_op jit(solution)/shard_map/ppermute | solution.py:16
  383.8 123.1 %collective-permute-start.5 = (bf16[256,2048]{1,0:T(8,128)(2,1)S(1)}, bf16[256,2048]{1,0:T(8,128)(2,1)}, u32[]{:S(2)}, u32[]{:S(2)}) collective-permute-start(bf16[256,2048]{1,0:T(8,128)(2,1)S(1)} %bitcast.88), channel_id=1, source_target_pairs={{0,32},{32,0},{1,33},{33,1},{2,34},{34,2},{3,35},{35,3},{4,36},{36... | collective-permute-start | bytes 3145736 | tf_op jit(solution)/shard_map/ppermute | solution.py:16
  385.0 144.4 %collective-permute-start.2 = (bf16[2048,256]{1,0:T(8,128)(2,1)}, bf16[2048,256]{1,0:T(8,128)(2,1)}, u32[]{:S(2)}, u32[]{:S(2)}) collective-permute-start(bf16[2048,256]{1,0:T(8,128)(2,1)} %bitcast.91), channel_id=1, source_target_pairs={{0,32},{32,0},{1,33},{33,1},{2,34},{34,2},{3,35},{35,3},{4,36},{36... | collective-permute-start | bytes 3145736 | tf_op jit(solution)/shard_map/ppermute | solution.py:16
  387.3 162.8 %collective-permute-start.3 = (bf16[2048,256]{1,0:T(8,128)(2,1)}, bf16[2048,256]{1,0:T(8,128)(2,1)}, u32[]{:S(2)}, u32[]{:S(2)}) collective-permute-start(bf16[2048,256]{1,0:T(8,128)(2,1)} %bitcast.90), channel_id=1, source_target_pairs={{0,32},{32,0},{1,33},{33,1},{2,34},{34,2},{3,35},{35,3},{4,36},{36... | collective-permute-start | bytes 3145736 | tf_op jit(solution)/shard_map/ppermute | solution.py:16
  506.9 43.2 %copy-start.4 = (f32[1,2048,256]{2,1,0:T(8,128)S(1)}, f32[1,2048,256]{2,1,0:T(8,128)}, u32[]{:S(2)}) copy-start(f32[1,2048,256]{2,1,0:T(8,128)} %param.24) | copy-start | bytes 6291460
  506.9 43.2 %copy-start.8 = (bf16[2048,256]{1,0:T(8,128)(2,1)S(1)}, bf16[2048,256]{1,0:T(8,128)(2,1)}, u32[]{:S(2)}) copy-start(bf16[2048,256]{1,0:T(8,128)(2,1)} %copy-done.7) | copy-start | bytes 3145732
  506.9 43.2 %copy-start.9 = (f32[2048,256]{1,0:T(8,128)S(1)}, f32[2048,256]{1,0:T(8,128)}, u32[]{:S(2)}) copy-start(f32[2048,256]{1,0:T(8,128)} %get-tuple-element.23) | copy-start | bytes 6291460
  506.9 43.2 %copy-start.13 = (bf16[1,2048,256]{2,1,0:T(8,128)(2,1)S(1)}, bf16[1,2048,256]{2,1,0:T(8,128)(2,1)}, u32[]{:S(2)}) copy-start(bf16[1,2048,256]{2,1,0:T(8,128)(2,1)} %param.27) | copy-start | bytes 3145732
  506.9 43.2 %copy-start.14 = (bf16[1,2048,256]{2,1,0:T(8,128)(2,1)S(1)}, bf16[1,2048,256]{2,1,0:T(8,128)(2,1)}, u32[]{:S(2)}) copy-start(bf16[1,2048,256]{2,1,0:T(8,128)(2,1)} %param.26) | copy-start | bytes 3145732
  601.5 6.4 %copy-start.1 = (s32[64]{0:T(128)S(1)}, s32[64]{0:T(128)}, u32[]{:S(2)}) copy-start(s32[64]{0:T(128)} %param.22) | copy-start | bytes 772
Sparse Core Ops, SparseCore 0:
  297.2 35.3 all-reduce.4
where the time goes:
time: 625 us; the launch traced here: 615 us
  waiting for transfers between devices  325 us (52%)
  blocking collectives  80.8 us (13%)
  matrix products  54 us (9%)
  starting transfers between devices  48.3 us (8%)
  other arithmetic  47.9 us (8%)
  local copies, waits for them, and re-layouts  43.2 us (7%)
  between operations  15.5 us (2%)
    ppermute x6, waiting for transfers between devices, from_partner(): return lax.ppermute(block, axis, route)  264 us
    all_to_all x1, blocking collectives, local(): lax.all_to_all(send_x, 'expert', split_axis=0, concat_axis=0, tiled=True)  80.8 us
    all_to_all x1, waiting for transfers between devices, local(): lax.all_to_all(xpart.reshape(nexp, slots, width), 'expert', split_axis=0,...  61 us
    all_to_all x1, starting transfers between devices, local(): lax.all_to_all(part.reshape(nexp, slots, width), 'expert', split_axis=0,...  17.3 us
  transfers between devices with their start and end apart: 10, of which 7 were waited for; matrix products, arithmetic and copies ran while one was open for 9% of the time, Pallas kernels for 0%

commit v1 on v0

--- a/solution.py
+++ b/solution.py
@@ -6,14 +6,27 @@
 GROUP = 4
 
 
-def from_partner(block, axis, bit):
-    count = lax.axis_size(axis)
+def relay(block, step):
+    ndp = lax.axis_size("dp")
+    nexp = lax.axis_size("expert")
     route = []
-    for low in range(count):
-        high = low | 1 << bit
-        if high != low and high < count:
-            route += [(low, high), (high, low)]
-    return lax.ppermute(block, axis, route)
+    for d in range(ndp):
+        sign = 1 if d % 2 == 0 else -1
+        for e in range(nexp):
+            route.append((d * nexp + e, d * nexp + (e + sign * step) % nexp))
+    return lax.ppermute(block, ("dp", "expert"), route)
+
+
+def migrate(blocks):
+    ndp = lax.axis_size("dp")
+    step = lax.axis_size("expert") // 4
+    here = lax.axis_index("dp")
+    halves = tuple(
+        lax.dynamic_slice_in_dim(b, here * (b.shape[0] // ndp), b.shape[0] // ndp, 0)
+        for b in blocks
+    )
+    moved = relay(relay(halves, step), step)
+    return tuple(lax.all_gather(m, "dp", axis=0, tiled=True) for m in moved)
 
 
 def gelu_tanh(value):
@@ -50,7 +63,6 @@
     slots = 3 * count * topk // (2 * experts)
     nexp = lax.axis_size("expert")
     here = lax.axis_index("expert")
-    far_bit = (nexp // 2).bit_length() - 1
     moved = jnp.take(partner, here) != here
     flat_routes = routes.reshape(-1)
     onehot = (flat_routes[:, None] == jnp.arange(experts, dtype=jnp.int32)[None, :]).astype(
@@ -73,11 +85,18 @@
     weight_in, weight_out = (w_in[0], w_out[0])
     first_in, second_in, first_out, second_out = (m_in[0], v_in[0], m_out[0], v_out[0])
     held = jnp.take(layout, partner, axis=0)
-    other_w = (
-        from_partner(weight_in.astype(jnp.bfloat16), "expert", far_bit).astype(weight_in.dtype),
-        from_partner(weight_out.astype(jnp.bfloat16), "expert", far_bit).astype(weight_out.dtype),
+    other = migrate(
+        (
+            weight_in.astype(jnp.bfloat16),
+            weight_out.astype(jnp.bfloat16),
+            first_in,
+            second_in,
+            first_out,
+            second_out,
+        )
     )
-    other_m = from_partner((first_in, second_in, first_out, second_out), "expert", far_bit)
+    other_w = (other[0].astype(weight_in.dtype), other[1].astype(weight_out.dtype))
+    other_m = other[2:]
     weight_in = jnp.where(moved, other_w[0], weight_in)
     weight_out = jnp.where(moved, other_w[1], weight_out)
     first_in = jnp.where(moved, other_m[0], first_in)

time: 625 us -> 621 us (level)
  the two profiles are of different devices: /device:TPU:76 before, /device:TPU:50 now
where the time goes in v1:
time: 621 us; the launch traced here: 610 us
  waiting for transfers between devices  299 us (48%)
  blocking collectives  82 us (13%)
  starting transfers between devices  60.2 us (10%)
  matrix products  54 us (9%)
  local copies, waits for them, and re-layouts  51.8 us (8%)
  other arithmetic  47.3 us (8%)
  between operations  15.6 us (3%)
    ppermute x12, waiting for transfers between devices, relay(): return lax.ppermute(block, ('dp', 'expert'), route)  274 us
    all_to_all x1, blocking collectives, local(): lax.all_to_all(send_x, 'expert', split_axis=0, concat_axis=0, tiled=True)  82 us
    all_gather x6, waiting for transfers between devices, migrate(): return tuple((lax.all_gather(m, 'dp', axis=0, tiled=True) for m in moved))  24.8 us
    ppermute x12, starting transfers between devices, relay(): return lax.ppermute(block, ('dp', 'expert'), route)  24.4 us
    all_to_all x1, starting transfers between devices, local(): lax.all_to_all(part.reshape(nexp, slots, width), 'expert', split_axis=0,...  15.3 us
  transfers between devices with their start and end apart: 22, of which 15 were waited for; matrix products, arithmetic and copies ran while one was open for 10% of the time, Pallas kernels for 0%

profile of v1, /device:TPU:50, one launch (start us, length us, event | category | flops | bytes accessed | tf_op | source)
XLA Modules:
  0.0 609.9 jit_solution(7909800098683608369)
XLA Ops:
  13.1 2.4 convert_element_type.87
  15.6 3.7 scatter_custom_fusion.1
  22.8 4.2 scatter_custom_fusion
  28.5 3.6 gather_fusion.3
  32.1 3.6 gather_fusion.1
  35.7 8.4 %broadcast_select_fusion = (bf16[64,24,2048]{2,1,0:T(8,128)(2,1)}, bf16[64,24,2048]{2,1,0:T(8,128)(2,1)S(1)}) fusion(bf16[64,24,2048]{2,1,0:T(8,128)(2,1)} %gather_fusion.3, pred[64]{0:T(512)(128)(4,1)S(1)} %get-tuple-element.27, bf16[64,24,2048]{2,1,0:T(8,128)(2,1)} %gather_fusion.1), kind=kLoop, calls=%fused_computation.13 | loop fusion | flops 6291456 | bytes 25165888 | tf_op jit(solution)/shard_map/jit(_take)/select_n | solution.py:108
  44.1 82.0 %all_to_all.20 = bf16[64,24,2048]{2,1,0:T(8,128)(2,1)} all-to-all(bf16[64,24,2048]{2,1,0:T(8,128)(2,1)S(1)} %get-tuple-element.38), channel_id=1, replica_groups=mesh['dp'=2,'expert'=64] {'expert'}, dimensions={0} | all-to-all | bytes 12582912 | tf_op jit(solution)/shard_map/all_to_all | solution.py:110
  126.1 9.3 %all-to-all-start.2 = ((bf16[64,24,2048]{2,1,0:T(8,128)(2,1)}), bf16[64,24,2048]{2,1,0:T(8,128)(2,1)}, u32[]{:S(2)}, u32[]{:S(2)}) async-start(bf16[64,24,2048]{2,1,0:T(8,128)(2,1)} %get-tuple-element.37), calls=%async_computation.2 | async-start | bytes 12582912 | tf_op jit(solution)/shard_map/all_to_all | solution.py:111
  138.1 72.7 %collective-permute-done = bf16[1024,256]{1,0:T(8,128)(2,1)} collective-permute-done((bf16[1024,256]{1,0:T(8,128)(2,1)S(1)}, bf16[1024,256]{1,0:T(8,128)(2,1)}, u32[]{:S(2)}, u32[]{:S(2)}) %collective-permute-start) | collective-permute-done | bytes 524320 | tf_op jit(solution)/shard_map/ppermute | solution.py:17
  213.0 3.9 collective-permute-start.2
  216.8 4.9 collective-permute-done.1
  222.6 4.6 collective-permute-done.2
  227.3 2.6 collective-permute-start.3
  229.9 7.0 %collective-permute-done.3 = bf16[128,2048]{1,0:T(8,128)(2,1)S(1)} collective-permute-done((bf16[128,2048]{1,0:T(8,128)(2,1)}, bf16[128,2048]{1,0:T(8,128)(2,1)S(1)}, u32[]{:S(2)}, u32[]{:S(2)}) %collective-permute-start.3) | collective-permute-done | bytes 524320 | tf_op jit(solution)/shard_map/ppermute | solution.py:17
  240.3 3.1 fusion.13
  243.4 12.8 %all-gather.9.cloned.1.call-done = bf16[256,2048]{1,0:T(8,128)(2,1)} async-done(((bf16[128,2048]{1,0:T(8,128)(2,1)}), bf16[256,2048]{1,0:T(8,128)(2,1)}) %all-gather.9.cloned.1.call-update) | async-done | bytes 1048592 | tf_op jit(solution)/shard_map/all_gather | solution.py:29
  257.8 5.7 fusion.37
  263.6 6.0 fusion.12
  269.6 4.5 convolution_convert_fusion
  274.1 10.6 %all-to-all-start.3 = ((bf16[64,24,2048]{2,1,0:T(8,128)(2,1)}), bf16[64,24,2048]{2,1,0:T(8,128)(2,1)}, u32[]{:S(2)}, u32[]{:S(2)}) async-start(bf16[64,24,2048]{2,1,0:T(8,128)(2,1)} %bitcast.95), calls=%async_computation.3 | async-start | bytes 12582912 | tf_op jit(solution)/shard_map/all_to_all | solution.py:138
  287.1 77.1 %collective-permute-done.8 = bf16[128,2048]{1,0:T(8,128)(2,1)S(1)} collective-permute-done((bf16[128,2048]{1,0:T(8,128)(2,1)S(1)}, bf16[128,2048]{1,0:T(8,128)(2,1)S(1)}, u32[]{:S(2)}, u32[]{:S(2)}) %collective-permute-start.8) | collective-permute-done | bytes 524320 | tf_op jit(solution)/shard_map/ppermute | solution.py:17
  364.2 2.5 collective-permute-start.9
  368.6 4.9 collective-permute-done.9
  373.6 5.5 collective-permute-done.10
  379.2 2.5 collective-permute-start.11
  381.6 7.0 %collective-permute-done.11 = bf16[128,2048]{1,0:T(8,128)(2,1)} collective-permute-done((bf16[128,2048]{1,0:T(8,128)(2,1)}, bf16[128,2048]{1,0:T(8,128)(2,1)}, u32[]{:S(2)}, u32[]{:S(2)}) %collective-permute-start.11) | collective-permute-done | bytes 524320 | tf_op jit(solution)/shard_map/ppermute | solution.py:17
  389.1 6.6 %fusion.36 = f32[256,2048]{1,0:T(8,128)} fusion(bf16[1536,2048]{1,0:T(8,128)(2,1)} %bitcast.14, f32[1536,256]{1,0:T(8,128)} %fusion.37), kind=kOutput, calls=%fused_computation.94 | convolution fusion | flops 1614151680 | bytes 9961472 | tf_op jit(solution)/shard_map/dot_general | solution.py:131
  395.7 6.0 fusion.38
  401.7 6.0 convolution_convert_fusion.1
  407.8 15.3 %all-to-all-start.1 = ((bf16[64,24,2048]{2,1,0:T(8,128)(2,1)}), bf16[64,24,2048]{2,1,0:T(8,128)(2,1)}, u32[]{:S(2)}, u32[]{:S(2)}) async-start(bf16[64,24,2048]{2,1,0:T(8,128)(2,1)} %bitcast.94), calls=%async_computation.1 | async-start | bytes 12582912 | tf_op jit(solution)/shard_map/all_to_all | solution.py:135
  424.6 73.7 %collective-permute-done.4 = bf16[1024,256]{1,0:T(8,128)(2,1)S(1)} collective-permute-done((bf16[1024,256]{1,0:T(8,128)(2,1)S(1)}, bf16[1024,256]{1,0:T(8,128)(2,1)S(1)}, u32[]{:S(2)}, u32[]{:S(2)}) %collective-permute-start.4) | collective-permute-done | bytes 524320 | tf_op jit(solution)/shard_map/ppermute | solution.py:17
  500.0 3.8 collective-permute-start.6
  503.7 3.8 collective-permute-done.5
  508.4 4.9 collective-permute-done.6
  513.2 2.4 collective-permute-start.7
  515.6 7.8 %collective-permute-done.7 = bf16[1024,256]{1,0:T(8,128)(2,1)S(1)} collective-permute-done((bf16[1024,256]{1,0:T(8,128)(2,1)}, bf16[1024,256]{1,0:T(8,128)(2,1)S(1)}, u32[]{:S(2)}, u32[]{:S(2)}) %collective-permute-start.7) | collective-permute-done | bytes 524320 | tf_op jit(solution)/shard_map/ppermute | solution.py:17
  524.4 8.0 %fusion.20 = (bf16[1,256,2048]{2,1,0:T(8,128)(2,1)}, f32[1,256,2048]{2,1,0:T(8,128)}, bf16[1,256,2048]{2,1,0:T(8,128)(2,1)}) fusion(f32[256,2048]{1,0:T(8,128)} %get-tuple-element.24, bf16[256,2048]{1,0:T(8,128)(2,1)} %all-gather.17.cloned.1.call-done, bf16[1,256,2048]{2,1,0:T(8,128)(2,1)} %param.29, pred[]{:T(512)S(6)} %ne.24, ...), kind=kLoop, calls=%fused_computation.44 | loop fusion | flops 12058624 | bytes 13631489 | tf_op jit(solution)/shard_map/broadcast_in_dim | solution.py:165
  532.4 10.6 %all-gather.13.cloned.1.call-done = bf16[2048,256]{1,0:T(8,128)(2,1)} async-done(((bf16[1024,256]{1,0:T(8,128)(2,1)}), bf16[2048,256]{1,0:T(8,128)(2,1)}) %all-gather.13.cloned.1.call-update) | async-done | bytes 1048592 | tf_op jit(solution)/shard_map/all_gather | solution.py:29
  543.0 8.1 %fusion.19 = (bf16[1,2048,256]{2,1,0:T(8,128)(2,1)}, f32[1,2048,256]{2,1,0:T(8,128)}, bf16[1,2048,256]{2,1,0:T(8,128)(2,1)}) fusion(f32[2048,256]{1,0:T(8,128)} %get-tuple-element.23, bf16[2048,256]{1,0:T(8,128)(2,1)} %all-gather.13.cloned.1.call-done, bf16[1,2048,256]{2,1,0:T(8,128)(2,1)} %param.27, pred[]{:T(512)S(6)} %ne.24, ...), kind=kLoop, calls=%fused_computation.43 | loop fusion | flops 12058624 | bytes 13631489 | tf_op jit(solution)/shard_map/broadcast_in_dim | solution.py:163
  551.2 9.7 %fusion = f32[16,24,2048]{2,0,1:T(8,128)S(1)} fusion(bf16[64,24,2048]{2,1,0:T(8,128)(2,1)} %all-to-all-done.3, s32[64]{0:T(128)S(1)} %get-tuple-element.28), kind=kOutput, calls=%fused_computation.9 | convolution fusion | flops 100664320 | bytes 9437440 | tf_op jit(solution)/shard_map/je,jcd->ecd/dot_general | solution.py:149
  562.7 9.5 %fusion.2 = f32[16,24,2048]{2,0,1:T(8,128)S(1)} fusion(bf16[64,24,2048]{2,1,0:T(8,128)(2,1)} %all-to-all-done.1, s32[64]{0:T(128)S(1)} %get-tuple-element.28), kind=kOutput, calls=%fused_computation.11 | convolution fusion | flops 100664320 | bytes 9437440 | tf_op jit(solution)/shard_map/je,jcd->ecd/dot_general | solution.py:148
  576.5 5.5 gather_fusion.4
  582.1 2.7 gather_fusion.2
  584.8 5.0 broadcast_select_fusion.2
  589.8 2.5 reshape.156
  592.3 4.0 multiply_reduce_fusion
  596.3 2.5 reshape.161
  598.8 3.9 reduce_sum.45
  (103 shorter events, 36.8 us)
Async XLA Ops:
  7.2 12.9 %copy-start = (s32[64]{0:T(128)S(1)}, s32[64]{0:T(128)}, u32[]{:S(2)}) copy-start(s32[64]{0:T(128)} %param.22) | copy-start | bytes 772
  13.0 2.5 copy-start.16
  19.3 2.2 copy-start.2
  19.4 0.7 copy-start.15
  19.4 1.5 copy-start.10
  22.8 5.7 slice-start
  126.1 86.8 %copy-start.3 = (f32[1,256,2048]{2,1,0:T(8,128)S(1)}, f32[1,256,2048]{2,1,0:T(8,128)}, u32[]{:S(2)}) copy-start(f32[1,256,2048]{2,1,0:T(8,128)} %param.25) | copy-start | bytes 6291460
  126.1 137.5 %all-to-all-start.2 = ((bf16[64,24,2048]{2,1,0:T(8,128)(2,1)}), bf16[64,24,2048]{2,1,0:T(8,128)(2,1)}, u32[]{:S(2)}, u32[]{:S(2)}) async-start(bf16[64,24,2048]{2,1,0:T(8,128)(2,1)} %get-tuple-element.37), calls=%async_computation.2 | async-start | bytes 12582912 | tf_op jit(solution)/shard_map/all_to_all | solution.py:111
  135.4 104.9 %all-gather.7.cloned.1.call-start = ((), (), s32[]{:S(2)}) async-start(), calls=%async_computation.4 | async-start | bytes 1572864 | tf_op jit(solution)/shard_map/all_gather | solution.py:29
  136.8 74.0 %collective-permute-start = (bf16[1024,256]{1,0:T(8,128)(2,1)S(1)}, bf16[1024,256]{1,0:T(8,128)(2,1)}, u32[]{:S(2)}, u32[]{:S(2)}) collective-permute-start(bf16[1024,256]{1,0:T(8,128)(2,1)S(1)} %dynamic-slice_convert_fusion.1), channel_id=1, source_target_pairs={{0,16},{1,17},{2,18},{3,19},{4,20},{5,21},{6,22},{7,23},{8,24},{9,... | collective-permute-start | bytes 1572872 | tf_op jit(solution)/shard_map/ppermute | solution.py:17
  210.7 11.0 %collective-permute-start.1 = (bf16[1024,256]{1,0:T(8,128)(2,1)}, bf16[1024,256]{1,0:T(8,128)(2,1)S(1)}, u32[]{:S(2)}, u32[]{:S(2)}) collective-permute-start(bf16[1024,256]{1,0:T(8,128)(2,1)} %collective-permute-done), channel_id=1, source_target_pairs={{0,16},{1,17},{2,18},{3,19},{4,20},{5,21},{6,22},{7,23},{8,24},{9,... | collective-permute-start | bytes 1572872 | tf_op jit(solution)/shard_map/ppermute | solution.py:17
  213.0 14.3 %collective-permute-start.2 = (bf16[128,2048]{1,0:T(8,128)(2,1)S(1)}, bf16[128,2048]{1,0:T(8,128)(2,1)}, u32[]{:S(2)}, u32[]{:S(2)}) collective-permute-start(bf16[128,2048]{1,0:T(8,128)(2,1)S(1)} %dynamic-slice_convert_fusion), channel_id=1, source_target_pairs={{0,16},{1,17},{2,18},{3,19},{4,20},{5,21},{6,22},{7,23},{8,24},{9,... | collective-permute-start | bytes 1572872 | tf_op jit(solution)/shard_map/ppermute | solution.py:17
  221.8 0.8 copy-start.11
  222.6 33.6 %all-gather.9.cloned.1.call-start = ((), (), s32[]{:S(2)}) async-start(), calls=%async_computation.5 | async-start | bytes 1572864 | tf_op jit(solution)/shard_map/all_gather | solution.py:29
  227.3 9.6 %collective-permute-start.3 = (bf16[128,2048]{1,0:T(8,128)(2,1)}, bf16[128,2048]{1,0:T(8,128)(2,1)S(1)}, u32[]{:S(2)}, u32[]{:S(2)}) collective-permute-start(bf16[128,2048]{1,0:T(8,128)(2,1)} %collective-permute-done.2), channel_id=1, source_target_pairs={{0,16},{1,17},{2,18},{3,19},{4,20},{5,21},{6,22},{7,23},{8,24},{9,... | collective-permute-start | bytes 1572872 | tf_op jit(solution)/shard_map/ppermute | solution.py:17
  236.9 0.8 copy-start.14
  256.2 1.6 copy-start.4
  263.6 6.0 copy-start.5
  269.5 4.5 copy-start.8
  274.1 133.7 %all-to-all-start.3 = ((bf16[64,24,2048]{2,1,0:T(8,128)(2,1)}), bf16[64,24,2048]{2,1,0:T(8,128)(2,1)}, u32[]{:S(2)}, u32[]{:S(2)}) async-start(bf16[64,24,2048]{2,1,0:T(8,128)(2,1)} %bitcast.95), calls=%async_computation.3 | async-start | bytes 12582912 | tf_op jit(solution)/shard_map/all_to_all | solution.py:138
  284.6 239.7 %all-gather.15.cloned.1.call-start = ((), (), s32[]{:S(2)}) async-start(), calls=%async_computation.8 | async-start | bytes 1572864 | tf_op jit(solution)/shard_map/all_gather | solution.py:29
  285.8 78.5 %collective-permute-start.8 = (bf16[128,2048]{1,0:T(8,128)(2,1)S(1)}, bf16[128,2048]{1,0:T(8,128)(2,1)S(1)}, u32[]{:S(2)}, u32[]{:S(2)}) collective-permute-start(bf16[128,2048]{1,0:T(8,128)(2,1)S(1)} %dynamic-slice_bitcast_fusion.1), channel_id=1, source_target_pairs={{0,16},{1,17},{2,18},{3,19},{4,20},{5,21},{6,22},{7,23},{8,24},{9,... | collective-permute-start | bytes 1572872 | tf_op jit(solution)/shard_map/ppermute | solution.py:17
  364.2 9.3 %collective-permute-start.9 = (bf16[128,2048]{1,0:T(8,128)(2,1)S(1)}, bf16[128,2048]{1,0:T(8,128)(2,1)}, u32[]{:S(2)}, u32[]{:S(2)}) collective-permute-start(bf16[128,2048]{1,0:T(8,128)(2,1)S(1)} %collective-permute-done.8), channel_id=1, source_target_pairs={{0,16},{1,17},{2,18},{3,19},{4,20},{5,21},{6,22},{7,23},{8,24},{9,... | collective-permute-start | bytes 1572872 | tf_op jit(solution)/shard_map/ppermute | solution.py:17
  368.6 10.5 %collective-permute-start.10 = (bf16[128,2048]{1,0:T(8,128)(2,1)}, bf16[128,2048]{1,0:T(8,128)(2,1)}, u32[]{:S(2)}, u32[]{:S(2)}) collective-permute-start(bf16[128,2048]{1,0:T(8,128)(2,1)} %dynamic-slice_bitcast_fusion), channel_id=1, source_target_pairs={{0,16},{1,17},{2,18},{3,19},{4,20},{5,21},{6,22},{7,23},{8,24},{9,... | collective-permute-start | bytes 1572872 | tf_op jit(solution)/shard_map/ppermute | solution.py:17
  373.6 150.8 %all-gather.17.cloned.1.call-start = ((), (), s32[]{:S(2)}) async-start(), calls=%async_computation.9 | async-start | bytes 1572864 | tf_op jit(solution)/shard_map/all_gather | solution.py:29
  379.2 9.5 %collective-permute-start.11 = (bf16[128,2048]{1,0:T(8,128)(2,1)}, bf16[128,2048]{1,0:T(8,128)(2,1)}, u32[]{:S(2)}, u32[]{:S(2)}) collective-permute-start(bf16[128,2048]{1,0:T(8,128)(2,1)} %collective-permute-done.10), channel_id=1, source_target_pairs={{0,16},{1,17},{2,18},{3,19},{4,20},{5,21},{6,22},{7,23},{8,24},{9,... | collective-permute-start | bytes 1572872 | tf_op jit(solution)/shard_map/ppermute | solution.py:17
  388.7 135.7 %all-reduce.5.cloned.1.call-start = ((), (), s32[]{:S(2)}) async-start(), calls=%async_computation.10 | async-start | bytes 8388608 | tf_op jit(solution)/shard_map/psum | solution.py:142
  389.1 6.6 %copy-start.9 = (bf16[1536,256]{1,0:T(8,128)(2,1)S(1)}, bf16[1536,256]{1,0:T(8,128)(2,1)}, u32[]{:S(2)}) copy-start(bf16[1536,256]{1,0:T(8,128)(2,1)} %copy-done.8) | copy-start | bytes 2359300
  407.8 15.4 %copy-start.7 = (bf16[1,2048,256]{2,1,0:T(8,128)(2,1)S(1)}, bf16[1,2048,256]{2,1,0:T(8,128)(2,1)}, u32[]{:S(2)}) copy-start(bf16[1,2048,256]{2,1,0:T(8,128)(2,1)} %param.26) | copy-start | bytes 3145732
  407.8 154.9 %all-to-all-start.1 = ((bf16[64,24,2048]{2,1,0:T(8,128)(2,1)}), bf16[64,24,2048]{2,1,0:T(8,128)(2,1)}, u32[]{:S(2)}, u32[]{:S(2)}) async-start(bf16[64,24,2048]{2,1,0:T(8,128)(2,1)} %bitcast.94), calls=%async_computation.1 | async-start | bytes 12582912 | tf_op jit(solution)/shard_map/all_to_all | solution.py:135
  423.1 109.3 %all-gather.11.cloned.1.call-start = ((), (), s32[]{:S(2)}) async-start(), calls=%async_computation.6 | async-start | bytes 1572864 | tf_op jit(solution)/shard_map/all_gather | solution.py:29
  423.2 75.1 %collective-permute-start.4 = (bf16[1024,256]{1,0:T(8,128)(2,1)S(1)}, bf16[1024,256]{1,0:T(8,128)(2,1)S(1)}, u32[]{:S(2)}, u32[]{:S(2)}) collective-permute-start(bf16[1024,256]{1,0:T(8,128)(2,1)S(1)} %dynamic-slice_bitcast_fusion.3), channel_id=1, source_target_pairs={{0,16},{1,17},{2,18},{3,19},{4,20},{5,21},{6,22},{7,23},{8,24},{9,... | collective-permute-start | bytes 1572872 | tf_op jit(solution)/shard_map/ppermute | solution.py:17
  498.3 9.2 %collective-permute-start.5 = (bf16[1024,256]{1,0:T(8,128)(2,1)S(1)}, bf16[1024,256]{1,0:T(8,128)(2,1)S(1)}, u32[]{:S(2)}, u32[]{:S(2)}) collective-permute-start(bf16[1024,256]{1,0:T(8,128)(2,1)S(1)} %collective-permute-done.4), channel_id=1, source_target_pairs={{0,16},{1,17},{2,18},{3,19},{4,20},{5,21},{6,22},{7,23},{8,24},{9,... | collective-permute-start | bytes 1572872 | tf_op jit(solution)/shard_map/ppermute | solution.py:17
  500.0 13.3 %collective-permute-start.6 = (bf16[1024,256]{1,0:T(8,128)(2,1)S(1)}, bf16[1024,256]{1,0:T(8,128)(2,1)}, u32[]{:S(2)}, u32[]{:S(2)}) collective-permute-start(bf16[1024,256]{1,0:T(8,128)(2,1)S(1)} %dynamic-slice_bitcast_fusion.2), channel_id=1, source_target_pairs={{0,16},{1,17},{2,18},{3,19},{4,20},{5,21},{6,22},{7,23},{8,24},{9,... | collective-permute-start | bytes 1572872 | tf_op jit(solution)/shard_map/ppermute | solution.py:17
  507.5 0.8 copy-start.12
  508.3 34.7 %all-gather.13.cloned.1.call-start = ((), (), s32[]{:S(2)}) async-start(), calls=%async_computation.7 | async-start | bytes 1572864 | tf_op jit(solution)/shard_map/all_gather | solution.py:29
  513.2 10.2 %collective-permute-start.7 = (bf16[1024,256]{1,0:T(8,128)(2,1)}, bf16[1024,256]{1,0:T(8,128)(2,1)S(1)}, u32[]{:S(2)}, u32[]{:S(2)}) collective-permute-start(bf16[1024,256]{1,0:T(8,128)(2,1)} %collective-permute-done.6), channel_id=1, source_target_pairs={{0,16},{1,17},{2,18},{3,19},{4,20},{5,21},{6,22},{7,23},{8,24},{9,... | collective-permute-start | bytes 1572872 | tf_op jit(solution)/shard_map/ppermute | solution.py:17
  523.4 0.8 copy-start.13
  524.4 18.7 %copy-start.6 = (bf16[2048,256]{1,0:T(8,128)(2,1)S(1)}, bf16[2048,256]{1,0:T(8,128)(2,1)}, u32[]{:S(2)}) copy-start(bf16[2048,256]{1,0:T(8,128)(2,1)} %all-gather.7.cloned.1.call-done) | copy-start | bytes 3145732
  596.3 6.4 %copy-start.1 = (s32[64]{0:T(128)S(1)}, s32[64]{0:T(128)}, u32[]{:S(2)}) copy-start(s32[64]{0:T(128)} %param.22) | copy-start | bytes 772
Sparse Core Ops, SparseCore 0:
  222.7 17.5 all-gather.6
  242.5 13.6 all-gather.8
  373.7 16.8 all-gather.14
  392.1 14.0 all-gather.16
  409.3 35.2 all-reduce.4
  508.4 19.2 all-gather.10
  529.9 13.0 all-gather.12

commit v2 on v1

--- a/solution.py
+++ b/solution.py
@@ -70,21 +70,28 @@
     )
     position = jnp.sum((jnp.cumsum(onehot, 0) - 1) * onehot, 1)
     limit = jnp.sum(onehot * capacity[None, :], 1)
-    slot = jnp.where(position < limit, flat_routes * slots + position, experts * slots)
-    x_rows = jnp.repeat(tokens, topk, axis=0)
-    scaled = (
-        gates.reshape(-1)[:, None] * jnp.repeat(cotangent, topk, axis=0).astype(jnp.float32)
+    kept = position < limit
+    npairs = count * topk
+    slot = jnp.where(kept, flat_routes * slots + position, experts * slots)
+    pair_of = (
+        jnp.full((experts * slots + 1,), npairs, jnp.int32)
+        .at[slot]
+        .set(jnp.arange(npairs, dtype=jnp.int32))[:-1]
+        .reshape(experts, slots)
+    )
+    held = jnp.take(layout, partner, axis=0)
+    target_expert = held // GROUP
+    send_pair = jnp.take(pair_of, target_expert, axis=0)
+    send_tok = jnp.where(send_pair < npairs, send_pair // topk, count)
+    gate_of = jnp.concatenate([gates.reshape(-1), jnp.zeros((1,), gates.dtype)])
+    blank = jnp.zeros((1, width), tokens.dtype)
+    send_x = jnp.take(jnp.concatenate([tokens, blank]), send_tok, axis=0)
+    send_g = (
+        jnp.take(gate_of, send_pair)[:, :, None]
+        * jnp.take(jnp.concatenate([cotangent, blank]), send_tok, axis=0).astype(jnp.float32)
     ).astype(jnp.bfloat16)
-
-    def build(rows):
-        filled = jnp.zeros((experts * slots + 1, width), jnp.bfloat16).at[slot].set(rows)
-        return filled[:-1].reshape(experts, slots, width)
-
-    x_buf = build(x_rows)
-    g_buf = build(scaled)
     weight_in, weight_out = (w_in[0], w_out[0])
     first_in, second_in, first_out, second_out = (m_in[0], v_in[0], m_out[0], v_out[0])
-    held = jnp.take(layout, partner, axis=0)
     other = migrate(
         (
             weight_in.astype(jnp.bfloat16),
@@ -95,6 +102,7 @@
             second_out,
         )
     )
+    send_x, send_g, other = lax.optimization_barrier((send_x, send_g, other))
     other_w = (other[0].astype(weight_in.dtype), other[1].astype(weight_out.dtype))
     other_m = other[2:]
     weight_in = jnp.where(moved, other_w[0], weight_in)
@@ -103,9 +111,6 @@
     second_in = jnp.where(moved, other_m[1], second_in)
     first_out = jnp.where(moved, other_m[2], first_out)
     second_out = jnp.where(moved, other_m[3], second_out)
-    target_expert = held // GROUP
-    send_x = jnp.take(x_buf, target_expert, axis=0)
-    send_g = jnp.take(g_buf, target_expert, axis=0)
     recv_x, recv_g = (
         lax.all_to_all(send_x, "expert", split_axis=0, concat_axis=0, tiled=True),
         lax.all_to_all(send_g, "expert", split_axis=0, concat_axis=0, tiled=True),
@@ -142,14 +147,19 @@
     grad_in, grad_out = lax.psum((grad_in, grad_out), "dp")
     new_w_in, new_m_in, new_v_in = adamw(weight_in, first_in, second_in, grad_in)
     new_w_out, new_m_out, new_v_out = adamw(weight_out, first_out, second_out, grad_out)
-    owners = (target_expert[:, None] == jnp.arange(experts, dtype=jnp.int32)[None, :]).astype(
-        jnp.bfloat16
-    )
-    out_sum = jnp.einsum("je,jcd->ecd", owners, back_part, preferred_element_type=jnp.float32)
-    dx_sum = jnp.einsum("je,jcd->ecd", owners, back_dx, preferred_element_type=jnp.float32)
-    blank = jnp.zeros((1, width), jnp.float32)
-    out_vals = jnp.take(jnp.concatenate([out_sum.reshape(-1, width), blank]), slot, axis=0)
-    dx_vals = jnp.take(jnp.concatenate([dx_sum.reshape(-1, width), blank]), slot, axis=0)
+    holder_of = jnp.zeros((nexp,), jnp.int32).at[held].set(jnp.arange(nexp, dtype=jnp.int32))
+    shard_ids = flat_routes[:, None] * GROUP + jnp.arange(GROUP, dtype=jnp.int32)[None, :]
+    back_row = jnp.where(
+        kept[:, None], jnp.take(holder_of, shard_ids) * slots + position[:, None], nexp * slots
+    )
+    zero = jnp.zeros((1, width), jnp.bfloat16)
+
+    def gather_sum(back):
+        table = jnp.concatenate([back.reshape(-1, width), zero])
+        return jnp.sum(jnp.take(table, back_row, axis=0).astype(jnp.float32), axis=1)
+
+    out_vals = gather_sum(back_part)
+    dx_vals = gather_sum(back_dx)
     mixed = jnp.sum(out_vals.reshape(count, topk, width) * gates[:, :, None], axis=1).astype(
         jnp.bfloat16
     )

time: 621 us -> 590 us (0.950)
  waiting for transfers between devices: 299 us -> 223 us
  local copies, waits for them, and re-layouts: 51.8 us -> 110 us
  matrix products: 54 us -> 33.7 us
  other arithmetic: 47.3 us -> 57.8 us
    ppermute x12, waiting for transfers between devices: 274 us -> 46.1 us  [relay(): return lax.ppermute(block, ('dp', 'expert'), route)]
    all_to_all x1, waiting for transfers between devices: 0.01 us -> 76.8 us  [local(): lax.all_to_all(send_x, 'expert', split_axis=0, concat_axis=0, tiled=True)]
    all_to_all x1, waiting for transfers between devices: 0.01 us -> 70.8 us  [local(): lax.all_to_all(xpart.reshape(nexp, slots, width), 'expert', split_axis=0,...]
    gather x4 -> x11, local copies, waits for them, and re-layouts: 15.4 us -> 70.3 us  [the longest x4 39.4 us: gather_sum(): jnp.take(table, back_row, axis=0).astype(jnp.float32)]
    psum x1, waiting for transfers between devices: 0.02 us -> 26.9 us  [local(): grad_in, grad_out = lax.psum((grad_in, grad_out), 'dp')]
    all_gather x6, waiting for transfers between devices: 24.8 us -> 0.05 us  [migrate(): return tuple((lax.all_gather(m, 'dp', axis=0, tiled=True) for m in moved))]
    dot_general x2 -> x0, matrix products: 19.2 us -> none  [the longest x1 9.71 us: local(): jnp.einsum('je,jcd->ecd', owners, back_dx, preferred_element_type=jnp.flo...]
    reduce_sum x0 -> x1, other arithmetic: none -> 16.8 us  [gather_sum(): jnp.sum(jnp.take(table, back_row, axis=0).astype(jnp.float32), axis=1)]
  transfers between devices with their start and end apart: 22 -> 22, of which waited for: 15 -> 13; matrix products, arithmetic and copies ran while one was open for 10% -> 21% of each run, Pallas kernels for 0% -> 0%
where the time goes in v2:
time: 590 us; the launch traced here: 578 us
  waiting for transfers between devices  223 us (38%)
  local copies, waits for them, and re-layouts  110 us (19%)
  blocking collectives  80 us (14%)
  starting transfers between devices  58.2 us (10%)
  other arithmetic  57.8 us (10%)
  matrix products  33.7 us (6%)
  between operations  15.5 us (3%)
    all_to_all x1, blocking collectives, local(): lax.all_to_all(send_g, 'expert', split_axis=0, concat_axis=0, tiled=True)  80 us
    all_to_all x1, waiting for transfers between devices, local(): lax.all_to_all(send_x, 'expert', split_axis=0, concat_axis=0, tiled=True)  76.8 us
    all_to_all x1, waiting for transfers between devices, local(): lax.all_to_all(xpart.reshape(nexp, slots, width), 'expert', split_axis=0,...  70.8 us
    ppermute x12, waiting for transfers between devices, relay(): return lax.ppermute(block, ('dp', 'expert'), route)  46.1 us
    gather x4, local copies, waits for them, and re-layouts, gather_sum(): jnp.take(table, back_row, axis=0).astype(jnp.float32)  39.4 us
    psum x1, waiting for transfers between devices, local(): grad_in, grad_out = lax.psum((grad_in, grad_out), 'dp')  26.9 us
    ppermute x12, starting transfers between devices, relay(): return lax.ppermute(block, ('dp', 'expert'), route)  26 us
    reduce_sum x1, other arithmetic, gather_sum(): jnp.sum(jnp.take(table, back_row, axis=0).astype(jnp.float32), axis=1)  16.8 us
  transfers between devices with their start and end apart: 22, of which 13 were waited for; matrix products, arithmetic and copies ran while one was open for 21% of the time, Pallas kernels for 0%

profile of v2, /device:TPU:50, one launch (start us, length us, event | category | flops | bytes accessed | tf_op | source)
XLA Modules:
  0.0 578.3 jit_solution(13327080892768381)
XLA Ops:
  9.7 7.9 %collective-permute-done.10 = bf16[128,2048]{1,0:T(8,128)(2,1)S(1)} collective-permute-done((bf16[128,2048]{1,0:T(8,128)(2,1)S(1)}, bf16[128,2048]{1,0:T(8,128)(2,1)S(1)}, u32[]{:S(2)}, u32[]{:S(2)}) %collective-permute-start.10) | collective-permute-done | bytes 524320 | tf_op jit(solution)/shard_map/ppermute | solution.py:17
  21.4 5.3 collective-permute-done.11
  27.6 4.9 collective-permute-done.8
  34.8 2.7 collective-permute-start.6
  37.6 4.3 collective-permute-done.9
  42.8 4.8 collective-permute-done.6
  50.8 3.8 collective-permute-start.4
  57.9 2.1 dynamic-slice_convert_fusion
  60.0 2.8 collective-permute-start.2
  63.0 3.7 collective-permute-start.5
  69.5 10.0 %collective-permute-done.5 = bf16[1024,256]{1,0:T(8,128)(2,1)S(1)} collective-permute-done((bf16[1024,256]{1,0:T(8,128)(2,1)}, bf16[1024,256]{1,0:T(8,128)(2,1)S(1)}, u32[]{:S(2)}, u32[]{:S(2)}) %collective-permute-start.5) | collective-permute-done | bytes 524320 | tf_op jit(solution)/shard_map/ppermute | solution.py:17
  81.2 2.8 collective-permute-start.1
  84.7 6.4 %collective-permute-done.1 = bf16[1024,256]{1,0:T(8,128)(2,1)S(1)} collective-permute-done((bf16[1024,256]{1,0:T(8,128)(2,1)}, bf16[1024,256]{1,0:T(8,128)(2,1)S(1)}, u32[]{:S(2)}, u32[]{:S(2)}) %collective-permute-start.1) | collective-permute-done | bytes 524320 | tf_op jit(solution)/shard_map/ppermute | solution.py:17
  94.0 7.0 %gather_fusion.4 = bf16[1536,2048]{1,0:T(8,128)(2,1)} fusion(bf16[129,2048]{1,0:T(8,128)(2,1)S(1)} %concatenate.15, s32[2048]{0:T(1024)S(1)} %pad_clamp_fusion.1), kind=kCustom, calls=%fused_computation.clone | custom fusion | bytes 12589056 | tf_op jit(solution)/shard_map/jit(_take)/gather | solution.py:88
  101.1 3.5 collective-permute-start.3
  104.6 6.1 %broadcast_select_fusion = bf16[64,24,2048]{2,1,0:T(8,128)(2,1)} fusion(bf16[64,24,2048]{2,1,0:T(8,128)(2,1)} %bitcast.101, pred[64,24]{1,0:T(8,128)(4,1)S(1)} %get-tuple-element.47), kind=kLoop, calls=%fused_computation.15 | loop fusion | flops 3145728 | bytes 12584448 | tf_op jit(solution)/shard_map/jit(_take)/select_n | solution.py:88
  112.6 9.5 %gather_fusion.2 = f32[1536]{0:T(1024)S(1)} fusion(f32[257]{0:T(512)S(1)} %pad_maximum_fusion, s32[2048]{0:T(1024)S(1)} %pad_clamp_fusion), kind=kCustom, calls=%fused_computation.6 | custom fusion | bytes 18432 | tf_op jit(solution)/shard_map/jit(_take)/gather | solution.py:90
  122.2 7.1 %gather_fusion.5 = bf16[1536,2048]{1,0:T(8,128)(2,1)} fusion(bf16[129,2048]{1,0:T(8,128)(2,1)S(1)} %concatenate.17, s32[2048]{0:T(1024)S(1)} %pad_clamp_fusion.1), kind=kCustom, calls=%fused_computation.2.clone | custom fusion | bytes 12589056 | tf_op jit(solution)/shard_map/jit(_take)/gather | solution.py:91
  129.3 7.2 %multiply_convert_fusion = bf16[64,24,2048]{2,1,0:T(8,128)(2,1)} fusion(bf16[64,24,2048]{2,1,0:T(8,128)(2,1)} %bitcast.102, f32[64,24]{1,0:T(8,128)S(1)} %and_select_fusion, pred[64,24]{1,0:T(8,128)(4,1)S(1)} %get-tuple-element.47), kind=kLoop, calls=%fused_computation.10 | loop fusion | flops 12582912 | bytes 12590592 | tf_op jit(solution)/shard_map/convert_element_type | solution.py:92
  136.6 80.0 %all_to_all.20 = bf16[64,24,2048]{2,1,0:T(8,128)(2,1)} all-to-all(bf16[64,24,2048]{2,1,0:T(8,128)(2,1)} %multiply_convert_fusion), channel_id=1, replica_groups=mesh['dp'=2,'expert'=64] {'expert'}, dimensions={0} | all-to-all | bytes 12582912 | tf_op jit(solution)/shard_map/all_to_all | solution.py:116
  216.5 10.7 %all-to-all-start = ((bf16[64,24,2048]{2,1,0:T(8,128)(2,1)}), bf16[64,24,2048]{2,1,0:T(8,128)(2,1)}, u32[]{:S(2)}, u32[]{:S(2)}) async-start(bf16[64,24,2048]{2,1,0:T(8,128)(2,1)} %broadcast_select_fusion), calls=%async_computation | async-start | bytes 12582912 | tf_op jit(solution)/shard_map/all_to_all | solution.py:115
  228.5 2.7 fusion.9
  231.2 1.9 fusion.10
  234.2 3.0 fusion.33
  237.2 76.8 %all-to-all-done = bf16[64,24,2048]{2,1,0:T(8,128)(2,1)} async-done(((bf16[64,24,2048]{2,1,0:T(8,128)(2,1)}), bf16[64,24,2048]{2,1,0:T(8,128)(2,1)}, u32[]{:S(2)}, u32[]{:S(2)}) %all-to-all-start) | async-done | bytes 6291488 | tf_op jit(solution)/shard_map/all_to_all | solution.py:115
  314.0 7.4 %fusion.8 = (bf16[1536,256]{1,0:T(8,128)(2,1)S(1)}, f32[1536,256]{1,0:T(8,128)}) fusion(f32[1536,256]{1,0:T(8,128)} %fusion.33, bf16[1536,2048]{1,0:T(8,128)(2,1)} %bitcast.13, bf16[2048,256]{1,0:T(8,128)(2,1)} %fusion.9), kind=kOutput, calls=%fused_computation.35 | convolution fusion | flops 1618477056 | bytes 11272192 | tf_op jit(solution)/shard_map/dot_general | solution.py:122
  321.4 4.4 convolution_convert_fusion
  325.8 10.4 %all-to-all-start.3 = ((bf16[64,24,2048]{2,1,0:T(8,128)(2,1)}), bf16[64,24,2048]{2,1,0:T(8,128)(2,1)}, u32[]{:S(2)}, u32[]{:S(2)}) async-start(bf16[64,24,2048]{2,1,0:T(8,128)(2,1)} %bitcast.100), calls=%async_computation.3 | async-start | bytes 12582912 | tf_op jit(solution)/shard_map/all_to_all | solution.py:143
  336.2 6.3 %convolution_convert_fusion.1 = bf16[1536,2048]{1,0:T(8,128)(2,1)} fusion(bf16[256,2048]{1,0:T(8,128)(2,1)} %copy-done.6, f32[1536,256]{1,0:T(8,128)} %get-tuple-element.58), kind=kOutput, calls=%fused_computation.14 | convolution fusion | flops 1617297408 | bytes 8912896 | tf_op jit(solution)/shard_map/dot_general | solution.py:125
  342.6 6.0 %fusion.34 = f32[2048,256]{1,0:T(8,128)} fusion(bf16[1536,2048]{1,0:T(8,128)(2,1)} %bitcast.13, bf16[1536,256]{1,0:T(8,128)(2,1)S(1)} %get-tuple-element.57), kind=kOutput, calls=%fused_computation.113 | convolution fusion | flops 1610612736 | bytes 9175040 | tf_op jit(solution)/shard_map/dot_general | solution.py:133
  348.6 70.8 %all-to-all-done.3 = bf16[64,24,2048]{2,1,0:T(8,128)(2,1)} async-done(((bf16[64,24,2048]{2,1,0:T(8,128)(2,1)}), bf16[64,24,2048]{2,1,0:T(8,128)(2,1)}, u32[]{:S(2)}, u32[]{:S(2)}) %all-to-all-start.3) | async-done | bytes 6291488 | tf_op jit(solution)/shard_map/all_to_all | solution.py:143
  419.4 10.7 %all-to-all-start.1 = ((bf16[64,24,2048]{2,1,0:T(8,128)(2,1)}), bf16[64,24,2048]{2,1,0:T(8,128)(2,1)}, u32[]{:S(2)}, u32[]{:S(2)}) async-start(bf16[64,24,2048]{2,1,0:T(8,128)(2,1)} %bitcast.99), calls=%async_computation.1 | async-start | bytes 12582912 | tf_op jit(solution)/shard_map/all_to_all | solution.py:140
  430.1 6.5 %fusion.32 = f32[256,2048]{1,0:T(8,128)} fusion(bf16[1536,2048]{1,0:T(8,128)(2,1)} %bitcast.105, f32[1536,256]{1,0:T(8,128)} %get-tuple-element.58), kind=kOutput, calls=%fused_computation.111 | convolution fusion | flops 1614151680 | bytes 9961472 | tf_op jit(solution)/shard_map/dot_general | solution.py:136
  438.1 6.6 %gather_fusion.3 = s32[1024]{0:T(1024)S(1)} fusion(s32[64]{0:T(128)S(1)} %scatter_custom_fusion.1, s32[1024]{0:T(1024)S(1)} %broadcast_clamp_fusion.1), kind=kCustom, calls=%fused_computation.7 | custom fusion | bytes 12288 | tf_op jit(solution)/shard_map/jit(_take)/gather | solution.py:153
  445.1 26.9 %all-reduce.7.cloned.1.call-done = (f32[2048,256]{1,0:T(8,128)}, f32[256,2048]{1,0:T(8,128)}) async-done(((f32[2048,256]{1,0:T(8,128)}, f32[256,2048]{1,0:T(8,128)}), (f32[2048,256]{1,0:T(8,128)}, f32[256,2048]{1,0:T(8,128)})) %all-reduce.7.cloned.1.call-update) | async-done | bytes 4194320 | tf_op jit(solution)/shard_map/psum | solution.py:147
  472.1 7.9 %fusion.15 = (bf16[1,2048,256]{2,1,0:T(8,128)(2,1)}, f32[1,2048,256]{2,1,0:T(8,128)}, bf16[1,2048,256]{2,1,0:T(8,128)(2,1)}) fusion(f32[2048,256]{1,0:T(8,128)} %get-tuple-element.41, bf16[2048,256]{1,0:T(8,128)(2,1)} %all-gather.13.cloned.1.call-done, bf16[1,2048,256]{2,1,0:T(8,128)(2,1)} %param.27, pred[]{:T(512)S(6)} %ne.48, ...), kind=kLoop, calls=%fused_computation.43 | loop fusion | flops 12058624 | bytes 13631489 | tf_op jit(solution)/shard_map/broadcast_in_dim | solution.py:173
  480.0 4.4 fusion.16
  484.4 6.6 %concatenate.19 = bf16[1537,2048]{1,0:T(8,128)(2,1)} pad(bf16[1536,2048]{1,0:T(8,128)(2,1)} %bitcast.20, bf16[]{:T(256)} %constant.94.clone.1), padding=0_1x0_0 | pad | bytes 12587010 | tf_op jit(solution)/shard_map/concatenate | solution.py:158
  491.1 12.4 %gather_fusion.7 = bf16[1024,2048]{1,0:T(8,128)(2,1)} fusion(bf16[1537,2048]{1,0:T(8,128)(2,1)} %concatenate.19, s32[1024]{0:T(1024)S(1)} %broadcast_clamp_fusion), kind=kCustom, calls=%fused_computation.3.clone | custom fusion | bytes 8392704 | tf_op jit(solution)/shard_map/jit(_take)/gather | solution.py:159
  503.5 7.2 %reshape.437 = bf16[256,4,2048]{2,1,0:T(4,128)(2,1)} reshape(bf16[1024,2048]{1,0:T(8,128)(2,1)} %gather_fusion.7) | data formatting | bytes 8388608 | tf_op jit(solution)/shard_map/jit(_take)/gather | solution.py:159
  512.6 6.6 %concatenate.18 = bf16[1537,2048]{1,0:T(8,128)(2,1)} pad(bf16[1536,2048]{1,0:T(8,128)(2,1)} %bitcast.17, bf16[]{:T(256)} %constant.94.clone.1), padding=0_1x0_0 | pad | bytes 12587010 | tf_op jit(solution)/shard_map/concatenate | solution.py:158
  519.2 12.4 %gather_fusion.6 = bf16[1024,2048]{1,0:T(8,128)(2,1)} fusion(bf16[1537,2048]{1,0:T(8,128)(2,1)} %concatenate.18, s32[1024]{0:T(1024)S(1)} %broadcast_clamp_fusion), kind=kCustom, calls=%fused_computation.1.clone | custom fusion | bytes 8392704 | tf_op jit(solution)/shard_map/jit(_take)/gather | solution.py:159
  531.6 7.4 %reshape.433 = bf16[256,4,2048]{2,1,0:T(4,128)(2,1)} reshape(bf16[1024,2048]{1,0:T(8,128)(2,1)} %gather_fusion.6) | data formatting | bytes 8388608 | tf_op jit(solution)/shard_map/jit(_take)/gather | solution.py:159
  539.0 16.8 %convert_reduce_fusion = (f32[256,2048]{1,0:T(8,128)}, f32[256,2048]{1,0:T(8,128)}) fusion(bf16[256,4,2048]{2,1,0:T(4,128)(2,1)} %reshape.437, pred[256,4]{1,0:T(8,128)(4,1)S(1)} %get-tuple-element.43, bf16[256,4,2048]{2,1,0:T(4,128)(2,1)} %reshape.433), kind=kLoop, calls=%fused_computation.11 | loop fusion | flops 11534336 | bytes 12583936 | tf_op jit(solution)/shard_map/reduce_sum | solution.py:159
  555.8 2.5 reshape.299
  558.3 3.5 reshape.295
  561.8 5.6 multiply_reduce_fusion
  567.4 3.9 reduce_sum.65
  (139 shorter events, 32.6 us)
Async XLA Ops:
  7.2 73.2 %copy-start = (s32[64]{0:T(128)S(1)}, s32[64]{0:T(128)}, u32[]{:S(2)}) copy-start(s32[64]{0:T(128)} %param.22) | copy-start | bytes 772
  7.2 129.3 %all-gather.17.cloned.1.call-start = ((), (), s32[]{:S(2)}) async-start(), calls=%async_computation.9 | async-start | bytes 1572864 | tf_op jit(solution)/shard_map/all_gather | solution.py:29
  8.3 46.3 %copy-start.2 = (f32[1,2048,256]{2,1,0:T(8,128)S(1)}, f32[1,2048,256]{2,1,0:T(8,128)}, u32[]{:S(2)}) copy-start(f32[1,2048,256]{2,1,0:T(8,128)} %param.24) | copy-start | bytes 6291460
  8.3 9.2 %collective-permute-start.10 = (bf16[128,2048]{1,0:T(8,128)(2,1)S(1)}, bf16[128,2048]{1,0:T(8,128)(2,1)S(1)}, u32[]{:S(2)}, u32[]{:S(2)}) collective-permute-start(bf16[128,2048]{1,0:T(8,128)(2,1)S(1)} %dynamic-slice_bitcast_fusion), channel_id=1, source_target_pairs={{0,16},{1,17},{2,18},{3,19},{4,20},{5,21},{6,22},{7,23},{8,24},{9,... | collective-permute-start | bytes 1572872 | tf_op jit(solution)/shard_map/ppermute | solution.py:17
  17.6 9.2 %collective-permute-start.11 = (bf16[128,2048]{1,0:T(8,128)(2,1)S(1)}, bf16[128,2048]{1,0:T(8,128)(2,1)S(1)}, u32[]{:S(2)}, u32[]{:S(2)}) collective-permute-start(bf16[128,2048]{1,0:T(8,128)(2,1)S(1)} %collective-permute-done.10), channel_id=1, source_target_pairs={{0,16},{1,17},{2,18},{3,19},{4,20},{5,21},{6,22},{7,23},{8,24},{9,... | collective-permute-start | bytes 1572872 | tf_op jit(solution)/shard_map/ppermute | solution.py:17
  19.9 12.5 %collective-permute-start.8 = (bf16[128,2048]{1,0:T(8,128)(2,1)S(1)}, bf16[128,2048]{1,0:T(8,128)(2,1)}, u32[]{:S(2)}, u32[]{:S(2)}) collective-permute-start(bf16[128,2048]{1,0:T(8,128)(2,1)S(1)} %dynamic-slice_bitcast_fusion.1), channel_id=1, source_target_pairs={{0,16},{1,17},{2,18},{3,19},{4,20},{5,21},{6,22},{7,23},{8,24},{9,... | collective-permute-start | bytes 1572872 | tf_op jit(solution)/shard_map/ppermute | solution.py:17
  26.8 0.8 copy-start.16
  27.6 108.9 %all-gather.15.cloned.1.call-start = ((), (), s32[]{:S(2)}) async-start(), calls=%async_computation.8 | async-start | bytes 1572864 | tf_op jit(solution)/shard_map/all_gather | solution.py:29
  32.5 9.4 %collective-permute-start.9 = (bf16[128,2048]{1,0:T(8,128)(2,1)}, bf16[128,2048]{1,0:T(8,128)(2,1)S(1)}, u32[]{:S(2)}, u32[]{:S(2)}) collective-permute-start(bf16[128,2048]{1,0:T(8,128)(2,1)} %collective-permute-done.8), channel_id=1, source_target_pairs={{0,16},{1,17},{2,18},{3,19},{4,20},{5,21},{6,22},{7,23},{8,24},{9,... | collective-permute-start | bytes 1572872 | tf_op jit(solution)/shard_map/ppermute | solution.py:17
  34.8 12.8 %collective-permute-start.6 = (bf16[1024,256]{1,0:T(8,128)(2,1)S(1)}, bf16[1024,256]{1,0:T(8,128)(2,1)}, u32[]{:S(2)}, u32[]{:S(2)}) collective-permute-start(bf16[1024,256]{1,0:T(8,128)(2,1)S(1)} %dynamic-slice_bitcast_fusion.2), channel_id=1, source_target_pairs={{0,16},{1,17},{2,18},{3,19},{4,20},{5,21},{6,22},{7,23},{8,24},{9,... | collective-permute-start | bytes 1572872 | tf_op jit(solution)/shard_map/ppermute | solution.py:17
  41.9 0.8 copy-start.17
  41.9 20.8 %copy-start.23 = (s32[128,2]{0,1:T(2,128)S(1)}, s32[128,2]{0,1:T(2,128)}, u32[]{:S(2)}) copy-start(s32[128,2]{0,1:T(2,128)} %param.19) | copy-start | bytes 3076
  42.7 25.2 %copy-start.26 = (s32[16]{0:T(128)S(1)}, s32[16]{0:T(128)}, u32[]{:S(2)}) copy-start(s32[16]{0:T(128)} %param.21) | copy-start | bytes 196
  42.7 37.6 %copy-start.25 = (s32[64]{0:T(128)S(1)}, s32[64]{0:T(128)}, u32[]{:S(2)}) copy-start(s32[64]{0:T(128)} %param.23) | copy-start | bytes 772
  42.7 93.8 %all-gather.13.cloned.1.call-start = ((), (), s32[]{:S(2)}) async-start(), calls=%async_computation.7 | async-start | bytes 1572864 | tf_op jit(solution)/shard_map/all_gather | solution.py:29
  47.6 9.4 %collective-permute-start.7 = (bf16[1024,256]{1,0:T(8,128)(2,1)}, bf16[1024,256]{1,0:T(8,128)(2,1)S(1)}, u32[]{:S(2)}, u32[]{:S(2)}) collective-permute-start(bf16[1024,256]{1,0:T(8,128)(2,1)} %collective-permute-done.6), channel_id=1, source_target_pairs={{0,16},{1,17},{2,18},{3,19},{4,20},{5,21},{6,22},{7,23},{8,24},{9,... | collective-permute-start | bytes 1572872 | tf_op jit(solution)/shard_map/ppermute | solution.py:17
  50.8 12.2 %collective-permute-start.4 = (bf16[1024,256]{1,0:T(8,128)(2,1)}, bf16[1024,256]{1,0:T(8,128)(2,1)}, u32[]{:S(2)}, u32[]{:S(2)}) collective-permute-start(bf16[1024,256]{1,0:T(8,128)(2,1)} %dynamic-slice_bitcast_fusion.3), channel_id=1, source_target_pairs={{0,16},{1,17},{2,18},{3,19},{4,20},{5,21},{6,22},{7,23},{8,24},{9,... | collective-permute-start | bytes 1572872 | tf_op jit(solution)/shard_map/ppermute | solution.py:17
  55.5 36.6 %copy-start.24 = (f32[128,2]{0,1:T(2,128)S(1)}, f32[128,2]{0,1:T(2,128)}, u32[]{:S(2)}) copy-start(f32[128,2]{0,1:T(2,128)} %param.20) | copy-start | bytes 3076
  55.5 25.7 %collective-permute-start = (bf16[1024,256]{1,0:T(8,128)(2,1)}, bf16[1024,256]{1,0:T(8,128)(2,1)}, u32[]{:S(2)}, u32[]{:S(2)}) collective-permute-start(bf16[1024,256]{1,0:T(8,128)(2,1)} %dynamic-slice_convert_fusion.1), channel_id=1, source_target_pairs={{0,16},{1,17},{2,18},{3,19},{4,20},{5,21},{6,22},{7,23},{8,24},{9,... | collective-permute-start | bytes 1572872 | tf_op jit(solution)/shard_map/ppermute | solution.py:17
  57.0 0.8 copy-start.18
  57.8 78.7 %all-gather.11.cloned.1.call-start = ((), (), s32[]{:S(2)}) async-start(), calls=%async_computation.6 | async-start | bytes 1572864 | tf_op jit(solution)/shard_map/all_gather | solution.py:29
  60.0 41.1 %collective-permute-start.2 = (bf16[128,2048]{1,0:T(8,128)(2,1)}, bf16[128,2048]{1,0:T(8,128)(2,1)}, u32[]{:S(2)}, u32[]{:S(2)}) collective-permute-start(bf16[128,2048]{1,0:T(8,128)(2,1)} %dynamic-slice_convert_fusion), channel_id=1, source_target_pairs={{0,16},{1,17},{2,18},{3,19},{4,20},{5,21},{6,22},{7,23},{8,24},{9,... | collective-permute-start | bytes 1572872 | tf_op jit(solution)/shard_map/ppermute | solution.py:17
  63.0 16.5 %collective-permute-start.5 = (bf16[1024,256]{1,0:T(8,128)(2,1)}, bf16[1024,256]{1,0:T(8,128)(2,1)S(1)}, u32[]{:S(2)}, u32[]{:S(2)}) collective-permute-start(bf16[1024,256]{1,0:T(8,128)(2,1)} %collective-permute-done.4), channel_id=1, source_target_pairs={{0,16},{1,17},{2,18},{3,19},{4,20},{5,21},{6,22},{7,23},{8,24},{9,... | collective-permute-start | bytes 1572872 | tf_op jit(solution)/shard_map/ppermute | solution.py:17
  79.5 0.8 copy-start.19
  80.3 56.2 %all-gather.7.cloned.1.call-start = ((), (), s32[]{:S(2)}) async-start(), calls=%async_computation.4 | async-start | bytes 1572864 | tf_op jit(solution)/shard_map/all_gather | solution.py:29
  81.2 9.9 %collective-permute-start.1 = (bf16[1024,256]{1,0:T(8,128)(2,1)}, bf16[1024,256]{1,0:T(8,128)(2,1)S(1)}, u32[]{:S(2)}, u32[]{:S(2)}) collective-permute-start(bf16[1024,256]{1,0:T(8,128)(2,1)} %collective-permute-done), channel_id=1, source_target_pairs={{0,16},{1,17},{2,18},{3,19},{4,20},{5,21},{6,22},{7,23},{8,24},{9,... | collective-permute-start | bytes 1572872 | tf_op jit(solution)/shard_map/ppermute | solution.py:17
  91.1 0.8 copy-start.20
  91.9 44.6 %all-gather.9.cloned.1.call-start = ((), (), s32[]{:S(2)}) async-start(), calls=%async_computation.5 | async-start | bytes 1572864 | tf_op jit(solution)/shard_map/all_gather | solution.py:29
  101.1 10.6 %collective-permute-start.3 = (bf16[128,2048]{1,0:T(8,128)(2,1)}, bf16[128,2048]{1,0:T(8,128)(2,1)S(1)}, u32[]{:S(2)}, u32[]{:S(2)}) collective-permute-start(bf16[128,2048]{1,0:T(8,128)(2,1)} %collective-permute-done.2), channel_id=1, source_target_pairs={{0,16},{1,17},{2,18},{3,19},{4,20},{5,21},{6,22},{7,23},{8,24},{9,... | collective-permute-start | bytes 1572872 | tf_op jit(solution)/shard_map/ppermute | solution.py:17
  111.7 0.8 copy-start.21
  112.5 9.6 %copy-start.22 = (bf16[128,2048]{1,0:T(8,128)(2,1)S(1)}, bf16[128,2048]{1,0:T(8,128)(2,1)}, u32[]{:S(2)}) copy-start(bf16[128,2048]{1,0:T(8,128)(2,1)} %param.18) | copy-start | bytes 1572868
  216.5 97.4 %all-to-all-start = ((bf16[64,24,2048]{2,1,0:T(8,128)(2,1)}), bf16[64,24,2048]{2,1,0:T(8,128)(2,1)}, u32[]{:S(2)}, u32[]{:S(2)}) async-start(bf16[64,24,2048]{2,1,0:T(8,128)(2,1)} %broadcast_select_fusion), calls=%async_computation | async-start | bytes 12582912 | tf_op jit(solution)/shard_map/all_to_all | solution.py:115
  228.5 2.7 copy-start.3
  228.5 5.6 copy-start.5
  233.2 1.0 copy-start.6
  314.0 7.4 %copy-start.7 = (bf16[2048,256]{1,0:T(8,128)(2,1)S(1)}, bf16[2048,256]{1,0:T(8,128)(2,1)}, u32[]{:S(2)}) copy-start(bf16[2048,256]{1,0:T(8,128)(2,1)} %fusion.9) | copy-start | bytes 3145732
  325.8 93.6 %all-to-all-start.3 = ((bf16[64,24,2048]{2,1,0:T(8,128)(2,1)}), bf16[64,24,2048]{2,1,0:T(8,128)(2,1)}, u32[]{:S(2)}, u32[]{:S(2)}) async-start(bf16[64,24,2048]{2,1,0:T(8,128)(2,1)} %bitcast.100), calls=%async_computation.3 | async-start | bytes 12582912 | tf_op jit(solution)/shard_map/all_to_all | solution.py:143
  419.4 93.2 %all-to-all-start.1 = ((bf16[64,24,2048]{2,1,0:T(8,128)(2,1)}), bf16[64,24,2048]{2,1,0:T(8,128)(2,1)}, u32[]{:S(2)}, u32[]{:S(2)}) async-start(bf16[64,24,2048]{2,1,0:T(8,128)(2,1)} %bitcast.99), calls=%async_computation.1 | async-start | bytes 12582912 | tf_op jit(solution)/shard_map/all_to_all | solution.py:140
  430.1 41.9 %all-reduce.7.cloned.1.call-start = ((), (), s32[]{:S(2)}) async-start(), calls=%async_computation.10 | async-start | bytes 8388608 | tf_op jit(solution)/shard_map/psum | solution.py:147
  472.0 8.0 %copy-start.4 = (f32[1,256,2048]{2,1,0:T(8,128)S(1)}, f32[1,256,2048]{2,1,0:T(8,128)}, u32[]{:S(2)}) copy-start(f32[1,256,2048]{2,1,0:T(8,128)} %param.25) | copy-start | bytes 6291460
  472.0 8.0 %copy-start.8 = (bf16[256,2048]{1,0:T(8,128)(2,1)S(1)}, bf16[256,2048]{1,0:T(8,128)(2,1)}, u32[]{:S(2)}) copy-start(bf16[256,2048]{1,0:T(8,128)(2,1)} %all-gather.9.cloned.1.call-done) | copy-start | bytes 3145732
  472.0 8.0 %copy-start.9 = (bf16[1,256,2048]{2,1,0:T(8,128)(2,1)S(1)}, bf16[1,256,2048]{2,1,0:T(8,128)(2,1)}, u32[]{:S(2)}) copy-start(bf16[1,256,2048]{2,1,0:T(8,128)(2,1)} %param.29) | copy-start | bytes 3145732
  472.0 8.0 %copy-start.10 = (bf16[1,256,2048]{2,1,0:T(8,128)(2,1)S(1)}, bf16[1,256,2048]{2,1,0:T(8,128)(2,1)}, u32[]{:S(2)}) copy-start(bf16[1,256,2048]{2,1,0:T(8,128)(2,1)} %param.28) | copy-start | bytes 3145732
  472.0 8.0 %copy-start.11 = (f32[256,2048]{1,0:T(8,128)S(1)}, f32[256,2048]{1,0:T(8,128)}, u32[]{:S(2)}) copy-start(f32[256,2048]{1,0:T(8,128)} %get-tuple-element.42) | copy-start | bytes 6291460
  472.0 8.0 %copy-start.12 = (bf16[256,2048]{1,0:T(8,128)(2,1)S(1)}, bf16[256,2048]{1,0:T(8,128)(2,1)}, u32[]{:S(2)}) copy-start(bf16[256,2048]{1,0:T(8,128)(2,1)} %all-gather.17.cloned.1.call-done) | copy-start | bytes 3145732
  472.0 8.0 %copy-start.13 = (bf16[256,2048]{1,0:T(8,128)(2,1)S(1)}, bf16[256,2048]{1,0:T(8,128)(2,1)}, u32[]{:S(2)}) copy-start(bf16[256,2048]{1,0:T(8,128)(2,1)} %all-gather.15.cloned.1.call-done) | copy-start | bytes 3145732
  558.3 3.5 copy-start.15
  558.3 13.0 %copy-start.1 = (s32[64]{0:T(128)S(1)}, s32[64]{0:T(128)}, u32[]{:S(2)}) copy-start(s32[64]{0:T(128)} %param.22) | copy-start | bytes 772
  (1 other events, 0.6 us)
Sparse Core Ops, SparseCore 0:
  27.7 13.6 all-gather.16
  43.6 13.8 all-gather.14
  59.7 14.0 all-gather.12
  80.4 15.8 all-gather.10
  98.4 13.0 all-gather.6
  113.5 15.6 all-gather.8
  436.8 35.2 all-reduce.6

commit v3 on v2

--- a/solution.py
+++ b/solution.py
@@ -84,11 +84,21 @@
     send_pair = jnp.take(pair_of, target_expert, axis=0)
     send_tok = jnp.where(send_pair < npairs, send_pair // topk, count)
     gate_of = jnp.concatenate([gates.reshape(-1), jnp.zeros((1,), gates.dtype)])
-    blank = jnp.zeros((1, width), tokens.dtype)
-    send_x = jnp.take(jnp.concatenate([tokens, blank]), send_tok, axis=0)
+    pick = (send_tok[:, :, None] == jnp.arange(count, dtype=jnp.int32)[None, None, :]).astype(
+        jnp.bfloat16
+    )
+    pick = pick.reshape(nexp * slots, count)
+    send_x = (
+        jnp.dot(pick, tokens, preferred_element_type=jnp.float32)
+        .astype(jnp.bfloat16)
+        .reshape(nexp, slots, width)
+    )
     send_g = (
         jnp.take(gate_of, send_pair)[:, :, None]
-        * jnp.take(jnp.concatenate([cotangent, blank]), send_tok, axis=0).astype(jnp.float32)
+        * jnp.dot(pick, cotangent, preferred_element_type=jnp.float32)
+        .astype(jnp.bfloat16)
+        .astype(jnp.float32)
+        .reshape(nexp, slots, width)
     ).astype(jnp.bfloat16)
     weight_in, weight_out = (w_in[0], w_out[0])
     first_in, second_in, first_out, second_out = (m_in[0], v_in[0], m_out[0], v_out[0])
@@ -147,23 +157,24 @@
     grad_in, grad_out = lax.psum((grad_in, grad_out), "dp")
     new_w_in, new_m_in, new_v_in = adamw(weight_in, first_in, second_in, grad_in)
     new_w_out, new_m_out, new_v_out = adamw(weight_out, first_out, second_out, grad_out)
-    holder_of = jnp.zeros((nexp,), jnp.int32).at[held].set(jnp.arange(nexp, dtype=jnp.int32))
-    shard_ids = flat_routes[:, None] * GROUP + jnp.arange(GROUP, dtype=jnp.int32)[None, :]
-    back_row = jnp.where(
-        kept[:, None], jnp.take(holder_of, shard_ids) * slots + position[:, None], nexp * slots
-    )
-    zero = jnp.zeros((1, width), jnp.bfloat16)
-
-    def gather_sum(back):
-        table = jnp.concatenate([back.reshape(-1, width), zero])
-        return jnp.sum(jnp.take(table, back_row, axis=0).astype(jnp.float32), axis=1)
-
-    out_vals = gather_sum(back_part)
-    dx_vals = gather_sum(back_dx)
+    row_expert = jnp.repeat(target_expert, slots)
+    row_pos = jnp.tile(jnp.arange(slots, dtype=jnp.int32), nexp)
+    owns = (
+        kept[:, None]
+        & (flat_routes[:, None] == row_expert[None, :])
+        & (position[:, None] == row_pos[None, :])
+    )
+    owns_pair = owns.astype(jnp.bfloat16)
+    owns_tok = owns.reshape(count, topk, nexp * slots).any(axis=1).astype(jnp.bfloat16)
+    out_vals = jnp.dot(
+        owns_pair, back_part.reshape(-1, width), preferred_element_type=jnp.float32
+    )
     mixed = jnp.sum(out_vals.reshape(count, topk, width) * gates[:, :, None], axis=1).astype(
         jnp.bfloat16
     )
-    token_grad = jnp.sum(dx_vals.reshape(count, topk, width), axis=1).astype(jnp.bfloat16)
+    token_grad = jnp.dot(
+        owns_tok, back_dx.reshape(-1, width), preferred_element_type=jnp.float32
+    ).astype(jnp.bfloat16)
     return (
         mixed,
         token_grad,

time: 590 us -> 527 us (0.89)
  local copies, waits for them, and re-layouts: 110 us -> 30.4 us
  waiting for transfers between devices: 223 us -> 260 us
  other arithmetic: 57.8 us -> 22.1 us
  matrix products: 33.7 us -> 51.8 us
    all_to_all x1, waiting for transfers between devices: 1.9 us -> 65.3 us  [local(): lax.all_to_all(part.reshape(nexp, slots, width), 'expert', split_axis=0,...]
    gather x8 -> x0, local copies, waits for them, and re-layouts: 60.2 us -> none  [the longest x4 39.4 us: gather_sum(): jnp.take(table, back_row, axis=0).astype(jnp.float32)]
    psum x1, waiting for transfers between devices: 26.9 us -> 0.02 us  [local(): grad_in, grad_out = lax.psum((grad_in, grad_out), 'dp')]
    reduce_sum x3 -> x0, other arithmetic: 26.3 us -> none  [the longest x1 16.8 us: gather_sum(): jnp.sum(jnp.take(table, back_row, axis=0).astype(jnp.float32), axis=1)]
    dot_general x0 -> x4, matrix products: none -> 19.7 us  [the longest x1 5.67 us: local(): jnp.dot(owns_pair, back_part.reshape(-1, width), preferred_element_type=j...]
    concatenate x4 -> x0, local copies, waits for them, and re-layouts: 14.4 us -> none  [the longest x2 13.2 us: gather_sum(): table = jnp.concatenate([back.reshape(-1, width), zero])]
    all_gather x6, waiting for transfers between devices: 0.05 us -> 7.73 us  [migrate(): return tuple((lax.all_gather(m, 'dp', axis=0, tiled=True) for m in moved))]
    all_to_all x1, waiting for transfers between devices: 70.8 us -> 63.5 us  [local(): lax.all_to_all(xpart.reshape(nexp, slots, width), 'expert', split_axis=0,...]
  transfers between devices with their start and end apart: 22 -> 22, of which waited for: 13 -> 13; matrix products, arithmetic and copies ran while one was open for 21% -> 16% of each run, Pallas kernels for 0% -> 0%
where the time goes in v3:
time: 527 us; the launch traced here: 518 us
  waiting for transfers between devices  260 us (49%)
  blocking collectives  82.1 us (16%)
  starting transfers between devices  56.4 us (11%)
  matrix products  51.8 us (10%)
  local copies, waits for them, and re-layouts  30.4 us (6%)
  other arithmetic  22.1 us (4%)
  between operations  15.5 us (3%)
    all_to_all x1, blocking collectives, local(): lax.all_to_all(send_g, 'expert', split_axis=0, concat_axis=0, tiled=True)  82.1 us
    all_to_all x1, waiting for transfers between devices, local(): lax.all_to_all(send_x, 'expert', split_axis=0, concat_axis=0, tiled=True)  76.7 us
    all_to_all x1, waiting for transfers between devices, local(): lax.all_to_all(part.reshape(nexp, slots, width), 'expert', split_axis=0,...  65.3 us
    all_to_all x1, waiting for transfers between devices, local(): lax.all_to_all(xpart.reshape(nexp, slots, width), 'expert', split_axis=0,...  63.5 us
    ppermute x12, waiting for transfers between devices, relay(): return lax.ppermute(block, ('dp', 'expert'), route)  46.3 us
    ppermute x12, starting transfers between devices, relay(): return lax.ppermute(block, ('dp', 'expert'), route)  25.9 us
    all_to_all x1, starting transfers between devices, local(): lax.all_to_all(part.reshape(nexp, slots, width), 'expert', split_axis=0,...  10.6 us
  transfers between devices with their start and end apart: 22, of which 13 were waited for; matrix products, arithmetic and copies ran while one was open for 16% of the time, Pallas kernels for 0%

profile of v3, /device:TPU:50, one launch (start us, length us, event | category | flops | bytes accessed | tf_op | source)
XLA Modules:
  0.0 518.0 jit_solution(3442786277888967353)
XLA Ops:
  8.4 1.4 collective-permute-start.10
  9.7 7.9 %collective-permute-done.10 = bf16[128,2048]{1,0:T(8,128)(2,1)S(1)} collective-permute-done((bf16[128,2048]{1,0:T(8,128)(2,1)S(1)}, bf16[128,2048]{1,0:T(8,128)(2,1)S(1)}, u32[]{:S(2)}, u32[]{:S(2)}) %collective-permute-start.10) | collective-permute-done | bytes 524320 | tf_op jit(solution)/shard_map/ppermute | solution.py:17
  17.6 1.3 collective-permute-start.11
  18.9 1.9 dynamic-slice_bitcast_fusion.1
  20.8 1.4 collective-permute-start.8
  22.2 4.6 collective-permute-done.11
  27.7 4.9 collective-permute-done.8
  33.8 1.9 dynamic-slice_bitcast_fusion.2
  35.7 2.6 collective-permute-start.6
  38.3 3.6 collective-permute-done.9
  42.8 4.8 collective-permute-done.6
  47.6 1.4 collective-permute-start.7
  49.1 1.9 dynamic-slice_bitcast_fusion.3
  51.0 3.7 collective-permute-start.4
  55.5 1.5 collective-permute-done.7
  57.9 2.1 dynamic-slice_convert_fusion
  60.0 2.8 collective-permute-start.2
  63.0 3.7 collective-permute-start.5
  68.0 1.4 scatter_custom_fusion
  69.5 10.0 %collective-permute-done.5 = bf16[1024,256]{1,0:T(8,128)(2,1)S(1)} collective-permute-done((bf16[1024,256]{1,0:T(8,128)(2,1)}, bf16[1024,256]{1,0:T(8,128)(2,1)S(1)}, u32[]{:S(2)}, u32[]{:S(2)}) %collective-permute-start.5) | collective-permute-done | bytes 524320 | tf_op jit(solution)/shard_map/ppermute | solution.py:17
  81.2 2.8 collective-permute-start.1
  85.1 6.1 %collective-permute-done.1 = bf16[1024,256]{1,0:T(8,128)(2,1)S(1)} collective-permute-done((bf16[1024,256]{1,0:T(8,128)(2,1)}, bf16[1024,256]{1,0:T(8,128)(2,1)S(1)}, u32[]{:S(2)}, u32[]{:S(2)}) %collective-permute-start.1) | collective-permute-done | bytes 524320 | tf_op jit(solution)/shard_map/ppermute | solution.py:17
  92.1 9.5 %gather_fusion.2 = f32[1536]{0:T(1024)S(1)} fusion(f32[257]{0:T(512)S(1)} %pad_maximum_fusion, s32[2048]{0:T(1024)S(1)} %pad_clamp_fusion), kind=kCustom, calls=%fused_computation.2 | custom fusion | bytes 18432 | tf_op jit(solution)/shard_map/jit(_take)/gather | solution.py:97
  101.8 3.6 collective-permute-start.3
  105.4 4.1 convolution_convert_fusion.2
  109.5 3.0 collective-permute-done.3
  113.3 5.2 %convolution_convert_fusion.3 = bf16[1536,2048]{1,0:T(8,128)(2,1)} fusion(bf16[128,2048]{1,0:T(8,128)(2,1)} %param.13, s32[1536]{0:T(1024)S(1)} %fusion.33), kind=kOutput, calls=%fused_computation.9 | convolution fusion | flops 808648704 | bytes 6821888 | tf_op jit(solution)/shard_map/dot_general | solution.py:92
  118.6 3.7 fusion
  122.3 7.7 %all-gather.9.cloned.1.call-done = bf16[256,2048]{1,0:T(8,128)(2,1)} async-done(((bf16[128,2048]{1,0:T(8,128)(2,1)}), bf16[256,2048]{1,0:T(8,128)(2,1)}) %all-gather.9.cloned.1.call-update) | async-done | bytes 1048592 | tf_op jit(solution)/shard_map/all_gather | solution.py:29
  130.0 82.1 %all_to_all.20 = bf16[64,24,2048]{2,1,0:T(8,128)(2,1)} all-to-all(bf16[64,24,2048]{2,1,0:T(8,128)(2,1)} %fusion), channel_id=1, replica_groups=mesh['dp'=2,'expert'=64] {'expert'}, dimensions={0} | all-to-all | bytes 12582912 | tf_op jit(solution)/shard_map/all_to_all | solution.py:126
  212.1 9.4 %all-to-all-start = ((bf16[64,24,2048]{2,1,0:T(8,128)(2,1)}), bf16[64,24,2048]{2,1,0:T(8,128)(2,1)}, u32[]{:S(2)}, u32[]{:S(2)}) async-start(bf16[64,24,2048]{2,1,0:T(8,128)(2,1)} %bitcast.106), calls=%async_computation | async-start | bytes 12582912 | tf_op jit(solution)/shard_map/all_to_all | solution.py:125
  222.8 2.7 fusion.11
  225.4 2.0 fusion.12
  228.4 3.0 fusion.38
  231.4 76.7 %all-to-all-done = bf16[64,24,2048]{2,1,0:T(8,128)(2,1)} async-done(((bf16[64,24,2048]{2,1,0:T(8,128)(2,1)}), bf16[64,24,2048]{2,1,0:T(8,128)(2,1)}, u32[]{:S(2)}, u32[]{:S(2)}) %all-to-all-start) | async-done | bytes 6291488 | tf_op jit(solution)/shard_map/all_to_all | solution.py:125
  308.2 6.3 %fusion.9 = (bf16[1536,256]{1,0:T(8,128)(2,1)S(1)}, f32[1536,256]{1,0:T(8,128)S(1)}) fusion(f32[1536,256]{1,0:T(8,128)} %fusion.38, bf16[1536,2048]{1,0:T(8,128)(2,1)} %bitcast.13, bf16[2048,256]{1,0:T(8,128)(2,1)} %fusion.11), kind=kOutput, calls=%fused_computation.30 | convolution fusion | flops 1618477056 | bytes 11272192 | tf_op jit(solution)/shard_map/dot_general | solution.py:132
  314.5 4.6 convolution_convert_fusion.1
  319.1 10.6 %all-to-all-start.1 = ((bf16[64,24,2048]{2,1,0:T(8,128)(2,1)}), bf16[64,24,2048]{2,1,0:T(8,128)(2,1)}, u32[]{:S(2)}, u32[]{:S(2)}) async-start(bf16[64,24,2048]{2,1,0:T(8,128)(2,1)} %bitcast.105), calls=%async_computation.1 | async-start | bytes 12582912 | tf_op jit(solution)/shard_map/all_to_all | solution.py:150
  329.9 6.5 %fusion.37 = f32[256,2048]{1,0:T(8,128)} fusion(bf16[1536,2048]{1,0:T(8,128)(2,1)} %bitcast.110, f32[1536,256]{1,0:T(8,128)} %copy-done.11), kind=kOutput, calls=%fused_computation.102 | convolution fusion | flops 1614151680 | bytes 9961472 | tf_op jit(solution)/shard_map/dot_general | solution.py:146
  336.4 6.0 %fusion.39 = f32[2048,256]{1,0:T(8,128)} fusion(bf16[1536,2048]{1,0:T(8,128)(2,1)} %bitcast.13, bf16[1536,256]{1,0:T(8,128)(2,1)S(1)} %get-tuple-element.49), kind=kOutput, calls=%fused_computation.104 | convolution fusion | flops 1610612736 | bytes 9175040 | tf_op jit(solution)/shard_map/dot_general | solution.py:143
  342.4 5.7 %convolution_convert_fusion = bf16[1536,2048]{1,0:T(8,128)(2,1)} fusion(bf16[1536,256]{1,0:T(8,128)(2,1)S(1)} %get-tuple-element.49, bf16[2048,256]{1,0:T(8,128)(2,1)} %fusion.11), kind=kOutput, calls=%fused_computation.6 | convolution fusion | flops 1613758464 | bytes 8126464 | tf_op jit(solution)/shard_map/dot_general | solution.py:140
  348.2 65.3 %all-to-all-done.1 = bf16[64,24,2048]{2,1,0:T(8,128)(2,1)} async-done(((bf16[64,24,2048]{2,1,0:T(8,128)(2,1)}), bf16[64,24,2048]{2,1,0:T(8,128)(2,1)}, u32[]{:S(2)}, u32[]{:S(2)}) %all-to-all-start.1) | async-done | bytes 6291488 | tf_op jit(solution)/shard_map/all_to_all | solution.py:150
  413.5 10.0 %all-to-all-start.3 = ((bf16[64,24,2048]{2,1,0:T(8,128)(2,1)}), bf16[64,24,2048]{2,1,0:T(8,128)(2,1)}, u32[]{:S(2)}, u32[]{:S(2)}) async-start(bf16[64,24,2048]{2,1,0:T(8,128)(2,1)} %bitcast.104), calls=%async_computation.3 | async-start | bytes 12582912 | tf_op jit(solution)/shard_map/all_to_all | solution.py:153
  424.8 7.9 %fusion.17 = (bf16[1,2048,256]{2,1,0:T(8,128)(2,1)}, f32[1,2048,256]{2,1,0:T(8,128)}, bf16[1,2048,256]{2,1,0:T(8,128)(2,1)}) fusion(f32[2048,256]{1,0:T(8,128)} %get-tuple-element.37, bf16[2048,256]{1,0:T(8,128)(2,1)} %all-gather.13.cloned.1.call-done, bf16[1,2048,256]{2,1,0:T(8,128)(2,1)} %param.23, pred[]{:T(512)S(6)} %ne.53, ...), kind=kLoop, calls=%fused_computation.40 | loop fusion | flops 12058624 | bytes 13631489 | tf_op jit(solution)/shard_map/broadcast_in_dim | solution.py:184
  432.7 4.4 fusion.18
  437.1 5.7 %fusion.10 = bf16[128,2048]{1,0:T(8,128)(2,1)} fusion(bf16[1536,2048,1]{1,0,2:T(8,128)(2,1)} %bitcast.18, f32[128,2]{0,1:T(2,128)S(1)} %copy-done.24, s32[1536]{0:T(1024)S(1)} %eq.94, s32[128,2]{0,1:T(2,128)S(1)} %copy.25, s32[1536]{0:T(1024)S(1)} %eq.90, s32[128,2]{0,1:T(2,128)S(1)} %copy-done.23, pred[128,2]{0,1:T(4,128)(4,1)S(1)} %copy.24), kind=kOutput, calls=%fused_computation.33 | convolution fusion | flops 1612972032 | bytes 6831360 | tf_op jit(solution)/shard_map/dot_general | solution.py:169
  442.8 63.5 %all-to-all-done.3 = bf16[64,24,2048]{2,1,0:T(8,128)(2,1)} async-done(((bf16[64,24,2048]{2,1,0:T(8,128)(2,1)}), bf16[64,24,2048]{2,1,0:T(8,128)(2,1)}, u32[]{:S(2)}, u32[]{:S(2)}) %all-to-all-start.3) | async-done | bytes 6291488 | tf_op jit(solution)/shard_map/all_to_all | solution.py:153
  506.3 4.6 convolution_convert_fusion.4
  (124 shorter events, 15.2 us)
Async XLA Ops:
  7.2 98.2 %copy-start = (bf16[128,2048]{1,0:T(8,128)(2,1)S(1)}, bf16[128,2048]{1,0:T(8,128)(2,1)}, u32[]{:S(2)}) copy-start(bf16[128,2048]{1,0:T(8,128)(2,1)} %param.14) | copy-start | bytes 1572868
  7.2 115.1 %all-gather.17.cloned.1.call-start = ((), (), s32[]{:S(2)}) async-start(), calls=%async_computation.9 | async-start | bytes 1572864 | tf_op jit(solution)/shard_map/all_gather | solution.py:29
  8.4 46.3 %copy-start.4 = (f32[1,2048,256]{2,1,0:T(8,128)S(1)}, f32[1,2048,256]{2,1,0:T(8,128)}, u32[]{:S(2)}) copy-start(f32[1,2048,256]{2,1,0:T(8,128)} %param.20) | copy-start | bytes 6291460
  8.4 9.2 %collective-permute-start.10 = (bf16[128,2048]{1,0:T(8,128)(2,1)S(1)}, bf16[128,2048]{1,0:T(8,128)(2,1)S(1)}, u32[]{:S(2)}, u32[]{:S(2)}) collective-permute-start(bf16[128,2048]{1,0:T(8,128)(2,1)S(1)} %dynamic-slice_bitcast_fusion), channel_id=1, source_target_pairs={{0,16},{1,17},{2,18},{3,19},{4,20},{5,21},{6,22},{7,23},{8,24},{9,... | collective-permute-start | bytes 1572872 | tf_op jit(solution)/shard_map/ppermute | solution.py:17
  17.6 9.2 %collective-permute-start.11 = (bf16[128,2048]{1,0:T(8,128)(2,1)S(1)}, bf16[128,2048]{1,0:T(8,128)(2,1)S(1)}, u32[]{:S(2)}, u32[]{:S(2)}) collective-permute-start(bf16[128,2048]{1,0:T(8,128)(2,1)S(1)} %collective-permute-done.10), channel_id=1, source_target_pairs={{0,16},{1,17},{2,18},{3,19},{4,20},{5,21},{6,22},{7,23},{8,24},{9,... | collective-permute-start | bytes 1572872 | tf_op jit(solution)/shard_map/ppermute | solution.py:17
  20.8 11.7 %collective-permute-start.8 = (bf16[128,2048]{1,0:T(8,128)(2,1)}, bf16[128,2048]{1,0:T(8,128)(2,1)}, u32[]{:S(2)}, u32[]{:S(2)}) collective-permute-start(bf16[128,2048]{1,0:T(8,128)(2,1)} %dynamic-slice_bitcast_fusion.1), channel_id=1, source_target_pairs={{0,16},{1,17},{2,18},{3,19},{4,20},{5,21},{6,22},{7,23},{8,24},{9,... | collective-permute-start | bytes 1572872 | tf_op jit(solution)/shard_map/ppermute | solution.py:17
  26.8 0.8 copy-start.17
  27.6 94.7 %all-gather.15.cloned.1.call-start = ((), (), s32[]{:S(2)}) async-start(), calls=%async_computation.8 | async-start | bytes 1572864 | tf_op jit(solution)/shard_map/all_gather | solution.py:29
  32.5 9.4 %collective-permute-start.9 = (bf16[128,2048]{1,0:T(8,128)(2,1)}, bf16[128,2048]{1,0:T(8,128)(2,1)S(1)}, u32[]{:S(2)}, u32[]{:S(2)}) collective-permute-start(bf16[128,2048]{1,0:T(8,128)(2,1)} %collective-permute-done.8), channel_id=1, source_target_pairs={{0,16},{1,17},{2,18},{3,19},{4,20},{5,21},{6,22},{7,23},{8,24},{9,... | collective-permute-start | bytes 1572872 | tf_op jit(solution)/shard_map/ppermute | solution.py:17
  35.7 12.0 %collective-permute-start.6 = (bf16[1024,256]{1,0:T(8,128)(2,1)}, bf16[1024,256]{1,0:T(8,128)(2,1)}, u32[]{:S(2)}, u32[]{:S(2)}) collective-permute-start(bf16[1024,256]{1,0:T(8,128)(2,1)} %dynamic-slice_bitcast_fusion.2), channel_id=1, source_target_pairs={{0,16},{1,17},{2,18},{3,19},{4,20},{5,21},{6,22},{7,23},{8,24},{9,... | collective-permute-start | bytes 1572872 | tf_op jit(solution)/shard_map/ppermute | solution.py:17
  41.9 0.8 copy-start.18
  41.9 20.8 %copy-start.23 = (s32[128,2]{0,1:T(2,128)S(1)}, s32[128,2]{0,1:T(2,128)}, u32[]{:S(2)}) copy-start(s32[128,2]{0,1:T(2,128)} %param.15) | copy-start | bytes 3076
  42.7 25.2 %copy-start.26 = (s32[16]{0:T(128)S(1)}, s32[16]{0:T(128)}, u32[]{:S(2)}) copy-start(s32[16]{0:T(128)} %param.17) | copy-start | bytes 196
  42.8 37.6 %copy-start.25 = (s32[64]{0:T(128)S(1)}, s32[64]{0:T(128)}, u32[]{:S(2)}) copy-start(s32[64]{0:T(128)} %param.19) | copy-start | bytes 772
  42.8 37.6 %copy-start.2 = (s32[64]{0:T(128)S(1)}, s32[64]{0:T(128)}, u32[]{:S(2)}) copy-start(s32[64]{0:T(128)} %param.18) | copy-start | bytes 772
  42.8 79.5 %all-gather.13.cloned.1.call-start = ((), (), s32[]{:S(2)}) async-start(), calls=%async_computation.7 | async-start | bytes 1572864 | tf_op jit(solution)/shard_map/all_gather | solution.py:29
  47.6 9.4 %collective-permute-start.7 = (bf16[1024,256]{1,0:T(8,128)(2,1)}, bf16[1024,256]{1,0:T(8,128)(2,1)S(1)}, u32[]{:S(2)}, u32[]{:S(2)}) collective-permute-start(bf16[1024,256]{1,0:T(8,128)(2,1)} %collective-permute-done.6), channel_id=1, source_target_pairs={{0,16},{1,17},{2,18},{3,19},{4,20},{5,21},{6,22},{7,23},{8,24},{9,... | collective-permute-start | bytes 1572872 | tf_op jit(solution)/shard_map/ppermute | solution.py:17
  51.0 12.1 %collective-permute-start.4 = (bf16[1024,256]{1,0:T(8,128)(2,1)}, bf16[1024,256]{1,0:T(8,128)(2,1)}, u32[]{:S(2)}, u32[]{:S(2)}) collective-permute-start(bf16[1024,256]{1,0:T(8,128)(2,1)} %dynamic-slice_bitcast_fusion.3), channel_id=1, source_target_pairs={{0,16},{1,17},{2,18},{3,19},{4,20},{5,21},{6,22},{7,23},{8,24},{9,... | collective-permute-start | bytes 1572872 | tf_op jit(solution)/shard_map/ppermute | solution.py:17
  54.7 30.2 %copy-start.24 = (f32[128,2]{0,1:T(2,128)S(1)}, f32[128,2]{0,1:T(2,128)}, u32[]{:S(2)}) copy-start(f32[128,2]{0,1:T(2,128)} %param.16) | copy-start | bytes 3076
  55.5 25.7 %collective-permute-start = (bf16[1024,256]{1,0:T(8,128)(2,1)}, bf16[1024,256]{1,0:T(8,128)(2,1)}, u32[]{:S(2)}, u32[]{:S(2)}) collective-permute-start(bf16[1024,256]{1,0:T(8,128)(2,1)} %dynamic-slice_convert_fusion.1), channel_id=1, source_target_pairs={{0,16},{1,17},{2,18},{3,19},{4,20},{5,21},{6,22},{7,23},{8,24},{9,... | collective-permute-start | bytes 1572872 | tf_op jit(solution)/shard_map/ppermute | solution.py:17
  57.0 0.8 copy-start.19
  57.9 64.4 %all-gather.11.cloned.1.call-start = ((), (), s32[]{:S(2)}) async-start(), calls=%async_computation.6 | async-start | bytes 1572864 | tf_op jit(solution)/shard_map/all_gather | solution.py:29
  60.0 41.8 %collective-permute-start.2 = (bf16[128,2048]{1,0:T(8,128)(2,1)}, bf16[128,2048]{1,0:T(8,128)(2,1)}, u32[]{:S(2)}, u32[]{:S(2)}) collective-permute-start(bf16[128,2048]{1,0:T(8,128)(2,1)} %dynamic-slice_convert_fusion), channel_id=1, source_target_pairs={{0,16},{1,17},{2,18},{3,19},{4,20},{5,21},{6,22},{7,23},{8,24},{9,... | collective-permute-start | bytes 1572872 | tf_op jit(solution)/shard_map/ppermute | solution.py:17
  63.0 16.5 %collective-permute-start.5 = (bf16[1024,256]{1,0:T(8,128)(2,1)}, bf16[1024,256]{1,0:T(8,128)(2,1)S(1)}, u32[]{:S(2)}, u32[]{:S(2)}) collective-permute-start(bf16[1024,256]{1,0:T(8,128)(2,1)} %collective-permute-done.4), channel_id=1, source_target_pairs={{0,16},{1,17},{2,18},{3,19},{4,20},{5,21},{6,22},{7,23},{8,24},{9,... | collective-permute-start | bytes 1572872 | tf_op jit(solution)/shard_map/ppermute | solution.py:17
  79.5 0.8 copy-start.20
  80.3 42.0 %all-gather.7.cloned.1.call-start = ((), (), s32[]{:S(2)}) async-start(), calls=%async_computation.4 | async-start | bytes 1572864 | tf_op jit(solution)/shard_map/all_gather | solution.py:29
  81.2 9.9 %collective-permute-start.1 = (bf16[1024,256]{1,0:T(8,128)(2,1)}, bf16[1024,256]{1,0:T(8,128)(2,1)S(1)}, u32[]{:S(2)}, u32[]{:S(2)}) collective-permute-start(bf16[1024,256]{1,0:T(8,128)(2,1)} %collective-permute-done), channel_id=1, source_target_pairs={{0,16},{1,17},{2,18},{3,19},{4,20},{5,21},{6,22},{7,23},{8,24},{9,... | collective-permute-start | bytes 1572872 | tf_op jit(solution)/shard_map/ppermute | solution.py:17
  91.2 0.8 copy-start.21
  92.0 38.0 %all-gather.9.cloned.1.call-start = ((), (), s32[]{:S(2)}) async-start(), calls=%async_computation.5 | async-start | bytes 1572864 | tf_op jit(solution)/shard_map/all_gather | solution.py:29
  101.8 10.7 %collective-permute-start.3 = (bf16[128,2048]{1,0:T(8,128)(2,1)}, bf16[128,2048]{1,0:T(8,128)(2,1)S(1)}, u32[]{:S(2)}, u32[]{:S(2)}) collective-permute-start(bf16[128,2048]{1,0:T(8,128)(2,1)} %collective-permute-done.2), channel_id=1, source_target_pairs={{0,16},{1,17},{2,18},{3,19},{4,20},{5,21},{6,22},{7,23},{8,24},{9,... | collective-permute-start | bytes 1572872 | tf_op jit(solution)/shard_map/ppermute | solution.py:17
  113.3 5.3 %copy-start.3 = (bf16[1536,2048]{1,0:T(8,128)(2,1)S(1)}, bf16[1536,2048]{1,0:T(8,128)(2,1)}, u32[]{:S(2)}) copy-start(bf16[1536,2048]{1,0:T(8,128)(2,1)} %convolution_convert_fusion.2) | copy-start | bytes 18874372
  212.1 96.0 %all-to-all-start = ((bf16[64,24,2048]{2,1,0:T(8,128)(2,1)}), bf16[64,24,2048]{2,1,0:T(8,128)(2,1)}, u32[]{:S(2)}, u32[]{:S(2)}) async-start(bf16[64,24,2048]{2,1,0:T(8,128)(2,1)} %bitcast.106), calls=%async_computation | async-start | bytes 12582912 | tf_op jit(solution)/shard_map/all_to_all | solution.py:125
  222.8 2.7 copy-start.5
  222.8 5.6 %copy-start.7 = (bf16[64,24,2048]{2,1,0:T(8,128)(2,1)S(1)}, bf16[64,24,2048]{2,1,0:T(8,128)(2,1)}, u32[]{:S(2)}) copy-start(bf16[64,24,2048]{2,1,0:T(8,128)(2,1)} %all_to_all.20) | copy-start | bytes 18874372
  227.4 1.0 copy-start.8
  308.1 6.3 %copy-start.9 = (bf16[256,2048]{1,0:T(8,128)(2,1)S(1)}, bf16[256,2048]{1,0:T(8,128)(2,1)}, u32[]{:S(2)}) copy-start(bf16[256,2048]{1,0:T(8,128)(2,1)} %copy-done.8) | copy-start | bytes 3145732
  314.5 4.6 copy-start.11
  319.1 94.4 %all-to-all-start.1 = ((bf16[64,24,2048]{2,1,0:T(8,128)(2,1)}), bf16[64,24,2048]{2,1,0:T(8,128)(2,1)}, u32[]{:S(2)}, u32[]{:S(2)}) async-start(bf16[64,24,2048]{2,1,0:T(8,128)(2,1)} %bitcast.105), calls=%async_computation.1 | async-start | bytes 12582912 | tf_op jit(solution)/shard_map/all_to_all | solution.py:150
  329.7 95.0 %all-reduce.3.cloned.1.call-start = ((), (), s32[]{:S(2)}) async-start(), calls=%async_computation.10 | async-start | bytes 8388608 | tf_op jit(solution)/shard_map/psum | solution.py:157
  413.5 92.9 %all-to-all-start.3 = ((bf16[64,24,2048]{2,1,0:T(8,128)(2,1)}), bf16[64,24,2048]{2,1,0:T(8,128)(2,1)}, u32[]{:S(2)}, u32[]{:S(2)}) async-start(bf16[64,24,2048]{2,1,0:T(8,128)(2,1)} %bitcast.104), calls=%async_computation.3 | async-start | bytes 12582912 | tf_op jit(solution)/shard_map/all_to_all | solution.py:153
  424.7 8.0 %copy-start.6 = (f32[1,256,2048]{2,1,0:T(8,128)S(1)}, f32[1,256,2048]{2,1,0:T(8,128)}, u32[]{:S(2)}) copy-start(f32[1,256,2048]{2,1,0:T(8,128)} %param.21) | copy-start | bytes 6291460
  424.7 8.0 %copy-start.10 = (bf16[256,2048]{1,0:T(8,128)(2,1)S(1)}, bf16[256,2048]{1,0:T(8,128)(2,1)}, u32[]{:S(2)}) copy-start(bf16[256,2048]{1,0:T(8,128)(2,1)} %all-gather.9.cloned.1.call-done) | copy-start | bytes 3145732
  424.7 8.0 %copy-start.12 = (bf16[1,256,2048]{2,1,0:T(8,128)(2,1)S(1)}, bf16[1,256,2048]{2,1,0:T(8,128)(2,1)}, u32[]{:S(2)}) copy-start(bf16[1,256,2048]{2,1,0:T(8,128)(2,1)} %param.25) | copy-start | bytes 3145732
  424.7 8.0 %copy-start.13 = (bf16[1,256,2048]{2,1,0:T(8,128)(2,1)S(1)}, bf16[1,256,2048]{2,1,0:T(8,128)(2,1)}, u32[]{:S(2)}) copy-start(bf16[1,256,2048]{2,1,0:T(8,128)(2,1)} %param.24) | copy-start | bytes 3145732
  424.7 8.0 %copy-start.14 = (f32[256,2048]{1,0:T(8,128)S(1)}, f32[256,2048]{1,0:T(8,128)}, u32[]{:S(2)}) copy-start(f32[256,2048]{1,0:T(8,128)} %get-tuple-element.38) | copy-start | bytes 6291460
  424.8 8.0 %copy-start.15 = (bf16[256,2048]{1,0:T(8,128)(2,1)S(1)}, bf16[256,2048]{1,0:T(8,128)(2,1)}, u32[]{:S(2)}) copy-start(bf16[256,2048]{1,0:T(8,128)(2,1)} %all-gather.17.cloned.1.call-done) | copy-start | bytes 3145732
  424.8 8.0 %copy-start.16 = (bf16[256,2048]{1,0:T(8,128)(2,1)S(1)}, bf16[256,2048]{1,0:T(8,128)(2,1)}, u32[]{:S(2)}) copy-start(bf16[256,2048]{1,0:T(8,128)(2,1)} %all-gather.15.cloned.1.call-done) | copy-start | bytes 3145732
  506.3 4.6 copy-start.1
  (1 other events, 0.8 us)
Sparse Core Ops, SparseCore 0:
  27.7 13.6 all-gather.16
  43.6 13.8 all-gather.14
  59.8 14.0 all-gather.12
  80.4 15.8 all-gather.10
  98.4 13.0 all-gather.6
  113.6 16.4 all-gather.8
  342.5 35.2 all-reduce.2

commit v4 on v3

--- a/solution.py
+++ b/solution.py
@@ -21,12 +21,22 @@
     ndp = lax.axis_size("dp")
     step = lax.axis_size("expert") // 4
     here = lax.axis_index("dp")
-    halves = tuple(
+    halves = [
         lax.dynamic_slice_in_dim(b, here * (b.shape[0] // ndp), b.shape[0] // ndp, 0)
         for b in blocks
-    )
-    moved = relay(relay(halves, step), step)
-    return tuple(lax.all_gather(m, "dp", axis=0, tiled=True) for m in moved)
+    ]
+    lanes = 128
+    packed = jnp.concatenate([h.reshape(-1, lanes) for h in halves], axis=0)
+    moved = relay(relay(packed, step), step)
+    whole = lax.all_gather(moved, "dp", axis=0, tiled=False)
+    out = []
+    offset = 0
+    for h in halves:
+        n = h.size // lanes
+        piece = whole[:, offset : offset + n].reshape((ndp * h.shape[0],) + h.shape[1:])
+        out.append(piece)
+        offset += n
+    return tuple(out)
 
 
 def gelu_tanh(value):

time: 527 us -> 551 us (1.046)
  the two profiles are of different devices: /device:TPU:50 before, /device:TPU:18 now
where the time goes in v4:
time: 551 us; the launch traced here: 541 us
  waiting for transfers between devices  267 us (48%)
  blocking collectives  83.4 us (15%)
  starting transfers between devices  52.1 us (9%)
  matrix products  51.5 us (9%)
  local copies, waits for them, and re-layouts  51.4 us (9%)
  other arithmetic  20.5 us (4%)
  between operations  15.7 us (3%)
    all_to_all x1, blocking collectives, local(): lax.all_to_all(send_g, 'expert', split_axis=0, concat_axis=0, tiled=True)  83.4 us
    ppermute x2, waiting for transfers between devices, relay(): return lax.ppermute(block, ('dp', 'expert'), route)  72.1 us
    all_to_all x1, waiting for transfers between devices, local(): lax.all_to_all(send_x, 'expert', split_axis=0, concat_axis=0, tiled=True)  69.7 us
    all_to_all x1, waiting for transfers between devices, local(): lax.all_to_all(xpart.reshape(nexp, slots, width), 'expert', split_axis=0,...  63.8 us
    all_to_all x1, waiting for transfers between devices, local(): lax.all_to_all(part.reshape(nexp, slots, width), 'expert', split_axis=0,...  61.1 us
    all_to_all x1, starting transfers between devices, local(): lax.all_to_all(send_x, 'expert', split_axis=0, concat_axis=0, tiled=True)  19 us
    all_to_all x1, starting transfers between devices, local(): lax.all_to_all(xpart.reshape(nexp, slots, width), 'expert', split_axis=0,...  16.4 us
    all_to_all x1, starting transfers between devices, local(): lax.all_to_all(part.reshape(nexp, slots, width), 'expert', split_axis=0,...  13.9 us
  transfers between devices with their start and end apart: 7, of which 5 were waited for; matrix products, arithmetic and copies ran while one was open for 13% of the time, Pallas kernels for 0%

profile of v4, /device:TPU:18, one launch (start us, length us, event | category | flops | bytes accessed | tf_op | source)
XLA Modules:
  0.0 541.4 jit_solution(4192429837756728056)
XLA Ops:
  7.2 1.4 dynamic-slice_convert_fusion
  8.7 1.0 reshape.359
  9.8 1.0 reshape.358
  10.8 2.1 constant_dynamic-slice_fusion.2
  12.8 2.0 reshape.361
  14.8 1.0 reshape.360
  15.8 2.1 constant_dynamic-slice_fusion
  17.9 2.1 reshape.363
  19.9 1.0 reshape.362
  21.0 1.2 constant_dynamic-update-slice_fusion.5
  22.2 1.2 constant_dynamic-update-slice_fusion.4
  23.8 1.4 collective-permute-start
  25.1 36.0 %collective-permute-done = bf16[12288,128]{1,0:T(8,128)(2,1)S(1)} collective-permute-done((bf16[12288,128]{1,0:T(8,128)(2,1)S(1)}, bf16[12288,128]{1,0:T(8,128)(2,1)S(1)}, u32[]{:S(2)}, u32[]{:S(2)}) %collective-permute-start) | collective-permute-done | bytes 3145760 | tf_op jit(solution)/shard_map/ppermute | solution.py:17
  61.1 1.3 collective-permute-start.1
  62.4 36.1 %collective-permute-done.1 = bf16[12288,128]{1,0:T(8,128)(2,1)} collective-permute-done((bf16[12288,128]{1,0:T(8,128)(2,1)S(1)}, bf16[12288,128]{1,0:T(8,128)(2,1)}, u32[]{:S(2)}, u32[]{:S(2)}) %collective-permute-start.1) | collective-permute-done | bytes 3145760 | tf_op jit(solution)/shard_map/ppermute | solution.py:17
  100.1 1.4 scatter_custom_fusion
  101.7 0.8 gather_fusion
  102.5 0.6 gather_fusion.1
  103.6 9.5 %gather_fusion.2 = f32[1536]{0:T(1024)S(1)} fusion(f32[257]{0:T(512)S(1)} %pad_maximum_fusion, s32[2048]{0:T(1024)S(1)} %pad_clamp_fusion), kind=kCustom, calls=%fused_computation.2 | custom fusion | bytes 18432 | tf_op jit(solution)/shard_map/jit(_take)/gather | solution.py:107
  113.3 2.4 convolution_convert_fusion.2
  115.7 4.0 convolution_convert_fusion.3
  119.8 3.7 fusion
  123.5 5.5 %fusion.38 = (bf16[2,2048,128]{2,1,0:T(8,128)(2,1)}, bf16[2,2048,128]{2,1,0:T(8,128)(2,1)}, bf16[2,2048,128]{2,1,0:T(8,128)(2,1)}, bf16[2,2048,128]{2,1,0:T(8,12...) fusion(bf16[2,12288,128]{2,1,0:T(8,128)(2,1)} %bitcast.103), kind=kLoop, calls=%fused_computation.109 | loop fusion | bytes 12582912 | tf_op jit(solution)/shard_map/slice | solution.py:36
  129.0 2.3 reshape.369
  131.4 2.3 reshape.368
  133.7 2.2 reshape.367
  135.9 2.2 reshape.366
  138.1 2.3 reshape.365
  140.4 2.2 reshape.364
  142.6 83.4 %all_to_all.20 = bf16[64,24,2048]{2,1,0:T(8,128)(2,1)} all-to-all(bf16[64,24,2048]{2,1,0:T(8,128)(2,1)} %fusion), channel_id=1, replica_groups=mesh['dp'=2,'expert'=64] {'expert'}, dimensions={0} | all-to-all | bytes 12582912 | tf_op jit(solution)/shard_map/all_to_all | solution.py:136
  226.0 19.0 %all-to-all-start = ((bf16[64,24,2048]{2,1,0:T(8,128)(2,1)}), bf16[64,24,2048]{2,1,0:T(8,128)(2,1)}, u32[]{:S(2)}, u32[]{:S(2)}) async-start(bf16[64,24,2048]{2,1,0:T(8,128)(2,1)} %bitcast.99), calls=%async_computation | async-start | bytes 12582912 | tf_op jit(solution)/shard_map/all_to_all | solution.py:135
  246.3 2.7 fusion.11
  249.3 1.0 copy-done.8
  250.2 5.8 %fusion.39 = f32[1536,256]{1,0:T(8,128)} fusion(bf16[1536,2048]{1,0:T(8,128)(2,1)} %bitcast.104, bf16[256,2048]{1,0:T(8,128)(2,1)S(1)} %fusion.12), kind=kOutput, calls=%fused_computation.110 | convolution fusion | flops 1610612736 | bytes 8912896 | tf_op jit(solution)/shard_map/dot_general | solution.py:146
  256.0 69.7 %all-to-all-done = bf16[64,24,2048]{2,1,0:T(8,128)(2,1)} async-done(((bf16[64,24,2048]{2,1,0:T(8,128)(2,1)}), bf16[64,24,2048]{2,1,0:T(8,128)(2,1)}, u32[]{:S(2)}, u32[]{:S(2)}) %all-to-all-start) | async-done | bytes 6291488 | tf_op jit(solution)/shard_map/all_to_all | solution.py:135
  325.8 6.3 %fusion.9 = (bf16[1536,256]{1,0:T(8,128)(2,1)S(1)}, f32[1536,256]{1,0:T(8,128)S(1)}) fusion(f32[1536,256]{1,0:T(8,128)} %fusion.39, bf16[1536,2048]{1,0:T(8,128)(2,1)} %bitcast.10, bf16[2048,256]{1,0:T(8,128)(2,1)} %fusion.11), kind=kOutput, calls=%fused_computation.30 | convolution fusion | flops 1618477056 | bytes 11272192 | tf_op jit(solution)/shard_map/dot_general | solution.py:142
  332.1 4.5 convolution_convert_fusion.1
  336.7 13.9 %all-to-all-start.1 = ((bf16[64,24,2048]{2,1,0:T(8,128)(2,1)}), bf16[64,24,2048]{2,1,0:T(8,128)(2,1)}, u32[]{:S(2)}, u32[]{:S(2)}) async-start(bf16[64,24,2048]{2,1,0:T(8,128)(2,1)} %bitcast.98), calls=%async_computation.1 | async-start | bytes 12582912 | tf_op jit(solution)/shard_map/all_to_all | solution.py:160
  350.7 6.5 %fusion.37 = f32[256,2048]{1,0:T(8,128)} fusion(bf16[1536,2048]{1,0:T(8,128)(2,1)} %bitcast.105, f32[1536,256]{1,0:T(8,128)} %copy-done.12), kind=kOutput, calls=%fused_computation.108 | convolution fusion | flops 1614151680 | bytes 9961472 | tf_op jit(solution)/shard_map/dot_general | solution.py:156
  357.2 6.0 %fusion.40 = f32[2048,256]{1,0:T(8,128)} fusion(bf16[1536,2048]{1,0:T(8,128)(2,1)} %bitcast.10, bf16[1536,256]{1,0:T(8,128)(2,1)S(1)} %get-tuple-element.55), kind=kOutput, calls=%fused_computation.111 | convolution fusion | flops 1610612736 | bytes 9175040 | tf_op jit(solution)/shard_map/dot_general | solution.py:153
  363.2 5.7 %convolution_convert_fusion = bf16[1536,2048]{1,0:T(8,128)(2,1)} fusion(bf16[1536,256]{1,0:T(8,128)(2,1)S(1)} %get-tuple-element.55, bf16[2048,256]{1,0:T(8,128)(2,1)} %fusion.11), kind=kOutput, calls=%fused_computation.6 | convolution fusion | flops 1613758464 | bytes 8126464 | tf_op jit(solution)/shard_map/dot_general | solution.py:150
  368.9 61.1 %all-to-all-done.1 = bf16[64,24,2048]{2,1,0:T(8,128)(2,1)} async-done(((bf16[64,24,2048]{2,1,0:T(8,128)(2,1)}), bf16[64,24,2048]{2,1,0:T(8,128)(2,1)}, u32[]{:S(2)}, u32[]{:S(2)}) %all-to-all-start.1) | async-done | bytes 6291488 | tf_op jit(solution)/shard_map/all_to_all | solution.py:160
  430.0 16.4 %all-to-all-start.3 = ((bf16[64,24,2048]{2,1,0:T(8,128)(2,1)}), bf16[64,24,2048]{2,1,0:T(8,128)(2,1)}, u32[]{:S(2)}, u32[]{:S(2)}) async-start(bf16[64,24,2048]{2,1,0:T(8,128)(2,1)} %bitcast.97), calls=%async_computation.3 | async-start | bytes 12582912 | tf_op jit(solution)/shard_map/all_to_all | solution.py:163
  447.7 7.9 %fusion.17 = (bf16[1,2048,256]{2,1,0:T(8,128)(2,1)}, f32[1,2048,256]{2,1,0:T(8,128)}, bf16[1,2048,256]{2,1,0:T(8,128)(2,1)}) fusion(f32[2048,256]{1,0:T(8,128)} %get-tuple-element.37, bf16[2048,256]{1,0:T(8,128)(2,1)} %reshape.367, bf16[1,2048,256]{2,1,0:T(8,128)(2,1)} %param.23, pred[]{:T(512)S(6)} %ne.53, bf16[2048,256]{1,0:T(8,128)(2,1)} %reshape.366, ...), kind=kLoop, calls=%fused_computation.40 | loop fusion | flops 12058624 | bytes 13631489 | tf_op jit(solution)/shard_map/broadcast_in_dim | solution.py:194
  455.7 4.4 fusion.18
  460.1 5.7 %fusion.10 = bf16[128,2048]{1,0:T(8,128)(2,1)} fusion(bf16[1536,2048,1]{1,0,2:T(8,128)(2,1)} %bitcast.15, f32[128,2]{0,1:T(2,128)S(1)} %copy-done.22, s32[1536]{0:T(1024)S(1)} %eq.94, s32[128,2]{0,1:T(2,128)S(1)} %copy.25, s32[1536]{0:T(1024)S(1)} %eq.90, s32[128,2]{0,1:T(2,128)S(1)} %copy-done.21, pred[128,2]{0,1:T(4,128)(4,1)S(1)} %copy.24), kind=kOutput, calls=%fused_computation.33 | convolution fusion | flops 1612972032 | bytes 6831360 | tf_op jit(solution)/shard_map/dot_general | solution.py:179
  465.8 63.8 %all-to-all-done.3 = bf16[64,24,2048]{2,1,0:T(8,128)(2,1)} async-done(((bf16[64,24,2048]{2,1,0:T(8,128)(2,1)}), bf16[64,24,2048]{2,1,0:T(8,128)(2,1)}, u32[]{:S(2)}, u32[]{:S(2)}) %all-to-all-start.3) | async-done | bytes 6291488 | tf_op jit(solution)/shard_map/all_to_all | solution.py:163
  529.6 4.6 convolution_convert_fusion.4
  (102 shorter events, 5.0 us)
Async XLA Ops:
  7.2 106.2 %copy-start = (bf16[128,2048]{1,0:T(8,128)(2,1)S(1)}, bf16[128,2048]{1,0:T(8,128)(2,1)}, u32[]{:S(2)}) copy-start(bf16[128,2048]{1,0:T(8,128)(2,1)} %param.14) | copy-start | bytes 1572868
  7.2 2.5 copy-start.3
  7.2 116.3 %all-gather.3.cloned.1.call-start = ((), (), s32[]{:S(2)}) async-start(), calls=%async_computation.4 | async-start | bytes 9437184 | tf_op jit(solution)/shard_map/all_gather | solution.py:31
  21.0 2.4 copy-start.17
  21.0 2.5 copy-start.15
  21.0 2.6 copy-start.18
  22.2 1.4 copy-start.16
  23.6 74.9 %copy-start.21 = (s32[128,2]{0,1:T(2,128)S(1)}, s32[128,2]{0,1:T(2,128)}, u32[]{:S(2)}) copy-start(s32[128,2]{0,1:T(2,128)} %param.15) | copy-start | bytes 3076
  23.7 76.4 %copy-start.24 = (s32[16]{0:T(128)S(1)}, s32[16]{0:T(128)}, u32[]{:S(2)}) copy-start(s32[16]{0:T(128)} %param.17) | copy-start | bytes 196
  23.7 78.0 %copy-start.23 = (s32[64]{0:T(128)S(1)}, s32[64]{0:T(128)}, u32[]{:S(2)}) copy-start(s32[64]{0:T(128)} %param.19) | copy-start | bytes 772
  23.7 78.0 %copy-start.2 = (s32[64]{0:T(128)S(1)}, s32[64]{0:T(128)}, u32[]{:S(2)}) copy-start(s32[64]{0:T(128)} %param.18) | copy-start | bytes 772
  23.8 37.3 %collective-permute-start = (bf16[12288,128]{1,0:T(8,128)(2,1)S(1)}, bf16[12288,128]{1,0:T(8,128)(2,1)S(1)}, u32[]{:S(2)}, u32[]{:S(2)}) collective-permute-start(bf16[12288,128]{1,0:T(8,128)(2,1)S(1)} %constant_dynamic-update-slice_fusion), channel_id=1, source_target_pairs={{0,16},{1,17},{2,18},{3,19},{4,20},{5,21},{6,22},{7,23},{8,24},{9,... | collective-permute-start | bytes 9437192 | tf_op jit(solution)/shard_map/ppermute | solution.py:17
  61.1 37.4 %collective-permute-start.1 = (bf16[12288,128]{1,0:T(8,128)(2,1)S(1)}, bf16[12288,128]{1,0:T(8,128)(2,1)}, u32[]{:S(2)}, u32[]{:S(2)}) collective-permute-start(bf16[12288,128]{1,0:T(8,128)(2,1)S(1)} %collective-permute-done), channel_id=1, source_target_pairs={{0,16},{1,17},{2,18},{3,19},{4,20},{5,21},{6,22},{7,23},{8,24},{9,... | collective-permute-start | bytes 9437192 | tf_op jit(solution)/shard_map/ppermute | solution.py:17
  98.5 4.8 copy-start.22
  113.3 2.4 copy-start.20
  226.0 99.8 %all-to-all-start = ((bf16[64,24,2048]{2,1,0:T(8,128)(2,1)}), bf16[64,24,2048]{2,1,0:T(8,128)(2,1)}, u32[]{:S(2)}, u32[]{:S(2)}) async-start(bf16[64,24,2048]{2,1,0:T(8,128)(2,1)} %bitcast.99), calls=%async_computation | async-start | bytes 12582912 | tf_op jit(solution)/shard_map/all_to_all | solution.py:135
  246.3 2.7 copy-start.4
  246.3 2.7 copy-start.6
  249.3 1.0 copy-start.8
  325.8 6.4 %copy-start.9 = (bf16[256,2048]{1,0:T(8,128)(2,1)S(1)}, bf16[256,2048]{1,0:T(8,128)(2,1)}, u32[]{:S(2)}) copy-start(bf16[256,2048]{1,0:T(8,128)(2,1)} %copy-done.8) | copy-start | bytes 3145732
  332.1 4.6 copy-start.12
  336.7 93.3 %all-to-all-start.1 = ((bf16[64,24,2048]{2,1,0:T(8,128)(2,1)}), bf16[64,24,2048]{2,1,0:T(8,128)(2,1)}, u32[]{:S(2)}, u32[]{:S(2)}) async-start(bf16[64,24,2048]{2,1,0:T(8,128)(2,1)} %bitcast.98), calls=%async_computation.1 | async-start | bytes 12582912 | tf_op jit(solution)/shard_map/all_to_all | solution.py:160
  350.6 97.0 %all-reduce.3.cloned.1.call-start = ((), (), s32[]{:S(2)}) async-start(), calls=%async_computation.5 | async-start | bytes 8388608 | tf_op jit(solution)/shard_map/psum | solution.py:167
  430.0 99.6 %all-to-all-start.3 = ((bf16[64,24,2048]{2,1,0:T(8,128)(2,1)}), bf16[64,24,2048]{2,1,0:T(8,128)(2,1)}, u32[]{:S(2)}, u32[]{:S(2)}) async-start(bf16[64,24,2048]{2,1,0:T(8,128)(2,1)} %bitcast.97), calls=%async_computation.3 | async-start | bytes 12582912 | tf_op jit(solution)/shard_map/all_to_all | solution.py:163
  447.7 8.0 %copy-start.5 = (f32[1,256,2048]{2,1,0:T(8,128)S(1)}, f32[1,256,2048]{2,1,0:T(8,128)}, u32[]{:S(2)}) copy-start(f32[1,256,2048]{2,1,0:T(8,128)} %param.21) | copy-start | bytes 6291460
  447.7 8.0 %copy-start.7 = (bf16[256,2048]{1,0:T(8,128)(2,1)S(1)}, bf16[256,2048]{1,0:T(8,128)(2,1)}, u32[]{:S(2)}) copy-start(bf16[256,2048]{1,0:T(8,128)(2,1)} %reshape.365) | copy-start | bytes 3145732
  447.7 8.0 %copy-start.10 = (bf16[256,2048]{1,0:T(8,128)(2,1)S(1)}, bf16[256,2048]{1,0:T(8,128)(2,1)}, u32[]{:S(2)}) copy-start(bf16[256,2048]{1,0:T(8,128)(2,1)} %reshape.369) | copy-start | bytes 3145732
  447.7 8.0 %copy-start.11 = (bf16[256,2048]{1,0:T(8,128)(2,1)S(1)}, bf16[256,2048]{1,0:T(8,128)(2,1)}, u32[]{:S(2)}) copy-start(bf16[256,2048]{1,0:T(8,128)(2,1)} %reshape.368) | copy-start | bytes 3145732
  447.7 8.0 %copy-start.13 = (bf16[1,256,2048]{2,1,0:T(8,128)(2,1)S(1)}, bf16[1,256,2048]{2,1,0:T(8,128)(2,1)}, u32[]{:S(2)}) copy-start(bf16[1,256,2048]{2,1,0:T(8,128)(2,1)} %param.25) | copy-start | bytes 3145732
  447.7 8.0 %copy-start.14 = (bf16[1,256,2048]{2,1,0:T(8,128)(2,1)S(1)}, bf16[1,256,2048]{2,1,0:T(8,128)(2,1)}, u32[]{:S(2)}) copy-start(bf16[1,256,2048]{2,1,0:T(8,128)(2,1)} %param.24) | copy-start | bytes 3145732
  447.7 8.0 %copy-start.19 = (f32[256,2048]{1,0:T(8,128)S(1)}, f32[256,2048]{1,0:T(8,128)}, u32[]{:S(2)}) copy-start(f32[256,2048]{1,0:T(8,128)} %get-tuple-element.38) | copy-start | bytes 6291460
  529.6 4.6 copy-start.1
Sparse Core Ops, SparseCore 0:
  98.6 21.7 all-gather.2
  363.3 35.1 all-reduce.2

commit v5 on v3

--- a/solution.py
+++ b/solution.py
@@ -17,16 +17,17 @@
     return lax.ppermute(block, ("dp", "expert"), route)
 
 
-def migrate(blocks):
+def migrate(groups):
     ndp = lax.axis_size("dp")
     step = lax.axis_size("expert") // 4
     here = lax.axis_index("dp")
     halves = tuple(
-        lax.dynamic_slice_in_dim(b, here * (b.shape[0] // ndp), b.shape[0] // ndp, 0)
-        for b in blocks
-    )
-    moved = relay(relay(halves, step), step)
-    return tuple(lax.all_gather(m, "dp", axis=0, tiled=True) for m in moved)
+        lax.dynamic_slice_in_dim(g, here * (g.shape[1] // ndp), g.shape[1] // ndp, 1)
+        for g in groups
+    )
+    moved = relay(halves, step)
+    moved = relay(moved, step)
+    return tuple(lax.all_gather(m, "dp", axis=1, tiled=True) for m in moved)
 
 
 def gelu_tanh(value):
@@ -41,7 +42,7 @@
     return (updated, first_f.astype(jnp.bfloat16), second_f.astype(jnp.bfloat16))
 
 
-def local(
+def body(
     tokens,
     cotangent,
     routes,
@@ -102,16 +103,13 @@
     ).astype(jnp.bfloat16)
     weight_in, weight_out = (w_in[0], w_out[0])
     first_in, second_in, first_out, second_out = (m_in[0], v_in[0], m_out[0], v_out[0])
-    other = migrate(
+    group_in, group_out = migrate(
         (
-            weight_in.astype(jnp.bfloat16),
-            weight_out.astype(jnp.bfloat16),
-            first_in,
-            second_in,
-            first_out,
-            second_out,
+            jnp.stack([weight_in.astype(jnp.bfloat16), first_in, second_in]),
+            jnp.stack([weight_out.astype(jnp.bfloat16), first_out, second_out]),
         )
     )
+    other = (group_in[0], group_out[0], group_in[1], group_in[2], group_out[1], group_out[2])
     send_x, send_g, other = lax.optimization_barrier((send_x, send_g, other))
     other_w = (other[0].astype(weight_in.dtype), other[1].astype(weight_out.dtype))
     other_m = other[2:]
@@ -213,4 +211,4 @@
         P("expert", None, None),
         P("expert", None, None),
     )
-    return jax.shard_map(local, mesh=mesh, in_specs=in_specs, out_specs=out_specs, check_vma=False)
+    return jax.shard_map(body, mesh=mesh, in_specs=in_specs, out_specs=out_specs, check_vma=False)

time: 527 us -> 511 us (0.970); the launches traced: 518 us -> 509 us
  starting transfers between devices: 56.4 us -> 33.3 us
  waiting for transfers between devices: 260 us -> 274 us
  other arithmetic: 22.1 us -> 28.5 us
  local copies, waits for them, and re-layouts: 30.4 us -> 24.6 us
    ppermute x12 -> x4, waiting for transfers between devices: 46.3 us -> 67.3 us  [relay(): return lax.ppermute(block, ('dp', 'expert'), route)]
    ppermute x12 -> x4, starting transfers between devices: 25.9 us -> 5.35 us  [relay(): return lax.ppermute(block, ('dp', 'expert'), route)]
    all_gather x6 -> x2, waiting for transfers between devices: 7.73 us -> 0.01 us  [migrate(): return tuple((lax.all_gather(m, 'dp', axis=1, tiled=True) for m in moved))]
    squeeze x0 -> x2, local copies, waits for them, and re-layouts: none -> 7.48 us  [the longest x1 3.75 us: body(): group_in[2]]
    dynamic_slice x4 -> x0, local copies, waits for them, and re-layouts: 6.74 us -> none  [migrate(): lax.dynamic_slice_in_dim(b, here * (b.shape[0] // ndp), b.shape[0] // ndp...]
  transfers between devices with their start and end apart: 22 -> 10, of which waited for: 13 -> 7; matrix products, arithmetic and copies ran while one was open for 16% -> 15% of each run, Pallas kernels for 0% -> 0%
where the time goes in v5:
time: 511 us; the launch traced here: 509 us
  waiting for transfers between devices  274 us (54%)
  blocking collectives  82.4 us (16%)
  matrix products  51.5 us (10%)
  starting transfers between devices  33.3 us (7%)
  other arithmetic  28.5 us (6%)
  local copies, waits for them, and re-layouts  24.6 us (5%)
  between operations  14.9 us (3%)
    all_to_all x1, blocking collectives, body(): lax.all_to_all(send_g, 'expert', split_axis=0, concat_axis=0, tiled=True)  82.4 us
    all_to_all x1, waiting for transfers between devices, body(): lax.all_to_all(send_x, 'expert', split_axis=0, concat_axis=0, tiled=True)  76.2 us
    ppermute x4, waiting for transfers between devices, relay(): return lax.ppermute(block, ('dp', 'expert'), route)  67.3 us
    all_to_all x1, waiting for transfers between devices, body(): lax.all_to_all(part.reshape(nexp, slots, width), 'expert', split_axis=0,...  66.4 us
    all_to_all x1, waiting for transfers between devices, body(): lax.all_to_all(xpart.reshape(nexp, slots, width), 'expert', split_axis=0,...  63.9 us
  transfers between devices with their start and end apart: 10, of which 7 were waited for; matrix products, arithmetic and copies ran while one was open for 15% of the time, Pallas kernels for 0%

profile of v5, /device:TPU:50, one launch (start us, length us, event | category | flops | bytes accessed | tf_op | source)
XLA Modules:
  0.0 509.0 jit_solution(2968584671928843550)
XLA Ops:
  7.2 2.8 convert_element_type.85
  10.0 1.6 fusion.11
  11.6 1.4 collective-permute-start.2
  13.0 19.2 %collective-permute-done.2 = bf16[3,128,2048]{2,1,0:T(8,128)(2,1)} collective-permute-done((bf16[3,128,2048]{2,1,0:T(8,128)(2,1)S(1)}, bf16[3,128,2048]{2,1,0:T(8,128)(2,1)}, u32[]{:S(2)}, u32[]{:S(2)}) %collective-permute-start.2) | collective-permute-done | bytes 1572896 | tf_op jit(solution)/shard_map/ppermute | solution.py:17
  32.2 1.3 collective-permute-start.3
  33.5 1.1 convert_element_type.84
  34.6 2.6 fusion.13
  37.2 1.4 collective-permute-start
  38.6 14.3 %collective-permute-done.3 = bf16[3,128,2048]{2,1,0:T(8,128)(2,1)} collective-permute-done((bf16[3,128,2048]{2,1,0:T(8,128)(2,1)}, bf16[3,128,2048]{2,1,0:T(8,128)(2,1)}, u32[]{:S(2)}, u32[]{:S(2)}) %collective-permute-start.3) | collective-permute-done | bytes 1572896 | tf_op jit(solution)/shard_map/ppermute | solution.py:17
  53.0 16.8 %collective-permute-done = bf16[3,1024,256]{2,1,0:T(8,128)(2,1)} collective-permute-done((bf16[3,1024,256]{2,1,0:T(8,128)(2,1)}, bf16[3,1024,256]{2,1,0:T(8,128)(2,1)}, u32[]{:S(2)}, u32[]{:S(2)}) %collective-permute-start) | collective-permute-done | bytes 1572896 | tf_op jit(solution)/shard_map/ppermute | solution.py:17
  69.8 1.3 collective-permute-start.1
  71.2 0.1 eq.85
  71.3 0.1 eq.81
  71.7 0.6 reduce-window.6
  72.3 0.2 slice_reduce_fusion
  72.6 0.8 gather_fusion
  73.5 17.0 %collective-permute-done.1 = bf16[3,1024,256]{2,1,0:T(8,128)(2,1)} collective-permute-done((bf16[3,1024,256]{2,1,0:T(8,128)(2,1)}, bf16[3,1024,256]{2,1,0:T(8,128)(2,1)}, u32[]{:S(2)}, u32[]{:S(2)}) %collective-permute-start.1) | collective-permute-done | bytes 1572896 | tf_op jit(solution)/shard_map/ppermute | solution.py:17
  90.6 1.4 scatter_custom_fusion
  92.1 0.6 gather_fusion.1
  93.1 9.5 %gather_fusion.2 = f32[1536]{0:T(1024)S(1)} fusion(f32[257]{0:T(512)S(1)} %pad_maximum_fusion, s32[2048]{0:T(1024)S(1)} %pad_clamp_fusion), kind=kCustom, calls=%fused_computation.2 | custom fusion | bytes 18432 | tf_op jit(solution)/shard_map/jit(_take)/gather | solution.py:98
  102.9 2.4 convolution_convert_fusion.2
  105.3 4.0 convolution_convert_fusion.3
  109.3 3.7 fusion
  113.0 3.7 slice_bitcast_fusion
  116.8 3.7 slice_bitcast_fusion.2
  120.5 1.1 copy-done.3
  121.6 82.4 %all_to_all.20 = bf16[64,24,2048]{2,1,0:T(8,128)(2,1)} all-to-all(bf16[64,24,2048]{2,1,0:T(8,128)(2,1)S(1)} %copy-done.3), channel_id=1, replica_groups=mesh['dp'=2,'expert'=64] {'expert'}, dimensions={0} | all-to-all | bytes 12582912 | tf_op jit(solution)/shard_map/all_to_all | solution.py:124
  204.1 8.6 %all-to-all-start = ((bf16[64,24,2048]{2,1,0:T(8,128)(2,1)}), bf16[64,24,2048]{2,1,0:T(8,128)(2,1)}, u32[]{:S(2)}, u32[]{:S(2)}) async-start(bf16[64,24,2048]{2,1,0:T(8,128)(2,1)} %bitcast.116), calls=%async_computation | async-start | bytes 12582912 | tf_op jit(solution)/shard_map/all_to_all | solution.py:123
  212.7 0.6 dynamic-slice.2
  214.0 2.6 fusion.15
  216.6 0.3 fusion.16
  216.9 1.0 copy-done.9
  217.8 5.8 %fusion.42 = f32[1536,256]{1,0:T(8,128)} fusion(bf16[1536,2048]{1,0:T(8,128)(2,1)} %bitcast.118, bf16[256,2048]{1,0:T(8,128)(2,1)S(1)} %fusion.16), kind=kOutput, calls=%fused_computation.113 | convolution fusion | flops 1610612736 | bytes 8912896 | tf_op jit(solution)/shard_map/dot_general | solution.py:134
  223.6 76.2 %all-to-all-done = bf16[64,24,2048]{2,1,0:T(8,128)(2,1)} async-done(((bf16[64,24,2048]{2,1,0:T(8,128)(2,1)}), bf16[64,24,2048]{2,1,0:T(8,128)(2,1)}, u32[]{:S(2)}, u32[]{:S(2)}) %all-to-all-start) | async-done | bytes 6291488 | tf_op jit(solution)/shard_map/all_to_all | solution.py:123
  299.8 6.3 %fusion.9 = (bf16[1536,256]{1,0:T(8,128)(2,1)S(1)}, f32[1536,256]{1,0:T(8,128)S(1)}) fusion(f32[1536,256]{1,0:T(8,128)} %fusion.42, bf16[1536,2048]{1,0:T(8,128)(2,1)} %bitcast.13, bf16[2048,256]{1,0:T(8,128)(2,1)} %fusion.15), kind=kOutput, calls=%fused_computation.36 | convolution fusion | flops 1618477056 | bytes 11272192 | tf_op jit(solution)/shard_map/dot_general | solution.py:130
  306.2 4.5 convolution_convert_fusion.1
  310.7 9.7 %all-to-all-start.1 = ((bf16[64,24,2048]{2,1,0:T(8,128)(2,1)}), bf16[64,24,2048]{2,1,0:T(8,128)(2,1)}, u32[]{:S(2)}, u32[]{:S(2)}) async-start(bf16[64,24,2048]{2,1,0:T(8,128)(2,1)} %bitcast.115), calls=%async_computation.1 | async-start | bytes 12582912 | tf_op jit(solution)/shard_map/all_to_all | solution.py:148
  320.5 6.5 %fusion.41 = f32[256,2048]{1,0:T(8,128)} fusion(bf16[1536,2048]{1,0:T(8,128)(2,1)} %bitcast.119, f32[1536,256]{1,0:T(8,128)} %copy-done.15), kind=kOutput, calls=%fused_computation.112 | convolution fusion | flops 1614151680 | bytes 9961472 | tf_op jit(solution)/shard_map/dot_general | solution.py:144
  327.0 6.0 %fusion.43 = f32[2048,256]{1,0:T(8,128)} fusion(bf16[1536,2048]{1,0:T(8,128)(2,1)} %bitcast.13, bf16[1536,256]{1,0:T(8,128)(2,1)S(1)} %get-tuple-element.55), kind=kOutput, calls=%fused_computation.114 | convolution fusion | flops 1610612736 | bytes 9175040 | tf_op jit(solution)/shard_map/dot_general | solution.py:141
  333.0 5.7 %convolution_convert_fusion = bf16[1536,2048]{1,0:T(8,128)(2,1)} fusion(bf16[1536,256]{1,0:T(8,128)(2,1)S(1)} %get-tuple-element.55, bf16[2048,256]{1,0:T(8,128)(2,1)} %fusion.15), kind=kOutput, calls=%fused_computation.6 | convolution fusion | flops 1613758464 | bytes 8126464 | tf_op jit(solution)/shard_map/dot_general | solution.py:138
  338.7 66.4 %all-to-all-done.1 = bf16[64,24,2048]{2,1,0:T(8,128)(2,1)} async-done(((bf16[64,24,2048]{2,1,0:T(8,128)(2,1)}), bf16[64,24,2048]{2,1,0:T(8,128)(2,1)}, u32[]{:S(2)}, u32[]{:S(2)}) %all-to-all-start.1) | async-done | bytes 6291488 | tf_op jit(solution)/shard_map/all_to_all | solution.py:148
  405.1 9.5 %all-to-all-start.3 = ((bf16[64,24,2048]{2,1,0:T(8,128)(2,1)}), bf16[64,24,2048]{2,1,0:T(8,128)(2,1)}, u32[]{:S(2)}, u32[]{:S(2)}) async-start(bf16[64,24,2048]{2,1,0:T(8,128)(2,1)} %bitcast.114), calls=%async_computation.3 | async-start | bytes 12582912 | tf_op jit(solution)/shard_map/all_to_all | solution.py:151
  415.3 0.5 fusion.25
  415.9 7.9 %fusion.21 = (bf16[1,2048,256]{2,1,0:T(8,128)(2,1)}, f32[1,2048,256]{2,1,0:T(8,128)}, bf16[1,2048,256]{2,1,0:T(8,128)(2,1)}) fusion(f32[2048,256]{1,0:T(8,128)} %get-tuple-element.37, bf16[2048,256]{1,0:T(8,128)(2,1)} %get-tuple-element.21, bf16[1,2048,256]{2,1,0:T(8,128)(2,1)} %param.23, pred[]{:T(512)S(6)} %ne.53, bf16[2048,256]{1,0:T(8,128)(2,1)} %get-tuple-element.20, ...), kind=kLoop, calls=%fused_computation.50 | loop fusion | flops 12058624 | bytes 13631489 | tf_op jit(solution)/shard_map/broadcast_in_dim | solution.py:182
  423.8 4.4 fusion.22
  428.3 5.7 %fusion.14 = bf16[128,2048]{1,0:T(8,128)(2,1)} fusion(bf16[1536,2048,1]{1,0,2:T(8,128)(2,1)} %bitcast.20, f32[128,2]{0,1:T(2,128)S(1)} %copy-done.19, s32[1536]{0:T(1024)S(1)} %eq.94, s32[128,2]{0,1:T(2,128)S(1)} %copy.25, s32[1536]{0:T(1024)S(1)} %eq.90, s32[128,2]{0,1:T(2,128)S(1)} %copy-done.18, pred[128,2]{0,1:T(4,128)(4,1)S(1)} %copy.24), kind=kOutput, calls=%fused_computation.43 | convolution fusion | flops 1612972032 | bytes 6831360 | tf_op jit(solution)/shard_map/dot_general | solution.py:167
  433.9 63.9 %all-to-all-done.3 = bf16[64,24,2048]{2,1,0:T(8,128)(2,1)} async-done(((bf16[64,24,2048]{2,1,0:T(8,128)(2,1)}), bf16[64,24,2048]{2,1,0:T(8,128)(2,1)}, u32[]{:S(2)}, u32[]{:S(2)}) %all-to-all-start.3) | async-done | bytes 6291488 | tf_op jit(solution)/shard_map/all_to_all | solution.py:151
  497.8 4.6 convolution_convert_fusion.4
  (86 shorter events, 2.3 us)
Async XLA Ops:
  7.2 95.7 %copy-start = (bf16[128,2048]{1,0:T(8,128)(2,1)S(1)}, bf16[128,2048]{1,0:T(8,128)(2,1)}, u32[]{:S(2)}) copy-start(bf16[128,2048]{1,0:T(8,128)(2,1)} %param.14) | copy-start | bytes 1572868
  7.2 105.9 %all-gather.5.cloned.1.call-start = ((), (), s32[]{:S(2)}) async-start(), calls=%async_computation.5 | async-start | bytes 4718592 | tf_op jit(solution)/shard_map/all_gather | solution.py:30
  10.0 23.5 %copy-start.4 = (f32[1,2048,256]{2,1,0:T(8,128)S(1)}, f32[1,2048,256]{2,1,0:T(8,128)}, u32[]{:S(2)}) copy-start(f32[1,2048,256]{2,1,0:T(8,128)} %param.20) | copy-start | bytes 6291460
  11.6 20.6 %collective-permute-start.2 = (bf16[3,128,2048]{2,1,0:T(8,128)(2,1)S(1)}, bf16[3,128,2048]{2,1,0:T(8,128)(2,1)}, u32[]{:S(2)}, u32[]{:S(2)}) collective-permute-start(bf16[3,128,2048]{2,1,0:T(8,128)(2,1)S(1)} %fusion.11), channel_id=1, source_target_pairs={{0,16},{1,17},{2,18},{3,19},{4,20},{5,21},{6,22},{7,23},{8,24},{9,... | collective-permute-start | bytes 4718600 | tf_op jit(solution)/shard_map/ppermute | solution.py:17
  32.2 20.7 %collective-permute-start.3 = (bf16[3,128,2048]{2,1,0:T(8,128)(2,1)}, bf16[3,128,2048]{2,1,0:T(8,128)(2,1)}, u32[]{:S(2)}, u32[]{:S(2)}) collective-permute-start(bf16[3,128,2048]{2,1,0:T(8,128)(2,1)} %collective-permute-done.2), channel_id=1, source_target_pairs={{0,16},{1,17},{2,18},{3,19},{4,20},{5,21},{6,22},{7,23},{8,24},{9,... | collective-permute-start | bytes 4718600 | tf_op jit(solution)/shard_map/ppermute | solution.py:17
  34.6 36.5 %copy-start.18 = (s32[128,2]{0,1:T(2,128)S(1)}, s32[128,2]{0,1:T(2,128)}, u32[]{:S(2)}) copy-start(s32[128,2]{0,1:T(2,128)} %param.15) | copy-start | bytes 3076
  34.6 38.0 %copy-start.20 = (s32[64]{0:T(128)S(1)}, s32[64]{0:T(128)}, u32[]{:S(2)}) copy-start(s32[64]{0:T(128)} %param.19) | copy-start | bytes 772
  37.2 35.4 %copy-start.2 = (s32[64]{0:T(128)S(1)}, s32[64]{0:T(128)}, u32[]{:S(2)}) copy-start(s32[64]{0:T(128)} %param.18) | copy-start | bytes 772
  37.2 36.2 %copy-start.21 = (s32[16]{0:T(128)S(1)}, s32[16]{0:T(128)}, u32[]{:S(2)}) copy-start(s32[16]{0:T(128)} %param.17) | copy-start | bytes 196
  37.2 32.6 %collective-permute-start = (bf16[3,1024,256]{2,1,0:T(8,128)(2,1)}, bf16[3,1024,256]{2,1,0:T(8,128)(2,1)}, u32[]{:S(2)}, u32[]{:S(2)}) collective-permute-start(bf16[3,1024,256]{2,1,0:T(8,128)(2,1)} %fusion.13), channel_id=1, source_target_pairs={{0,16},{1,17},{2,18},{3,19},{4,20},{5,21},{6,22},{7,23},{8,24},{9,... | collective-permute-start | bytes 4718600 | tf_op jit(solution)/shard_map/ppermute | solution.py:17
  52.9 39.9 %copy-start.19 = (f32[128,2]{0,1:T(2,128)S(1)}, f32[128,2]{0,1:T(2,128)}, u32[]{:S(2)}) copy-start(f32[128,2]{0,1:T(2,128)} %param.16) | copy-start | bytes 3076
  53.0 63.8 %all-gather.3.cloned.1.call-start = ((), (), s32[]{:S(2)}) async-start(), calls=%async_computation.4 | async-start | bytes 4718592 | tf_op jit(solution)/shard_map/all_gather | solution.py:30
  69.8 20.7 %collective-permute-start.1 = (bf16[3,1024,256]{2,1,0:T(8,128)(2,1)}, bf16[3,1024,256]{2,1,0:T(8,128)(2,1)}, u32[]{:S(2)}, u32[]{:S(2)}) collective-permute-start(bf16[3,1024,256]{2,1,0:T(8,128)(2,1)} %collective-permute-done), channel_id=1, source_target_pairs={{0,16},{1,17},{2,18},{3,19},{4,20},{5,21},{6,22},{7,23},{8,24},{9,... | collective-permute-start | bytes 4718600 | tf_op jit(solution)/shard_map/ppermute | solution.py:17
  102.9 2.4 copy-start.17
  116.8 4.9 copy-start.3
  204.1 95.7 %all-to-all-start = ((bf16[64,24,2048]{2,1,0:T(8,128)(2,1)}), bf16[64,24,2048]{2,1,0:T(8,128)(2,1)}, u32[]{:S(2)}, u32[]{:S(2)}) async-start(bf16[64,24,2048]{2,1,0:T(8,128)(2,1)} %bitcast.116), calls=%async_computation | async-start | bytes 12582912 | tf_op jit(solution)/shard_map/all_to_all | solution.py:123
  213.9 2.6 copy-start.5
  213.9 2.6 copy-start.7
  216.9 1.0 copy-start.9
  299.8 6.3 %copy-start.10 = (bf16[256,2048]{1,0:T(8,128)(2,1)S(1)}, bf16[256,2048]{1,0:T(8,128)(2,1)}, u32[]{:S(2)}) copy-start(bf16[256,2048]{1,0:T(8,128)(2,1)} %copy-done.9) | copy-start | bytes 3145732
  306.2 4.6 copy-start.15
  310.7 94.4 %all-to-all-start.1 = ((bf16[64,24,2048]{2,1,0:T(8,128)(2,1)}), bf16[64,24,2048]{2,1,0:T(8,128)(2,1)}, u32[]{:S(2)}, u32[]{:S(2)}) async-start(bf16[64,24,2048]{2,1,0:T(8,128)(2,1)} %bitcast.115), calls=%async_computation.1 | async-start | bytes 12582912 | tf_op jit(solution)/shard_map/all_to_all | solution.py:148
  320.5 95.3 %all-reduce.3.cloned.1.call-start = ((), (), s32[]{:S(2)}) async-start(), calls=%async_computation.6 | async-start | bytes 8388608 | tf_op jit(solution)/shard_map/psum | solution.py:155
  405.1 92.8 %all-to-all-start.3 = ((bf16[64,24,2048]{2,1,0:T(8,128)(2,1)}), bf16[64,24,2048]{2,1,0:T(8,128)(2,1)}, u32[]{:S(2)}, u32[]{:S(2)}) async-start(bf16[64,24,2048]{2,1,0:T(8,128)(2,1)} %bitcast.114), calls=%async_computation.3 | async-start | bytes 12582912 | tf_op jit(solution)/shard_map/all_to_all | solution.py:151
  415.8 8.0 %copy-start.6 = (f32[1,256,2048]{2,1,0:T(8,128)S(1)}, f32[1,256,2048]{2,1,0:T(8,128)}, u32[]{:S(2)}) copy-start(f32[1,256,2048]{2,1,0:T(8,128)} %param.21) | copy-start | bytes 6291460
  415.8 8.0 %copy-start.8 = (bf16[256,2048]{1,0:T(8,128)(2,1)S(1)}, bf16[256,2048]{1,0:T(8,128)(2,1)}, u32[]{:S(2)}) copy-start(bf16[256,2048]{1,0:T(8,128)(2,1)} %get-tuple-element.18) | copy-start | bytes 3145732
  415.8 8.0 %copy-start.11 = (bf16[1,256,2048]{2,1,0:T(8,128)(2,1)S(1)}, bf16[1,256,2048]{2,1,0:T(8,128)(2,1)}, u32[]{:S(2)}) copy-start(bf16[1,256,2048]{2,1,0:T(8,128)(2,1)} %param.24) | copy-start | bytes 3145732
  415.8 8.0 %copy-start.12 = (bf16[1,256,2048]{2,1,0:T(8,128)(2,1)S(1)}, bf16[1,256,2048]{2,1,0:T(8,128)(2,1)}, u32[]{:S(2)}) copy-start(bf16[1,256,2048]{2,1,0:T(8,128)(2,1)} %param.25) | copy-start | bytes 3145732
  415.9 8.0 %copy-start.13 = (bf16[256,2048]{1,0:T(8,128)(2,1)S(1)}, bf16[256,2048]{1,0:T(8,128)(2,1)}, u32[]{:S(2)}) copy-start(bf16[256,2048]{1,0:T(8,128)(2,1)} %get-tuple-element.23) | copy-start | bytes 3145732
  415.9 8.0 %copy-start.14 = (bf16[256,2048]{1,0:T(8,128)(2,1)S(1)}, bf16[256,2048]{1,0:T(8,128)(2,1)}, u32[]{:S(2)}) copy-start(bf16[256,2048]{1,0:T(8,128)(2,1)} %get-tuple-element.22) | copy-start | bytes 3145732
  415.9 8.0 %copy-start.16 = (f32[256,2048]{1,0:T(8,128)S(1)}, f32[256,2048]{1,0:T(8,128)}, u32[]{:S(2)}) copy-start(f32[256,2048]{1,0:T(8,128)} %get-tuple-element.38) | copy-start | bytes 6291460
  497.8 4.6 copy-start.1
Sparse Core Ops, SparseCore 0:
  53.1 16.6 all-gather.4
  90.7 17.6 all-gather.2
  333.1 35.2 all-reduce.2

commit v6 on v5

--- a/solution.py
+++ b/solution.py
@@ -27,6 +27,10 @@
     )
     moved = relay(halves, step)
     moved = relay(moved, step)
+    return moved
+
+
+def join(moved):
     return tuple(lax.all_gather(m, "dp", axis=1, tiled=True) for m in moved)
 
 
@@ -103,14 +107,15 @@
     ).astype(jnp.bfloat16)
     weight_in, weight_out = (w_in[0], w_out[0])
     first_in, second_in, first_out, second_out = (m_in[0], v_in[0], m_out[0], v_out[0])
-    group_in, group_out = migrate(
+    halves = migrate(
         (
             jnp.stack([weight_in.astype(jnp.bfloat16), first_in, second_in]),
             jnp.stack([weight_out.astype(jnp.bfloat16), first_out, second_out]),
         )
     )
+    send_x, send_g, halves = lax.optimization_barrier((send_x, send_g, halves))
+    group_in, group_out = join(halves)
     other = (group_in[0], group_out[0], group_in[1], group_in[2], group_out[1], group_out[2])
-    send_x, send_g, other = lax.optimization_barrier((send_x, send_g, other))
     other_w = (other[0].astype(weight_in.dtype), other[1].astype(weight_out.dtype))
     other_m = other[2:]
     weight_in = jnp.where(moved, other_w[0], weight_in)

time: 511 us -> 473 us (0.926)
  blocking collectives: 82.4 us -> 0 us
  waiting for transfers between devices: 274 us -> 318 us
  starting transfers between devices: 33.3 us -> 44.3 us
  local copies, waits for them, and re-layouts: 24.6 us -> 15.9 us
    all_to_all x1 -> x0, blocking collectives: 82.4 us -> none  [body(): lax.all_to_all(send_g, 'expert', split_axis=0, concat_axis=0, tiled=True)]
    all_to_all x0 -> x1, waiting for transfers between devices: none -> 61.1 us  [body(): lax.all_to_all(send_g, 'expert', split_axis=0, concat_axis=0, tiled=True)]
    ppermute x4, waiting for transfers between devices: 67.3 us -> 38.5 us  [relay(): return lax.ppermute(block, ('dp', 'expert'), route)]
    all_gather x2, waiting for transfers between devices: 0.01 us -> 10.5 us  [join(): return tuple((lax.all_gather(m, 'dp', axis=1, tiled=True) for m in moved))]
    all_to_all x0 -> x1, starting transfers between devices: none -> 8.67 us  [body(): lax.all_to_all(send_g, 'expert', split_axis=0, concat_axis=0, tiled=True)]
    squeeze x2 -> x0, local copies, waits for them, and re-layouts: 7.48 us -> none  [the longest x1 3.75 us: body(): group_in[2]]
    all_to_all x1, waiting for transfers between devices: 66.4 us -> 59.1 us  [body(): lax.all_to_all(part.reshape(nexp, slots, width), 'expert', split_axis=0,...]
    all_to_all x1, waiting for transfers between devices: 76.2 us -> 82.6 us  [body(): lax.all_to_all(send_x, 'expert', split_axis=0, concat_axis=0, tiled=True)]
  transfers between devices with their start and end apart: 10 -> 11, of which waited for: 7 -> 9; matrix products, arithmetic and copies ran while one was open for 15% -> 17% of each run, Pallas kernels for 0% -> 0%
where the time goes in v6:
time: 473 us; the launch traced here: 470 us
  waiting for transfers between devices  318 us (67%)
  matrix products  53.1 us (11%)
  starting transfers between devices  44.3 us (9%)
  other arithmetic  24.2 us (5%)
  local copies, waits for them, and re-layouts  15.9 us (3%)
  between operations  14.8 us (3%)
    all_to_all x1, waiting for transfers between devices, body(): lax.all_to_all(send_x, 'expert', split_axis=0, concat_axis=0, tiled=True)  82.6 us
    all_to_all x1, waiting for transfers between devices, body(): lax.all_to_all(xpart.reshape(nexp, slots, width), 'expert', split_axis=0,...  64.6 us
    all_to_all x1, waiting for transfers between devices, body(): lax.all_to_all(send_g, 'expert', split_axis=0, concat_axis=0, tiled=True)  61.1 us
    all_to_all x1, waiting for transfers between devices, body(): lax.all_to_all(part.reshape(nexp, slots, width), 'expert', split_axis=0,...  59.1 us
    ppermute x4, waiting for transfers between devices, relay(): return lax.ppermute(block, ('dp', 'expert'), route)  38.5 us
    all_to_all x1, starting transfers between devices, body(): lax.all_to_all(send_x, 'expert', split_axis=0, concat_axis=0, tiled=True)  11.1 us
    all_to_all x1, starting transfers between devices, body(): lax.all_to_all(xpart.reshape(nexp, slots, width), 'expert', split_axis=0,...  10.6 us
    all_gather x2, waiting for transfers between devices, join(): return tuple((lax.all_gather(m, 'dp', axis=1, tiled=True) for m in moved))  10.5 us
  transfers between devices with their start and end apart: 11, of which 9 were waited for; matrix products, arithmetic and copies ran while one was open for 17% of the time, Pallas kernels for 0%

profile of v6, /device:TPU:50, one launch (start us, length us, event | category | flops | bytes accessed | tf_op | source)
XLA Modules:
  0.0 470.0 jit_solution(12128064441500666083)
XLA Ops:
  7.2 2.8 convert_element_type.103
  10.0 2.8 fusion.17
  12.8 1.3 collective-permute-start.2
  14.1 1.1 convert_element_type.102
  15.2 2.7 fusion.19
  17.8 0.2 collective-permute-start
  18.3 0.1 eq.81
  18.6 0.1 mul.176
  18.7 0.6 reduce-window.6
  19.3 0.2 slice_reduce_fusion
  19.7 1.4 scatter_custom_fusion
  21.2 0.8 gather_fusion
  22.0 0.6 gather_fusion.1
  23.1 9.5 %gather_fusion.2 = f32[1536]{0:T(1024)S(1)} fusion(f32[257]{0:T(512)S(1)} %pad_maximum_fusion, s32[2048]{0:T(1024)S(1)} %pad_clamp_fusion), kind=kCustom, calls=%fused_computation.2 | custom fusion | bytes 18432 | tf_op jit(solution)/shard_map/jit(_take)/gather | solution.py:102
  32.8 0.7 collective-permute-done.2
  33.5 1.3 collective-permute-start.3
  34.8 15.6 %collective-permute-done = bf16[3,1024,256]{2,1,0:T(8,128)(2,1)} collective-permute-done((bf16[3,1024,256]{2,1,0:T(8,128)(2,1)}, bf16[3,1024,256]{2,1,0:T(8,128)(2,1)}, u32[]{:S(2)}, u32[]{:S(2)}) %collective-permute-start) | collective-permute-done | bytes 1572896 | tf_op jit(solution)/shard_map/ppermute | solution.py:17
  50.4 1.3 collective-permute-start.1
  51.7 2.4 convolution_convert_fusion.2
  54.1 4.0 convolution_convert_fusion.3
  58.1 3.8 fusion
  61.8 5.4 %collective-permute-done.3 = bf16[3,128,2048]{2,1,0:T(8,128)(2,1)} collective-permute-done((bf16[3,128,2048]{2,1,0:T(8,128)(2,1)}, bf16[3,128,2048]{2,1,0:T(8,128)(2,1)}, u32[]{:S(2)}, u32[]{:S(2)}) %collective-permute-start.3) | collective-permute-done | bytes 1572896 | tf_op jit(solution)/shard_map/ppermute | solution.py:17
  67.2 16.9 %collective-permute-done.1 = bf16[3,1024,256]{2,1,0:T(8,128)(2,1)} collective-permute-done((bf16[3,1024,256]{2,1,0:T(8,128)(2,1)}, bf16[3,1024,256]{2,1,0:T(8,128)(2,1)}, u32[]{:S(2)}, u32[]{:S(2)}) %collective-permute-start.1) | collective-permute-done | bytes 1572896 | tf_op jit(solution)/shard_map/ppermute | solution.py:17
  84.1 11.1 %all-to-all-start = ((bf16[64,24,2048]{2,1,0:T(8,128)(2,1)}), bf16[64,24,2048]{2,1,0:T(8,128)(2,1)}, u32[]{:S(2)}, u32[]{:S(2)}) async-start(bf16[64,24,2048]{2,1,0:T(8,128)(2,1)} %bitcast.130), calls=%async_computation | async-start | bytes 12582912 | tf_op jit(solution)/shard_map/all_to_all | solution.py:128
  95.2 0.7 all-gather.3.cloned.1.call-update
  95.9 82.6 %all-to-all-done = bf16[64,24,2048]{2,1,0:T(8,128)(2,1)} async-done(((bf16[64,24,2048]{2,1,0:T(8,128)(2,1)}), bf16[64,24,2048]{2,1,0:T(8,128)(2,1)}, u32[]{:S(2)}, u32[]{:S(2)}) %all-to-all-start) | async-done | bytes 6291488 | tf_op jit(solution)/shard_map/all_to_all | solution.py:128
  178.6 8.7 %all-to-all-start.2 = ((bf16[64,24,2048]{2,1,0:T(8,128)(2,1)}), bf16[64,24,2048]{2,1,0:T(8,128)(2,1)}, u32[]{:S(2)}, u32[]{:S(2)}) async-start(bf16[64,24,2048]{2,1,0:T(8,128)(2,1)} %fusion), calls=%async_computation.2 | async-start | bytes 12582912 | tf_op jit(solution)/shard_map/all_to_all | solution.py:129
  187.3 0.2 all-gather.5.cloned.1.call-start
  187.5 0.5 all-gather.5.cloned.1.call-update
  188.0 0.6 dynamic-slice.2
  189.3 6.0 %fusion.33 = f32[1536,256]{1,0:T(8,128)} fusion(bf16[1536,2048]{1,0:T(8,128)(2,1)} %bitcast.7, f32[1,2048,256]{2,1,0:T(8,128)S(1)} %copy-done.3, bf16[3,2048,256]{2,1,0:T(8,128)(2,1)} %all-gather.3.cloned.1.call-done, pred[]{:T(512)S(6)} %ne.53), kind=kOutput, calls=%fused_computation.68 | convolution fusion | flops 1611661312 | bytes 11010049 | tf_op jit(solution)/shard_map/dot_general | solution.py:135
  195.3 10.5 %all-gather.5.cloned.1.call-done = bf16[3,256,2048]{2,1,0:T(8,128)(2,1)} async-done(((bf16[3,128,2048]{2,1,0:T(8,128)(2,1)}), bf16[3,256,2048]{2,1,0:T(8,128)(2,1)}) %all-gather.5.cloned.1.call-update) | async-done | bytes 3145744 | tf_op jit(solution)/shard_map/all_gather | solution.py:34
  205.9 6.3 %convolution_convert_fusion.1 = bf16[1536,2048]{1,0:T(8,128)(2,1)} fusion(f32[1,256,2048]{2,1,0:T(8,128)} %param.21, bf16[3,256,2048]{2,1,0:T(8,128)(2,1)} %all-gather.5.cloned.1.call-done, pred[]{:T(512)S(6)} %ne.53, f32[1536,256]{1,0:T(8,128)} %fusion.33), kind=kOutput, calls=%fused_computation.7 | convolution fusion | flops 1618345984 | bytes 11010049 | tf_op jit(solution)/shard_map/dot_general | solution.py:138
  212.2 61.1 %all-to-all-done.2 = bf16[64,24,2048]{2,1,0:T(8,128)(2,1)} async-done(((bf16[64,24,2048]{2,1,0:T(8,128)(2,1)}), bf16[64,24,2048]{2,1,0:T(8,128)(2,1)}, u32[]{:S(2)}, u32[]{:S(2)}) %all-to-all-start.2) | async-done | bytes 6291488 | tf_op jit(solution)/shard_map/all_to_all | solution.py:129
  273.3 9.5 %all-to-all-start.1 = ((bf16[64,24,2048]{2,1,0:T(8,128)(2,1)}), bf16[64,24,2048]{2,1,0:T(8,128)(2,1)}, u32[]{:S(2)}, u32[]{:S(2)}) async-start(bf16[64,24,2048]{2,1,0:T(8,128)(2,1)} %bitcast.129), calls=%async_computation.1 | async-start | bytes 12582912 | tf_op jit(solution)/shard_map/all_to_all | solution.py:153
  282.9 6.6 %fusion.53 = f32[256,2048]{1,0:T(8,128)} fusion(bf16[1536,2048]{1,0:T(8,128)(2,1)} %bitcast.15, f32[1536,256]{1,0:T(8,128)} %fusion.33), kind=kOutput, calls=%fused_computation.120 | convolution fusion | flops 1614151680 | bytes 9961472 | tf_op jit(solution)/shard_map/dot_general | solution.py:149
  289.5 5.7 %fusion.15 = bf16[1536,256]{1,0:T(8,128)(2,1)S(1)} fusion(f32[1536,256]{1,0:T(8,128)S(1)} %copy-done.9, bf16[1536,2048]{1,0:T(8,128)(2,1)} %bitcast.15, f32[1,256,2048]{2,1,0:T(8,128)S(1)} %copy-done.4, bf16[3,256,2048]{2,1,0:T(8,128)(2,1)} %all-gather.5.cloned.1.call-done, pred[]{:T(512)S(6)} %ne.53), kind=kOutput, calls=%fused_computation.46 | convolution fusion | flops 1619525632 | bytes 11796481 | tf_op jit(solution)/shard_map/dot_general | solution.py:139
  295.2 6.0 %fusion.54 = f32[2048,256]{1,0:T(8,128)} fusion(bf16[1536,2048]{1,0:T(8,128)(2,1)} %bitcast.7, bf16[1536,256]{1,0:T(8,128)(2,1)S(1)} %fusion.15), kind=kOutput, calls=%fused_computation.121 | convolution fusion | flops 1610612736 | bytes 9175040 | tf_op jit(solution)/shard_map/dot_general | solution.py:146
  301.3 5.7 %convolution_convert_fusion = bf16[1536,2048]{1,0:T(8,128)(2,1)} fusion(bf16[1536,256]{1,0:T(8,128)(2,1)S(1)} %fusion.15, f32[1,2048,256]{2,1,0:T(8,128)S(1)} %copy-done.3, bf16[3,2048,256]{2,1,0:T(8,128)(2,1)} %all-gather.3.cloned.1.call-done, pred[]{:T(512)S(6)} %ne.53), kind=kOutput, calls=%fused_computation.6 | convolution fusion | flops 1614807040 | bytes 10223617 | tf_op jit(solution)/shard_map/dot_general | solution.py:143
  307.0 59.1 %all-to-all-done.1 = bf16[64,24,2048]{2,1,0:T(8,128)(2,1)} async-done(((bf16[64,24,2048]{2,1,0:T(8,128)(2,1)}), bf16[64,24,2048]{2,1,0:T(8,128)(2,1)}, u32[]{:S(2)}, u32[]{:S(2)}) %all-to-all-start.1) | async-done | bytes 6291488 | tf_op jit(solution)/shard_map/all_to_all | solution.py:153
  366.1 10.6 %all-to-all-start.3 = ((bf16[64,24,2048]{2,1,0:T(8,128)(2,1)}), bf16[64,24,2048]{2,1,0:T(8,128)(2,1)}, u32[]{:S(2)}, u32[]{:S(2)}) async-start(bf16[64,24,2048]{2,1,0:T(8,128)(2,1)} %bitcast.128), calls=%async_computation.3 | async-start | bytes 12582912 | tf_op jit(solution)/shard_map/all_to_all | solution.py:156
  377.4 0.5 fusion.37
  378.0 5.9 %fusion.25 = (bf16[1,2048,256]{2,1,0:T(8,128)(2,1)}, f32[1,2048,256]{2,1,0:T(8,128)}, bf16[1,2048,256]{2,1,0:T(8,128)(2,1)}) fusion(f32[2048,256]{1,0:T(8,128)} %get-tuple-element.29, bf16[1,2048,256]{2,1,0:T(8,128)(2,1)} %param.23, bf16[3,2048,256]{2,1,0:T(8,128)(2,1)} %all-gather.3.cloned.1.call-done, pred[]{:T(512)S(6)} %ne.53, ...), kind=kLoop, calls=%fused_computation.58 | loop fusion | flops 12058624 | bytes 13631489 | tf_op jit(solution)/shard_map/broadcast_in_dim | solution.py:187
  383.9 0.9 copy-done.10
  384.8 3.8 fusion.26
  388.6 5.7 %fusion.20 = bf16[128,2048]{1,0:T(8,128)(2,1)} fusion(bf16[1536,2048,1]{1,0,2:T(8,128)(2,1)} %bitcast.14, f32[128,2]{0,1:T(2,128)S(1)} %copy-done.13, s32[1536]{0:T(1024)S(1)} %eq.94, s32[128,2]{0,1:T(2,128)S(1)} %copy.25, s32[1536]{0:T(1024)S(1)} %eq.90, s32[128,2]{0,1:T(2,128)S(1)} %copy-done.12, pred[128,2]{0,1:T(4,128)(4,1)S(1)} %copy.24), kind=kOutput, calls=%fused_computation.53 | convolution fusion | flops 1612972032 | bytes 6831360 | tf_op jit(solution)/shard_map/dot_general | solution.py:172
  394.3 64.6 %all-to-all-done.3 = bf16[64,24,2048]{2,1,0:T(8,128)(2,1)} async-done(((bf16[64,24,2048]{2,1,0:T(8,128)(2,1)}), bf16[64,24,2048]{2,1,0:T(8,128)(2,1)}, u32[]{:S(2)}, u32[]{:S(2)}) %all-to-all-start.3) | async-done | bytes 6291488 | tf_op jit(solution)/shard_map/all_to_all | solution.py:156
  458.9 4.6 convolution_convert_fusion.4
  (71 shorter events, 2.2 us)
Async XLA Ops:
  7.2 44.5 %copy-start = (bf16[128,2048]{1,0:T(8,128)(2,1)S(1)}, bf16[128,2048]{1,0:T(8,128)(2,1)}, u32[]{:S(2)}) copy-start(bf16[128,2048]{1,0:T(8,128)(2,1)} %param.14) | copy-start | bytes 1572868
  10.0 4.1 copy-start.3
  12.8 20.7 %collective-permute-start.2 = (bf16[3,128,2048]{2,1,0:T(8,128)(2,1)}, bf16[3,128,2048]{2,1,0:T(8,128)(2,1)}, u32[]{:S(2)}, u32[]{:S(2)}) collective-permute-start(bf16[3,128,2048]{2,1,0:T(8,128)(2,1)} %fusion.17), channel_id=1, source_target_pairs={{0,16},{1,17},{2,18},{3,19},{4,20},{5,21},{6,22},{7,23},{8,24},{9,... | collective-permute-start | bytes 4718600 | tf_op jit(solution)/shard_map/ppermute | solution.py:17
  15.1 2.9 copy-start.12
  15.1 4.4 copy-start.15
  15.2 6.0 %copy-start.14 = (s32[64]{0:T(128)S(1)}, s32[64]{0:T(128)}, u32[]{:S(2)}) copy-start(s32[64]{0:T(128)} %param.19) | copy-start | bytes 772
  15.2 6.0 %copy-start.2 = (s32[64]{0:T(128)S(1)}, s32[64]{0:T(128)}, u32[]{:S(2)}) copy-start(s32[64]{0:T(128)} %param.18) | copy-start | bytes 772
  15.2 7.6 %copy-start.13 = (f32[128,2]{0,1:T(2,128)S(1)}, f32[128,2]{0,1:T(2,128)}, u32[]{:S(2)}) copy-start(f32[128,2]{0,1:T(2,128)} %param.16) | copy-start | bytes 3076
  17.8 32.5 %collective-permute-start = (bf16[3,1024,256]{2,1,0:T(8,128)(2,1)}, bf16[3,1024,256]{2,1,0:T(8,128)(2,1)}, u32[]{:S(2)}, u32[]{:S(2)}) collective-permute-start(bf16[3,1024,256]{2,1,0:T(8,128)(2,1)} %fusion.19), channel_id=1, source_target_pairs={{0,16},{1,17},{2,18},{3,19},{4,20},{5,21},{6,22},{7,23},{8,24},{9,... | collective-permute-start | bytes 4718600 | tf_op jit(solution)/shard_map/ppermute | solution.py:17
  33.5 33.7 %collective-permute-start.3 = (bf16[3,128,2048]{2,1,0:T(8,128)(2,1)}, bf16[3,128,2048]{2,1,0:T(8,128)(2,1)}, u32[]{:S(2)}, u32[]{:S(2)}) collective-permute-start(bf16[3,128,2048]{2,1,0:T(8,128)(2,1)} %collective-permute-done.2), channel_id=1, source_target_pairs={{0,16},{1,17},{2,18},{3,19},{4,20},{5,21},{6,22},{7,23},{8,24},{9,... | collective-permute-start | bytes 4718600 | tf_op jit(solution)/shard_map/ppermute | solution.py:17
  50.4 33.7 %collective-permute-start.1 = (bf16[3,1024,256]{2,1,0:T(8,128)(2,1)}, bf16[3,1024,256]{2,1,0:T(8,128)(2,1)}, u32[]{:S(2)}, u32[]{:S(2)}) collective-permute-start(bf16[3,1024,256]{2,1,0:T(8,128)(2,1)} %collective-permute-done), channel_id=1, source_target_pairs={{0,16},{1,17},{2,18},{3,19},{4,20},{5,21},{6,22},{7,23},{8,24},{9,... | collective-permute-start | bytes 4718600 | tf_op jit(solution)/shard_map/ppermute | solution.py:17
  51.7 2.4 copy-start.11
  84.1 94.5 %all-to-all-start = ((bf16[64,24,2048]{2,1,0:T(8,128)(2,1)}), bf16[64,24,2048]{2,1,0:T(8,128)(2,1)}, u32[]{:S(2)}, u32[]{:S(2)}) async-start(bf16[64,24,2048]{2,1,0:T(8,128)(2,1)} %bitcast.130), calls=%async_computation | async-start | bytes 12582912 | tf_op jit(solution)/shard_map/all_to_all | solution.py:128
  95.2 94.1 %all-gather.3.cloned.1.call-start = ((), (), s32[]{:S(2)}) async-start(), calls=%async_computation.4 | async-start | bytes 4718592 | tf_op jit(solution)/shard_map/all_gather | solution.py:34
  178.6 94.7 %all-to-all-start.2 = ((bf16[64,24,2048]{2,1,0:T(8,128)(2,1)}), bf16[64,24,2048]{2,1,0:T(8,128)(2,1)}, u32[]{:S(2)}, u32[]{:S(2)}) async-start(bf16[64,24,2048]{2,1,0:T(8,128)(2,1)} %fusion), calls=%async_computation.2 | async-start | bytes 12582912 | tf_op jit(solution)/shard_map/all_to_all | solution.py:129
  187.3 18.6 %all-gather.5.cloned.1.call-start = ((), (), s32[]{:S(2)}) async-start(), calls=%async_computation.5 | async-start | bytes 4718592 | tf_op jit(solution)/shard_map/all_gather | solution.py:34
  273.3 92.8 %all-to-all-start.1 = ((bf16[64,24,2048]{2,1,0:T(8,128)(2,1)}), bf16[64,24,2048]{2,1,0:T(8,128)(2,1)}, u32[]{:S(2)}, u32[]{:S(2)}) async-start(bf16[64,24,2048]{2,1,0:T(8,128)(2,1)} %bitcast.129), calls=%async_computation.1 | async-start | bytes 12582912 | tf_op jit(solution)/shard_map/all_to_all | solution.py:153
  282.8 95.1 %all-reduce.3.cloned.1.call-start = ((), (), s32[]{:S(2)}) async-start(), calls=%async_computation.6 | async-start | bytes 8388608 | tf_op jit(solution)/shard_map/psum | solution.py:160
  282.9 6.6 %copy-start.4 = (f32[1,256,2048]{2,1,0:T(8,128)S(1)}, f32[1,256,2048]{2,1,0:T(8,128)}, u32[]{:S(2)}) copy-start(f32[1,256,2048]{2,1,0:T(8,128)} %param.21) | copy-start | bytes 6291460
  282.9 6.6 %copy-start.9 = (f32[1536,256]{1,0:T(8,128)S(1)}, f32[1536,256]{1,0:T(8,128)}, u32[]{:S(2)}) copy-start(f32[1536,256]{1,0:T(8,128)} %fusion.33) | copy-start | bytes 4718596
  366.1 92.8 %all-to-all-start.3 = ((bf16[64,24,2048]{2,1,0:T(8,128)(2,1)}), bf16[64,24,2048]{2,1,0:T(8,128)(2,1)}, u32[]{:S(2)}, u32[]{:S(2)}) async-start(bf16[64,24,2048]{2,1,0:T(8,128)(2,1)} %bitcast.128), calls=%async_computation.3 | async-start | bytes 12582912 | tf_op jit(solution)/shard_map/all_to_all | solution.py:156
  377.9 5.9 %copy-start.5 = (f32[1,256,2048]{2,1,0:T(8,128)S(1)}, f32[1,256,2048]{2,1,0:T(8,128)}, u32[]{:S(2)}) copy-start(f32[1,256,2048]{2,1,0:T(8,128)} %param.21) | copy-start | bytes 6291460
  377.9 5.9 %copy-start.6 = (bf16[3,256,2048]{2,1,0:T(8,128)(2,1)S(1)}, bf16[3,256,2048]{2,1,0:T(8,128)(2,1)}, u32[]{:S(2)}) copy-start(bf16[3,256,2048]{2,1,0:T(8,128)(2,1)} %all-gather.5.cloned.1.call-done) | copy-start | bytes 9437188
  378.0 5.9 %copy-start.7 = (bf16[1,256,2048]{2,1,0:T(8,128)(2,1)S(1)}, bf16[1,256,2048]{2,1,0:T(8,128)(2,1)}, u32[]{:S(2)}) copy-start(bf16[1,256,2048]{2,1,0:T(8,128)(2,1)} %param.24) | copy-start | bytes 3145732
  378.0 5.9 %copy-start.8 = (bf16[1,256,2048]{2,1,0:T(8,128)(2,1)S(1)}, bf16[1,256,2048]{2,1,0:T(8,128)(2,1)}, u32[]{:S(2)}) copy-start(bf16[1,256,2048]{2,1,0:T(8,128)(2,1)} %param.25) | copy-start | bytes 3145732
  378.0 6.8 %copy-start.10 = (f32[256,2048]{1,0:T(8,128)S(1)}, f32[256,2048]{1,0:T(8,128)}, u32[]{:S(2)}) copy-start(f32[256,2048]{1,0:T(8,128)} %get-tuple-element.30) | copy-start | bytes 6291460
  458.9 4.6 copy-start.1
Sparse Core Ops, SparseCore 0:
  97.7 16.0 all-gather.2
  189.7 16.0 all-gather.4
  301.4 35.2 all-reduce.2

commit v7 on v6

--- a/solution.py
+++ b/solution.py
@@ -124,12 +124,11 @@
     second_in = jnp.where(moved, other_m[1], second_in)
     first_out = jnp.where(moved, other_m[2], first_out)
     second_out = jnp.where(moved, other_m[3], second_out)
-    recv_x, recv_g = (
-        lax.all_to_all(send_x, "expert", split_axis=0, concat_axis=0, tiled=True),
-        lax.all_to_all(send_g, "expert", split_axis=0, concat_axis=0, tiled=True),
-    )
-    rows = recv_x.reshape(-1, width)
-    grows = recv_g.reshape(-1, width)
+    recv = lax.all_to_all(
+        jnp.stack([send_x, send_g], axis=1), "expert", split_axis=0, concat_axis=0, tiled=True
+    )
+    rows = recv[:, 0].reshape(-1, width)
+    grows = recv[:, 1].reshape(-1, width)
     wb_in = weight_in.astype(jnp.bfloat16)
     wb_out = weight_out.astype(jnp.bfloat16)
     pre = jnp.dot(rows, wb_in, preferred_element_type=jnp.float32)
@@ -149,14 +148,17 @@
     grad_out = lax.dot_general(
         hidden, grows, (((0,), (0,)), ((), ())), preferred_element_type=jnp.float32
     )
-    back_part, back_dx = (
-        lax.all_to_all(
-            part.reshape(nexp, slots, width), "expert", split_axis=0, concat_axis=0, tiled=True
+    back = lax.all_to_all(
+        jnp.stack(
+            [part.reshape(nexp, slots, width), xpart.reshape(nexp, slots, width)], axis=1
         ),
-        lax.all_to_all(
-            xpart.reshape(nexp, slots, width), "expert", split_axis=0, concat_axis=0, tiled=True
-        ),
-    )
+        "expert",
+        split_axis=0,
+        concat_axis=0,
+        tiled=True,
+    )
+    back_part = back[:, 0]
+    back_dx = back[:, 1]
     grad_in, grad_out = lax.psum((grad_in, grad_out), "dp")
     new_w_in, new_m_in, new_v_in = adamw(weight_in, first_in, second_in, grad_in)
     new_w_out, new_m_out, new_v_out = adamw(weight_out, first_out, second_out, grad_out)

time: 473 us -> 536 us (1.13)
  waiting for transfers between devices: 318 us -> 381 us
  starting transfers between devices: 44.3 us -> 26.6 us
  local copies, waits for them, and re-layouts: 15.9 us -> 32.6 us
  other arithmetic: 24.2 us -> 39.9 us
  matrix products: 53.1 us -> 40.9 us
    all_to_all x4 -> x2, waiting for transfers between devices: 267 us -> 307 us  [the longest x1 187 us: body(): lax.all_to_all(jnp.stack([send_x, send_g], axis=1), 'expert', split_axis=...]
    psum x1, waiting for transfers between devices: 0.02 us -> 34.2 us  [body(): grad_in, grad_out = lax.psum((grad_in, grad_out), 'dp')]
    all_to_all x4 -> x2, starting transfers between devices: 39.9 us -> 22 us  [the longest x1 11.1 us: body(): lax.all_to_all(jnp.stack([send_x, send_g], axis=1), 'expert', split_axis=...]
    slice x1 -> x3, local copies, waits for them, and re-layouts: 0.18 us -> 16.5 us  [the longest x1 10.6 us: body(): grows = recv[:, 1].reshape(-1, width)]
    another operation x2 -> x4, other arithmetic: 0.63 us -> 16.4 us  [the longest x1 10.5 us: body(): jnp.stack([send_x, send_g], axis=1)]
    all_gather x2, waiting for transfers between devices: 10.5 us -> 0.01 us  [join(): return tuple((lax.all_gather(m, 'dp', axis=1, tiled=True) for m in moved))]
  transfers between devices with their start and end apart: 11 -> 9, of which waited for: 9 -> 7; matrix products, arithmetic and copies ran while one was open for 17% -> 13% of each run, Pallas kernels for 0% -> 0%
where the time goes in v7:
time: 536 us; the launch traced here: 535 us
  waiting for transfers between devices  381 us (71%)
  matrix products  40.9 us (8%)
  other arithmetic  39.9 us (7%)
  local copies, waits for them, and re-layouts  32.6 us (6%)
  starting transfers between devices  26.6 us (5%)
  between operations  14.8 us (3%)
    all_to_all x1, waiting for transfers between devices, body(): lax.all_to_all(jnp.stack([send_x, send_g], axis=1), 'expert', split_axis=...  187 us
    all_to_all x1, waiting for transfers between devices, body(): lax.all_to_all(jnp.stack([part.reshape(nexp, slots, width), xpart.reshape...  120 us
    ppermute x4, waiting for transfers between devices, relay(): return lax.ppermute(block, ('dp', 'expert'), route)  38.3 us
    psum x1, waiting for transfers between devices, body(): grad_in, grad_out = lax.psum((grad_in, grad_out), 'dp')  34.2 us
    all_to_all x1, starting transfers between devices, body(): lax.all_to_all(jnp.stack([send_x, send_g], axis=1), 'expert', split_axis=...  11.1 us
    all_to_all x1, starting transfers between devices, body(): lax.all_to_all(jnp.stack([part.reshape(nexp, slots, width), xpart.reshape...  10.9 us
  transfers between devices with their start and end apart: 9, of which 7 were waited for; matrix products, arithmetic and copies ran while one was open for 13% of the time, Pallas kernels for 0%

profile of v7, /device:TPU:50, one launch (start us, length us, event | category | flops | bytes accessed | tf_op | source)
XLA Modules:
  0.0 535.4 jit_solution(4924010102364820374)
XLA Ops:
  7.2 2.7 convert_element_type.102
  9.9 2.7 fusion.19
  12.7 1.3 collective-permute-start
  13.9 1.1 convert_element_type.103
  15.1 2.7 fusion.17
  17.8 0.2 collective-permute-start.2
  18.5 0.6 reduce-window.6
  19.1 0.2 slice_reduce_fusion
  19.4 0.1 mul.176
  19.7 1.4 scatter_custom_fusion
  21.2 0.8 gather_fusion
  22.0 0.6 gather_fusion.1
  23.1 9.5 %gather_fusion.2 = f32[1536]{0:T(1024)S(1)} fusion(f32[257]{0:T(512)S(1)} %pad_maximum_fusion.2, s32[2048]{0:T(1024)S(1)} %pad_clamp_fusion), kind=kCustom, calls=%fused_computation.2 | custom fusion | bytes 18432 | tf_op jit(solution)/shard_map/jit(_take)/gather | solution.py:102
  32.8 0.6 collective-permute-done
  33.4 1.3 collective-permute-start.1
  34.7 15.6 %collective-permute-done.2 = bf16[3,128,2048]{2,1,0:T(8,128)(2,1)} collective-permute-done((bf16[3,128,2048]{2,1,0:T(8,128)(2,1)}, bf16[3,128,2048]{2,1,0:T(8,128)(2,1)}, u32[]{:S(2)}, u32[]{:S(2)}) %collective-permute-start.2) | collective-permute-done | bytes 1572896 | tf_op jit(solution)/shard_map/ppermute | solution.py:17
  50.2 1.3 collective-permute-start.3
  51.6 2.4 convolution_convert_fusion.2
  54.0 4.0 convolution_convert_fusion.3
  58.0 3.8 fusion
  61.7 5.4 %collective-permute-done.1 = bf16[3,1024,256]{2,1,0:T(8,128)(2,1)} collective-permute-done((bf16[3,1024,256]{2,1,0:T(8,128)(2,1)}, bf16[3,1024,256]{2,1,0:T(8,128)(2,1)}, u32[]{:S(2)}, u32[]{:S(2)}) %collective-permute-start.1) | collective-permute-done | bytes 1572896 | tf_op jit(solution)/shard_map/ppermute | solution.py:17
  67.1 16.9 %collective-permute-done.3 = bf16[3,128,2048]{2,1,0:T(8,128)(2,1)} collective-permute-done((bf16[3,128,2048]{2,1,0:T(8,128)(2,1)}, bf16[3,128,2048]{2,1,0:T(8,128)(2,1)}, u32[]{:S(2)}, u32[]{:S(2)}) %collective-permute-start.3) | collective-permute-done | bytes 1572896 | tf_op jit(solution)/shard_map/ppermute | solution.py:17
  84.0 10.5 %pad_maximum_fusion = bf16[64,2,24,2048]{3,2,1,0:T(8,128)(2,1)} fusion(bf16[64,1,24,2048]{3,2,1,0:T(8,128)(2,1)} %bitcast.137, bf16[64,1,24,2048]{3,2,1,0:T(8,128)(2,1)} %bitcast.136), kind=kLoop, calls=%fused_computation.4 | loop fusion | flops 6291456 | bytes 25165824 | tf_op jit(solution)/shard_map/stack | solution.py:128
  94.4 11.1 %all-to-all-start = ((bf16[64,2,24,2048]{3,2,1,0:T(8,128)(2,1)}), bf16[64,2,24,2048]{3,2,1,0:T(8,128)(2,1)}, u32[]{:S(2)}, u32[]{:S(2)}) async-start(bf16[64,2,24,2048]{3,2,1,0:T(8,128)(2,1)} %pad_maximum_fusion), calls=%async_computation | async-start | bytes 25165824 | tf_op jit(solution)/shard_map/all_to_all | solution.py:127
  105.6 0.7 all-gather.3.cloned.1.call-update
  106.3 0.2 all-gather.5.cloned.1.call-start
  106.5 0.5 all-gather.5.cloned.1.call-update
  107.1 0.6 dynamic-slice.2
  108.3 187.1 %all-to-all-done = bf16[64,2,24,2048]{3,2,1,0:T(8,128)(2,1)} async-done(((bf16[64,2,24,2048]{3,2,1,0:T(8,128)(2,1)}), bf16[64,2,24,2048]{3,2,1,0:T(8,128)(2,1)}, u32[]{:S(2)}, u32[]{:S(2)}) %all-to-all-start) | async-done | bytes 12582944 | tf_op jit(solution)/shard_map/all_to_all | solution.py:127
  295.4 10.6 %fusion.55 = (bf16[64,1,24,2048]{3,2,1,0:T(8,128)(2,1)}, bf16[64,1,24,2048]{3,2,1,0:T(8,128)(2,1)}) fusion(bf16[64,2,24,2048]{3,2,1,0:T(8,128)(2,1)} %all-to-all-done), kind=kLoop, calls=%fused_computation.124 | loop fusion | bytes 25165824 | tf_op jit(solution)/shard_map/slice | solution.py:131
  306.0 6.1 %fusion.33 = f32[1536,256]{1,0:T(8,128)} fusion(bf16[1536,2048]{1,0:T(8,128)(2,1)} %bitcast.139, f32[1,2048,256]{2,1,0:T(8,128)} %param.20, bf16[3,2048,256]{2,1,0:T(8,128)(2,1)} %all-gather.3.cloned.1.call-done, pred[]{:T(512)S(6)} %ne.53), kind=kOutput, calls=%fused_computation.70 | convolution fusion | flops 1611661312 | bytes 11010049 | tf_op jit(solution)/shard_map/dot_general | solution.py:134
  312.1 3.9 convolution_convert_fusion.1
  316.1 4.2 fusion.15
  320.3 3.1 convolution_convert_fusion
  323.4 5.3 pad_maximum_fusion.1
  328.7 10.9 %all-to-all-start.1 = ((bf16[64,2,24,2048]{3,2,1,0:T(8,128)(2,1)}), bf16[64,2,24,2048]{3,2,1,0:T(8,128)(2,1)}, u32[]{:S(2)}, u32[]{:S(2)}) async-start(bf16[64,2,24,2048]{3,2,1,0:T(8,128)(2,1)} %pad_maximum_fusion.1), calls=%async_computation.1 | async-start | bytes 25165824 | tf_op jit(solution)/shard_map/all_to_all | solution.py:151
  339.6 0.3 all-reduce.3.cloned.1.call-start
  339.9 6.5 %fusion.53 = f32[256,2048]{1,0:T(8,128)} fusion(bf16[1536,2048]{1,0:T(8,128)(2,1)} %bitcast.141, f32[1536,256]{1,0:T(8,128)} %fusion.33), kind=kOutput, calls=%fused_computation.122 | convolution fusion | flops 1614151680 | bytes 9961472 | tf_op jit(solution)/shard_map/dot_general | solution.py:148
  346.4 6.0 %fusion.56 = f32[2048,256]{1,0:T(8,128)} fusion(bf16[1536,2048]{1,0:T(8,128)(2,1)} %bitcast.140, bf16[1536,256]{1,0:T(8,128)(2,1)S(1)} %fusion.15), kind=kOutput, calls=%fused_computation.125 | convolution fusion | flops 1610612736 | bytes 9175040 | tf_op jit(solution)/shard_map/dot_general | solution.py:145
  353.2 0.5 fusion.37
  353.6 34.2 %all-reduce.3.cloned.1.call-done = (f32[2048,256]{1,0:T(8,128)}, f32[256,2048]{1,0:T(8,128)}) async-done(((f32[2048,256]{1,0:T(8,128)}, f32[256,2048]{1,0:T(8,128)}), (f32[2048,256]{1,0:T(8,128)}, f32[256,2048]{1,0:T(8,128)})) %all-reduce.3.cloned.1.call-update) | async-done | bytes 4194320 | tf_op jit(solution)/shard_map/psum | solution.py:162
  387.8 5.6 %fusion.26 = (bf16[1,256,2048]{2,1,0:T(8,128)(2,1)}, f32[1,256,2048]{2,1,0:T(8,128)}, bf16[1,256,2048]{2,1,0:T(8,128)(2,1)}) fusion(f32[256,2048]{1,0:T(8,128)} %get-tuple-element.30, bf16[1,256,2048]{2,1,0:T(8,128)(2,1)} %param.25, bf16[3,256,2048]{2,1,0:T(8,128)(2,1)} %all-gather.5.cloned.1.call-done, pred[]{:T(512)S(6)} %ne.53, ...), kind=kLoop, calls=%fused_computation.61 | loop fusion | flops 12058624 | bytes 13631489 | tf_op jit(solution)/shard_map/broadcast_in_dim | solution.py:191
  393.6 1.1 copy-done.11
  394.6 4.0 fusion.25
  398.6 119.8 %all-to-all-done.1 = bf16[64,2,24,2048]{3,2,1,0:T(8,128)(2,1)} async-done(((bf16[64,2,24,2048]{3,2,1,0:T(8,128)(2,1)}), bf16[64,2,24,2048]{3,2,1,0:T(8,128)(2,1)}, u32[]{:S(2)}, u32[]{:S(2)}) %all-to-all-start.1) | async-done | bytes 12582944 | tf_op jit(solution)/shard_map/all_to_all | solution.py:151
  518.4 5.6 %fusion.54 = (bf16[64,1,24,2048]{3,2,1,0:T(8,128)(2,1)S(1)}, bf16[64,1,24,2048]{3,2,1,0:T(8,128)(2,1)S(1)}) fusion(bf16[64,2,24,2048]{3,2,1,0:T(8,128)(2,1)} %all-to-all-done.1), kind=kLoop, calls=%fused_computation.123 | loop fusion | bytes 25165824 | tf_op jit(solution)/shard_map/slice | solution.py:161
  524.0 3.0 fusion.20
  527.0 1.9 convolution_convert_fusion.4
  (73 shorter events, 2.5 us)
Async XLA Ops:
  7.2 44.4 %copy-start = (bf16[128,2048]{1,0:T(8,128)(2,1)S(1)}, bf16[128,2048]{1,0:T(8,128)(2,1)}, u32[]{:S(2)}) copy-start(bf16[128,2048]{1,0:T(8,128)(2,1)} %param.14) | copy-start | bytes 1572868
  9.9 4.0 copy-start.3
  12.7 20.7 %collective-permute-start = (bf16[3,1024,256]{2,1,0:T(8,128)(2,1)}, bf16[3,1024,256]{2,1,0:T(8,128)(2,1)}, u32[]{:S(2)}, u32[]{:S(2)}) collective-permute-start(bf16[3,1024,256]{2,1,0:T(8,128)(2,1)} %fusion.19), channel_id=1, source_target_pairs={{0,16},{1,17},{2,18},{3,19},{4,20},{5,21},{6,22},{7,23},{8,24},{9,... | collective-permute-start | bytes 4718600 | tf_op jit(solution)/shard_map/ppermute | solution.py:17
  15.1 3.0 copy-start.13
  15.1 4.5 copy-start.16
  15.1 6.1 %copy-start.15 = (s32[64]{0:T(128)S(1)}, s32[64]{0:T(128)}, u32[]{:S(2)}) copy-start(s32[64]{0:T(128)} %param.19) | copy-start | bytes 772
  15.1 6.1 %copy-start.2 = (s32[64]{0:T(128)S(1)}, s32[64]{0:T(128)}, u32[]{:S(2)}) copy-start(s32[64]{0:T(128)} %param.18) | copy-start | bytes 772
  15.1 7.7 %copy-start.14 = (f32[128,2]{0,1:T(2,128)S(1)}, f32[128,2]{0,1:T(2,128)}, u32[]{:S(2)}) copy-start(f32[128,2]{0,1:T(2,128)} %param.16) | copy-start | bytes 3076
  17.8 32.4 %collective-permute-start.2 = (bf16[3,128,2048]{2,1,0:T(8,128)(2,1)}, bf16[3,128,2048]{2,1,0:T(8,128)(2,1)}, u32[]{:S(2)}, u32[]{:S(2)}) collective-permute-start(bf16[3,128,2048]{2,1,0:T(8,128)(2,1)} %fusion.17), channel_id=1, source_target_pairs={{0,16},{1,17},{2,18},{3,19},{4,20},{5,21},{6,22},{7,23},{8,24},{9,... | collective-permute-start | bytes 4718600 | tf_op jit(solution)/shard_map/ppermute | solution.py:17
  33.4 33.7 %collective-permute-start.1 = (bf16[3,1024,256]{2,1,0:T(8,128)(2,1)}, bf16[3,1024,256]{2,1,0:T(8,128)(2,1)}, u32[]{:S(2)}, u32[]{:S(2)}) collective-permute-start(bf16[3,1024,256]{2,1,0:T(8,128)(2,1)} %collective-permute-done), channel_id=1, source_target_pairs={{0,16},{1,17},{2,18},{3,19},{4,20},{5,21},{6,22},{7,23},{8,24},{9,... | collective-permute-start | bytes 4718600 | tf_op jit(solution)/shard_map/ppermute | solution.py:17
  50.2 33.7 %collective-permute-start.3 = (bf16[3,128,2048]{2,1,0:T(8,128)(2,1)}, bf16[3,128,2048]{2,1,0:T(8,128)(2,1)}, u32[]{:S(2)}, u32[]{:S(2)}) collective-permute-start(bf16[3,128,2048]{2,1,0:T(8,128)(2,1)} %collective-permute-done.2), channel_id=1, source_target_pairs={{0,16},{1,17},{2,18},{3,19},{4,20},{5,21},{6,22},{7,23},{8,24},{9,... | collective-permute-start | bytes 4718600 | tf_op jit(solution)/shard_map/ppermute | solution.py:17
  51.6 2.4 copy-start.12
  94.4 201.0 %all-to-all-start = ((bf16[64,2,24,2048]{3,2,1,0:T(8,128)(2,1)}), bf16[64,2,24,2048]{3,2,1,0:T(8,128)(2,1)}, u32[]{:S(2)}, u32[]{:S(2)}) async-start(bf16[64,2,24,2048]{3,2,1,0:T(8,128)(2,1)} %pad_maximum_fusion), calls=%async_computation | async-start | bytes 25165824 | tf_op jit(solution)/shard_map/all_to_all | solution.py:127
  105.6 200.5 %all-gather.3.cloned.1.call-start = ((), (), s32[]{:S(2)}) async-start(), calls=%async_computation.2 | async-start | bytes 4718592 | tf_op jit(solution)/shard_map/all_gather | solution.py:34
  106.3 205.8 %all-gather.5.cloned.1.call-start = ((), (), s32[]{:S(2)}) async-start(), calls=%async_computation.3 | async-start | bytes 4718592 | tf_op jit(solution)/shard_map/all_gather | solution.py:34
  312.1 3.9 copy-start.6
  312.1 4.0 copy-start.10
  316.1 4.2 copy-start.4
  328.7 189.7 %all-to-all-start.1 = ((bf16[64,2,24,2048]{3,2,1,0:T(8,128)(2,1)}), bf16[64,2,24,2048]{3,2,1,0:T(8,128)(2,1)}, u32[]{:S(2)}, u32[]{:S(2)}) async-start(bf16[64,2,24,2048]{3,2,1,0:T(8,128)(2,1)} %pad_maximum_fusion.1), calls=%async_computation.1 | async-start | bytes 25165824 | tf_op jit(solution)/shard_map/all_to_all | solution.py:151
  339.6 48.2 %all-reduce.3.cloned.1.call-start = ((), (), s32[]{:S(2)}) async-start(), calls=%async_computation.4 | async-start | bytes 8388608 | tf_op jit(solution)/shard_map/psum | solution.py:162
  387.8 5.7 %copy-start.5 = (f32[1,2048,256]{2,1,0:T(8,128)S(1)}, f32[1,2048,256]{2,1,0:T(8,128)}, u32[]{:S(2)}) copy-start(f32[1,2048,256]{2,1,0:T(8,128)} %param.20) | copy-start | bytes 6291460
  387.8 5.7 %copy-start.7 = (bf16[3,2048,256]{2,1,0:T(8,128)(2,1)S(1)}, bf16[3,2048,256]{2,1,0:T(8,128)(2,1)}, u32[]{:S(2)}) copy-start(bf16[3,2048,256]{2,1,0:T(8,128)(2,1)} %all-gather.3.cloned.1.call-done) | copy-start | bytes 9437188
  387.8 5.7 %copy-start.8 = (bf16[1,2048,256]{2,1,0:T(8,128)(2,1)S(1)}, bf16[1,2048,256]{2,1,0:T(8,128)(2,1)}, u32[]{:S(2)}) copy-start(bf16[1,2048,256]{2,1,0:T(8,128)(2,1)} %param.22) | copy-start | bytes 3145732
  387.8 5.8 %copy-start.9 = (bf16[1,2048,256]{2,1,0:T(8,128)(2,1)S(1)}, bf16[1,2048,256]{2,1,0:T(8,128)(2,1)}, u32[]{:S(2)}) copy-start(bf16[1,2048,256]{2,1,0:T(8,128)(2,1)} %param.23) | copy-start | bytes 3145732
  387.8 6.8 %copy-start.11 = (f32[2048,256]{1,0:T(8,128)S(1)}, f32[2048,256]{1,0:T(8,128)}, u32[]{:S(2)}) copy-start(f32[2048,256]{1,0:T(8,128)} %get-tuple-element.29) | copy-start | bytes 6291460
  527.0 1.9 copy-start.1
Sparse Core Ops, SparseCore 0:
  108.0 16.0 all-gather.2
  125.8 16.1 all-gather.4
  352.5 35.1 all-reduce.2

commit v8 on v6

--- a/solution.py
+++ b/solution.py
@@ -6,18 +6,18 @@
 GROUP = 4
 
 
-def relay(block, step):
+def relay(block, step, both=True):
     ndp = lax.axis_size("dp")
     nexp = lax.axis_size("expert")
     route = []
     for d in range(ndp):
-        sign = 1 if d % 2 == 0 else -1
+        sign = 1 if d % 2 == 0 and both else -1
         for e in range(nexp):
             route.append((d * nexp + e, d * nexp + (e + sign * step) % nexp))
     return lax.ppermute(block, ("dp", "expert"), route)
 
 
-def migrate(groups):
+def migrate(groups, both=True):
     ndp = lax.axis_size("dp")
     step = lax.axis_size("expert") // 4
     here = lax.axis_index("dp")
@@ -25,8 +25,8 @@
         lax.dynamic_slice_in_dim(g, here * (g.shape[1] // ndp), g.shape[1] // ndp, 1)
         for g in groups
     )
-    moved = relay(halves, step)
-    moved = relay(moved, step)
+    moved = relay(halves, step, both)
+    moved = relay(moved, step, both)
     return moved
 
 
@@ -108,14 +108,16 @@
     weight_in, weight_out = (w_in[0], w_out[0])
     first_in, second_in, first_out, second_out = (m_in[0], v_in[0], m_out[0], v_out[0])
     halves = migrate(
-        (
-            jnp.stack([weight_in.astype(jnp.bfloat16), first_in, second_in]),
-            jnp.stack([weight_out.astype(jnp.bfloat16), first_out, second_out]),
-        )
+        (weight_in.astype(jnp.bfloat16)[None], weight_out.astype(jnp.bfloat16)[None])
     )
     send_x, send_g, halves = lax.optimization_barrier((send_x, send_g, halves))
     group_in, group_out = join(halves)
-    other = (group_in[0], group_out[0], group_in[1], group_in[2], group_out[1], group_out[2])
+    recv_x = lax.all_to_all(send_x, "expert", split_axis=0, concat_axis=0, tiled=True)
+    recv_x, moments = lax.optimization_barrier(
+        (recv_x, (jnp.stack([first_in, second_in]), jnp.stack([first_out, second_out])))
+    )
+    moment_in, moment_out = join(migrate(moments, False))
+    other = (group_in[0], group_out[0], moment_in[0], moment_in[1], moment_out[0], moment_out[1])
     other_w = (other[0].astype(weight_in.dtype), other[1].astype(weight_out.dtype))
     other_m = other[2:]
     weight_in = jnp.where(moved, other_w[0], weight_in)
@@ -124,10 +126,7 @@
     second_in = jnp.where(moved, other_m[1], second_in)
     first_out = jnp.where(moved, other_m[2], first_out)
     second_out = jnp.where(moved, other_m[3], second_out)
-    recv_x, recv_g = (
-        lax.all_to_all(send_x, "expert", split_axis=0, concat_axis=0, tiled=True),
-        lax.all_to_all(send_g, "expert", split_axis=0, concat_axis=0, tiled=True),
-    )
+    recv_g = lax.all_to_all(send_g, "expert", split_axis=0, concat_axis=0, tiled=True)
     rows = recv_x.reshape(-1, width)
     grows = recv_g.reshape(-1, width)
     wb_in = weight_in.astype(jnp.bfloat16)

time: 473 us -> 548 us (1.16)
  blocking collectives: 0 us -> 81.5 us
    ppermute x4 -> x8, waiting for transfers between devices: 38.5 us -> 236 us  [relay(): return lax.ppermute(block, ('dp', 'expert'), route)]
    all_to_all x1 -> x0, waiting for transfers between devices: 82.6 us -> none  [body(): lax.all_to_all(send_x, 'expert', split_axis=0, concat_axis=0, tiled=True)]
    all_to_all x0 -> x1, blocking collectives: none -> 81.5 us  [body(): lax.all_to_all(send_x, 'expert', split_axis=0, concat_axis=0, tiled=True)]
    all_to_all x1, waiting for transfers between devices: 64.6 us -> 0.01 us  [body(): lax.all_to_all(xpart.reshape(nexp, slots, width), 'expert', split_axis=0,...]
    all_to_all x1, waiting for transfers between devices: 59.1 us -> 0.01 us  [body(): lax.all_to_all(part.reshape(nexp, slots, width), 'expert', split_axis=0,...]
    all_gather x2 -> x4, waiting for transfers between devices: 10.5 us -> 30.2 us  [join(): return tuple((lax.all_gather(m, 'dp', axis=1, tiled=True) for m in moved))]
    all_to_all x1, waiting for transfers between devices: 61.1 us -> 49.3 us  [body(): lax.all_to_all(send_g, 'expert', split_axis=0, concat_axis=0, tiled=True)]
    all_to_all x1 -> x0, starting transfers between devices: 11.1 us -> none  [body(): lax.all_to_all(send_x, 'expert', split_axis=0, concat_axis=0, tiled=True)]
  transfers between devices with their start and end apart: 11 -> 16, of which waited for: 9 -> 9; matrix products, arithmetic and copies ran while one was open for 17% -> 16% of each run, Pallas kernels for 0% -> 0%
where the time goes in v8:
time: 548 us; the launch traced here: 545 us
  waiting for transfers between devices  317 us (58%)
  blocking collectives  81.5 us (15%)
  matrix products  50.3 us (9%)
  starting transfers between devices  40.1 us (7%)
  other arithmetic  21.2 us (4%)
  local copies, waits for them, and re-layouts  20.3 us (4%)
  between operations  14.9 us (3%)
    ppermute x8, waiting for transfers between devices, relay(): return lax.ppermute(block, ('dp', 'expert'), route)  236 us
    all_to_all x1, blocking collectives, body(): lax.all_to_all(send_x, 'expert', split_axis=0, concat_axis=0, tiled=True)  81.5 us
    all_to_all x1, waiting for transfers between devices, body(): lax.all_to_all(send_g, 'expert', split_axis=0, concat_axis=0, tiled=True)  49.3 us
    all_gather x4, waiting for transfers between devices, join(): return tuple((lax.all_gather(m, 'dp', axis=1, tiled=True) for m in moved))  30.2 us
    all_to_all x1, starting transfers between devices, body(): lax.all_to_all(xpart.reshape(nexp, slots, width), 'expert', split_axis=0,...  15.5 us
  transfers between devices with their start and end apart: 16, of which 9 were waited for; matrix products, arithmetic and copies ran while one was open for 16% of the time, Pallas kernels for 0%

profile of v8, /device:TPU:50, one launch (start us, length us, event | category | flops | bytes accessed | tf_op | source)
XLA Modules:
  0.0 545.2 jit_solution(1023478086548696622)
XLA Ops:
  7.2 1.4 dynamic-slice_convert_fusion
  8.6 1.4 collective-permute-start.2
  10.0 1.3 dynamic-slice_convert_fusion.1
  11.2 0.3 collective-permute-start
  12.0 0.8 gather_fusion
  13.1 0.6 reduce-window.6
  14.0 1.4 scatter_custom_fusion
  15.5 0.6 gather_fusion.1
  16.6 9.5 %gather_fusion.2 = f32[1536]{0:T(1024)S(1)} fusion(f32[257]{0:T(512)S(1)} %pad_maximum_fusion.2, s32[2048]{0:T(1024)S(1)} %pad_clamp_fusion), kind=kCustom, calls=%fused_computation.2 | custom fusion | bytes 18432 | tf_op jit(solution)/shard_map/jit(_take)/gather | solution.py:102
  26.3 2.4 convolution_convert_fusion.2
  28.7 1.6 collective-permute-start.3
  30.4 1.6 collective-permute-start.1
  32.0 3.7 fusion
  35.7 4.0 convolution_convert_fusion.3
  39.7 3.9 collective-permute-done.1
  43.6 81.5 %all_to_all.20 = bf16[64,24,2048]{2,1,0:T(8,128)(2,1)} all-to-all(bf16[64,24,2048]{2,1,0:T(8,128)(2,1)} %bitcast.131), channel_id=1, replica_groups=mesh['dp'=2,'expert'=64] {'expert'}, dimensions={0} | all-to-all | bytes 12582912 | tf_op jit(solution)/shard_map/all_to_all | solution.py:115
  125.2 8.9 %all-to-all-start.2 = ((bf16[64,24,2048]{2,1,0:T(8,128)(2,1)}), bf16[64,24,2048]{2,1,0:T(8,128)(2,1)}, u32[]{:S(2)}, u32[]{:S(2)}) async-start(bf16[64,24,2048]{2,1,0:T(8,128)(2,1)} %fusion), calls=%async_computation.2 | async-start | bytes 12582912 | tf_op jit(solution)/shard_map/all_to_all | solution.py:129
  134.1 0.7 all-gather.5.cloned.1.call-update
  135.0 0.5 all-gather.7.cloned.1.call-update
  135.5 1.5 pad_maximum_fusion
  137.0 0.6 dynamic-slice.6
  138.3 3.3 pad_maximum_fusion.1
  141.5 8.6 %all-gather.5.cloned.1.call-done = bf16[1,2048,256]{2,1,0:T(8,128)(2,1)} async-done(((bf16[1,1024,256]{2,1,0:T(8,128)(2,1)}), bf16[1,2048,256]{2,1,0:T(8,128)(2,1)}) %all-gather.5.cloned.1.call-update) | async-done | bytes 1048592 | tf_op jit(solution)/shard_map/all_gather | solution.py:34
  150.1 6.0 %fusion.29 = f32[1536,256]{1,0:T(8,128)} fusion(bf16[1536,2048]{1,0:T(8,128)(2,1)} %bitcast.132, f32[1,2048,256]{2,1,0:T(8,128)S(1)} %copy-done.3, bf16[1,2048,256]{2,1,0:T(8,128)(2,1)} %all-gather.5.cloned.1.call-done, pred[]{:T(512)S(6)} %ne.53), kind=kOutput, calls=%fused_computation.62 | convolution fusion | flops 1611661312 | bytes 11010049 | tf_op jit(solution)/shard_map/dot_general | solution.py:134
  156.1 9.3 %all-gather.7.cloned.1.call-done = bf16[1,256,2048]{2,1,0:T(8,128)(2,1)} async-done(((bf16[1,128,2048]{2,1,0:T(8,128)(2,1)}), bf16[1,256,2048]{2,1,0:T(8,128)(2,1)}) %all-gather.7.cloned.1.call-update) | async-done | bytes 1048592 | tf_op jit(solution)/shard_map/all_gather | solution.py:34
  165.4 6.4 %convolution_convert_fusion.1 = bf16[1536,2048]{1,0:T(8,128)(2,1)} fusion(f32[1,256,2048]{2,1,0:T(8,128)} %param.21, bf16[1,256,2048]{2,1,0:T(8,128)(2,1)} %all-gather.7.cloned.1.call-done, pred[]{:T(512)S(6)} %ne.53, f32[1536,256]{1,0:T(8,128)} %fusion.29), kind=kOutput, calls=%fused_computation.7 | convolution fusion | flops 1618345984 | bytes 11010049 | tf_op jit(solution)/shard_map/dot_general | solution.py:137
  171.8 49.3 %all-to-all-done.2 = bf16[64,24,2048]{2,1,0:T(8,128)(2,1)} async-done(((bf16[64,24,2048]{2,1,0:T(8,128)(2,1)}), bf16[64,24,2048]{2,1,0:T(8,128)(2,1)}, u32[]{:S(2)}, u32[]{:S(2)}) %all-to-all-start.2) | async-done | bytes 6291488 | tf_op jit(solution)/shard_map/all_to_all | solution.py:129
  221.1 9.2 %all-to-all-start.1 = ((bf16[64,24,2048]{2,1,0:T(8,128)(2,1)}), bf16[64,24,2048]{2,1,0:T(8,128)(2,1)}, u32[]{:S(2)}, u32[]{:S(2)}) async-start(bf16[64,24,2048]{2,1,0:T(8,128)(2,1)} %bitcast.129), calls=%async_computation.1 | async-start | bytes 12582912 | tf_op jit(solution)/shard_map/all_to_all | solution.py:152
  230.3 1.3 constant_dynamic-slice_fusion.1
  231.6 0.5 collective-permute-start.4
  232.1 92.3 %collective-permute-done.4 = bf16[2,1024,256]{2,1,0:T(8,128)(2,1)S(1)} collective-permute-done((bf16[2,1024,256]{2,1,0:T(8,128)(2,1)S(1)}, bf16[2,1024,256]{2,1,0:T(8,128)(2,1)S(1)}, u32[]{:S(2)}, u32[]{:S(2)}) %collective-permute-start.4) | collective-permute-done | bytes 1048608 | tf_op jit(solution)/shard_map/ppermute | solution.py:17
  324.4 23.3 %collective-permute-done.5 = bf16[2,1024,256]{2,1,0:T(8,128)(2,1)} collective-permute-done((bf16[2,1024,256]{2,1,0:T(8,128)(2,1)S(1)}, bf16[2,1024,256]{2,1,0:T(8,128)(2,1)}, u32[]{:S(2)}, u32[]{:S(2)}) %collective-permute-start.5) | collective-permute-done | bytes 1048608 | tf_op jit(solution)/shard_map/ppermute | solution.py:17
  347.7 0.3 all-reduce.3.cloned.1.call-start
  348.0 6.6 %fusion.49 = f32[256,2048]{1,0:T(8,128)} fusion(bf16[1536,2048]{1,0:T(8,128)(2,1)} %bitcast.15, f32[1536,256]{1,0:T(8,128)} %fusion.29), kind=kOutput, calls=%fused_computation.116 | convolution fusion | flops 1614151680 | bytes 9961472 | tf_op jit(solution)/shard_map/dot_general | solution.py:148
  354.7 5.6 %fusion.15 = bf16[1536,256]{1,0:T(8,128)(2,1)S(1)} fusion(f32[1536,256]{1,0:T(8,128)S(1)} %copy-done.8, bf16[1536,2048]{1,0:T(8,128)(2,1)} %bitcast.15, f32[1,256,2048]{2,1,0:T(8,128)S(1)} %copy-done.4, bf16[1,256,2048]{2,1,0:T(8,128)(2,1)S(1)} %copy-done.5, pred[]{:T(512)S(6)} %ne.53), kind=kOutput, calls=%fused_computation.42 | convolution fusion | flops 1619525632 | bytes 11796481 | tf_op jit(solution)/shard_map/dot_general | solution.py:138
  360.3 3.2 fusion.50
  363.6 5.8 %convolution_convert_fusion = bf16[1536,2048]{1,0:T(8,128)(2,1)} fusion(bf16[1536,256]{1,0:T(8,128)(2,1)S(1)} %fusion.15, f32[1,2048,256]{2,1,0:T(8,128)S(1)} %copy-done.3, bf16[1,2048,256]{2,1,0:T(8,128)(2,1)} %all-gather.5.cloned.1.call-done, pred[]{:T(512)S(6)} %ne.53), kind=kOutput, calls=%fused_computation.6 | convolution fusion | flops 1614807040 | bytes 10223617 | tf_op jit(solution)/shard_map/dot_general | solution.py:142
  369.4 15.5 %all-to-all-start.3 = ((bf16[64,24,2048]{2,1,0:T(8,128)(2,1)}), bf16[64,24,2048]{2,1,0:T(8,128)(2,1)}, u32[]{:S(2)}, u32[]{:S(2)}) async-start(bf16[64,24,2048]{2,1,0:T(8,128)(2,1)} %bitcast.128), calls=%async_computation.3 | async-start | bytes 12582912 | tf_op jit(solution)/shard_map/all_to_all | solution.py:155
  385.0 1.4 constant_dynamic-slice_fusion
  386.4 0.5 collective-permute-start.6
  386.9 93.4 %collective-permute-done.6 = bf16[2,128,2048]{2,1,0:T(8,128)(2,1)S(1)} collective-permute-done((bf16[2,128,2048]{2,1,0:T(8,128)(2,1)S(1)}, bf16[2,128,2048]{2,1,0:T(8,128)(2,1)S(1)}, u32[]{:S(2)}, u32[]{:S(2)}) %collective-permute-start.6) | collective-permute-done | bytes 1048608 | tf_op jit(solution)/shard_map/ppermute | solution.py:17
  480.2 23.3 %collective-permute-done.7 = bf16[2,128,2048]{2,1,0:T(8,128)(2,1)} collective-permute-done((bf16[2,128,2048]{2,1,0:T(8,128)(2,1)S(1)}, bf16[2,128,2048]{2,1,0:T(8,128)(2,1)}, u32[]{:S(2)}, u32[]{:S(2)}) %collective-permute-start.7) | collective-permute-done | bytes 1048608 | tf_op jit(solution)/shard_map/ppermute | solution.py:17
  504.3 0.5 fusion.33
  504.8 5.7 %fusion.21 = (bf16[1,2048,256]{2,1,0:T(8,128)(2,1)}, f32[1,2048,256]{2,1,0:T(8,128)}, bf16[1,2048,256]{2,1,0:T(8,128)(2,1)}) fusion(f32[2048,256]{1,0:T(8,128)} %get-tuple-element.35, bf16[1,2048,256]{2,1,0:T(8,128)(2,1)} %param.23, bf16[2,2048,256]{2,1,0:T(8,128)(2,1)} %all-gather.9.cloned.1.call-done, pred[]{:T(512)S(6)} %ne.53, ...), kind=kLoop, calls=%fused_computation.50 | loop fusion | flops 12058624 | bytes 13631489 | tf_op jit(solution)/shard_map/broadcast_in_dim | solution.py:186
  510.6 12.3 %all-gather.11.cloned.1.call-done = bf16[2,256,2048]{2,1,0:T(8,128)(2,1)} async-done(((bf16[2,128,2048]{2,1,0:T(8,128)(2,1)}), bf16[2,256,2048]{2,1,0:T(8,128)(2,1)}) %all-gather.11.cloned.1.call-update) | async-done | bytes 2097168 | tf_op jit(solution)/shard_map/all_gather | solution.py:34
  522.9 5.5 %fusion.22 = (bf16[1,256,2048]{2,1,0:T(8,128)(2,1)}, f32[1,256,2048]{2,1,0:T(8,128)}, bf16[1,256,2048]{2,1,0:T(8,128)(2,1)}) fusion(f32[256,2048]{1,0:T(8,128)} %get-tuple-element.36, bf16[1,256,2048]{2,1,0:T(8,128)(2,1)} %param.25, bf16[2,256,2048]{2,1,0:T(8,128)(2,1)} %all-gather.11.cloned.1.call-done, pred[]{:T(512)S(6)} %ne.53, ...), kind=kLoop, calls=%fused_computation.51 | loop fusion | flops 12058624 | bytes 13631489 | tf_op jit(solution)/shard_map/broadcast_in_dim | solution.py:188
  528.3 5.7 %fusion.16 = bf16[128,2048]{1,0:T(8,128)(2,1)} fusion(bf16[1536,2048,1]{1,0,2:T(8,128)(2,1)} %bitcast.14, f32[128,2]{0,1:T(2,128)S(1)} %copy-done.13, s32[1536]{0:T(1024)S(1)} %eq.94, s32[128,2]{0,1:T(2,128)S(1)} %copy.25, s32[1536]{0:T(1024)S(1)} %eq.90, s32[128,2]{0,1:T(2,128)S(1)} %copy-done.12, pred[128,2]{0,1:T(4,128)(4,1)S(1)} %copy.24), kind=kOutput, calls=%fused_computation.45 | convolution fusion | flops 1612972032 | bytes 6831360 | tf_op jit(solution)/shard_map/dot_general | solution.py:171
  534.0 4.6 convolution_convert_fusion.4
  (91 shorter events, 3.0 us)
Async XLA Ops:
  7.2 19.2 %copy-start = (bf16[128,2048]{1,0:T(8,128)(2,1)S(1)}, bf16[128,2048]{1,0:T(8,128)(2,1)}, u32[]{:S(2)}) copy-start(bf16[128,2048]{1,0:T(8,128)(2,1)} %param.14) | copy-start | bytes 1572868
  7.2 4.4 copy-start.12
  7.2 4.7 copy-start.14
  7.2 4.8 copy-start.2
  7.2 6.7 %copy-start.15 = (s32[16]{0:T(128)S(1)}, s32[16]{0:T(128)}, u32[]{:S(2)}) copy-start(s32[16]{0:T(128)} %param.17) | copy-start | bytes 196
  7.2 9.1 %copy-start.13 = (f32[128,2]{0,1:T(2,128)S(1)}, f32[128,2]{0,1:T(2,128)}, u32[]{:S(2)}) copy-start(f32[128,2]{0,1:T(2,128)} %param.16) | copy-start | bytes 3076
  8.6 20.1 %collective-permute-start.2 = (bf16[1,128,2048]{2,1,0:T(8,128)(2,1)S(1)}, bf16[1,128,2048]{2,1,0:T(8,128)(2,1)S(1)}, u32[]{:S(2)}, u32[]{:S(2)}) collective-permute-start(bf16[1,128,2048]{2,1,0:T(8,128)(2,1)S(1)} %dynamic-slice_convert_fusion), channel_id=1, source_target_pairs={{0,16},{1,17},{2,18},{3,19},{4,20},{5,21},{6,22},{7,23},{8,24},{9,... | collective-permute-start | bytes 1572872 | tf_op jit(solution)/shard_map/ppermute | solution.py:17
  11.2 19.1 %collective-permute-start = (bf16[1,1024,256]{2,1,0:T(8,128)(2,1)S(1)}, bf16[1,1024,256]{2,1,0:T(8,128)(2,1)}, u32[]{:S(2)}, u32[]{:S(2)}) collective-permute-start(bf16[1,1024,256]{2,1,0:T(8,128)(2,1)S(1)} %dynamic-slice_convert_fusion.1), channel_id=1, source_target_pairs={{0,16},{1,17},{2,18},{3,19},{4,20},{5,21},{6,22},{7,23},{8,24},{9,... | collective-permute-start | bytes 1572872 | tf_op jit(solution)/shard_map/ppermute | solution.py:17
  28.7 11.0 %collective-permute-start.3 = (bf16[1,128,2048]{2,1,0:T(8,128)(2,1)S(1)}, bf16[1,128,2048]{2,1,0:T(8,128)(2,1)S(1)}, u32[]{:S(2)}, u32[]{:S(2)}) collective-permute-start(bf16[1,128,2048]{2,1,0:T(8,128)(2,1)S(1)} %collective-permute-done.2), channel_id=1, source_target_pairs={{0,16},{1,17},{2,18},{3,19},{4,20},{5,21},{6,22},{7,23},{8,24},{9,... | collective-permute-start | bytes 1572872 | tf_op jit(solution)/shard_map/ppermute | solution.py:17
  30.4 13.2 %collective-permute-start.1 = (bf16[1,1024,256]{2,1,0:T(8,128)(2,1)}, bf16[1,1024,256]{2,1,0:T(8,128)(2,1)S(1)}, u32[]{:S(2)}, u32[]{:S(2)}) collective-permute-start(bf16[1,1024,256]{2,1,0:T(8,128)(2,1)} %collective-permute-done), channel_id=1, source_target_pairs={{0,16},{1,17},{2,18},{3,19},{4,20},{5,21},{6,22},{7,23},{8,24},{9,... | collective-permute-start | bytes 1572872 | tf_op jit(solution)/shard_map/ppermute | solution.py:17
  32.0 3.7 copy-start.11
  39.7 85.4 %copy-start.9 = (bf16[1,128,2048]{2,1,0:T(8,128)(2,1)}, bf16[1,128,2048]{2,1,0:T(8,128)(2,1)S(1)}, u32[]{:S(2)}) copy-start(bf16[1,128,2048]{2,1,0:T(8,128)(2,1)S(1)} %collective-permute-done.3) | copy-start | bytes 1572868
  43.6 81.5 %copy-start.10 = (bf16[1,1024,256]{2,1,0:T(8,128)(2,1)}, bf16[1,1024,256]{2,1,0:T(8,128)(2,1)S(1)}, u32[]{:S(2)}) copy-start(bf16[1,1024,256]{2,1,0:T(8,128)(2,1)S(1)} %collective-permute-done.1) | copy-start | bytes 1572868
  125.2 10.4 %copy-start.6 = (bf16[1,2048,256]{2,1,0:T(8,128)(2,1)S(1)}, bf16[1,2048,256]{2,1,0:T(8,128)(2,1)}, u32[]{:S(2)}) copy-start(bf16[1,2048,256]{2,1,0:T(8,128)(2,1)} %param.23) | copy-start | bytes 3145732
  125.2 10.4 %copy-start.7 = (bf16[1,2048,256]{2,1,0:T(8,128)(2,1)S(1)}, bf16[1,2048,256]{2,1,0:T(8,128)(2,1)}, u32[]{:S(2)}) copy-start(bf16[1,2048,256]{2,1,0:T(8,128)(2,1)} %param.22) | copy-start | bytes 3145732
  125.2 95.9 %all-to-all-start.2 = ((bf16[64,24,2048]{2,1,0:T(8,128)(2,1)}), bf16[64,24,2048]{2,1,0:T(8,128)(2,1)}, u32[]{:S(2)}, u32[]{:S(2)}) async-start(bf16[64,24,2048]{2,1,0:T(8,128)(2,1)} %fusion), calls=%async_computation.2 | async-start | bytes 12582912 | tf_op jit(solution)/shard_map/all_to_all | solution.py:129
  134.0 16.1 %all-gather.5.cloned.1.call-start = ((), (), s32[]{:S(2)}) async-start(), calls=%async_computation.4 | async-start | bytes 1572864 | tf_op jit(solution)/shard_map/all_gather | solution.py:34
  134.8 30.7 %all-gather.7.cloned.1.call-start = ((), (), s32[]{:S(2)}) async-start(), calls=%async_computation.5 | async-start | bytes 1572864 | tf_op jit(solution)/shard_map/all_gather | solution.py:34
  138.3 11.8 %copy-start.3 = (f32[1,2048,256]{2,1,0:T(8,128)S(1)}, f32[1,2048,256]{2,1,0:T(8,128)}, u32[]{:S(2)}) copy-start(f32[1,2048,256]{2,1,0:T(8,128)} %param.20) | copy-start | bytes 6291460
  221.1 148.3 %all-to-all-start.1 = ((bf16[64,24,2048]{2,1,0:T(8,128)(2,1)}), bf16[64,24,2048]{2,1,0:T(8,128)(2,1)}, u32[]{:S(2)}, u32[]{:S(2)}) async-start(bf16[64,24,2048]{2,1,0:T(8,128)(2,1)} %bitcast.129), calls=%async_computation.1 | async-start | bytes 12582912 | tf_op jit(solution)/shard_map/all_to_all | solution.py:152
  230.3 274.5 %all-gather.9.cloned.1.call-start = ((), (), s32[]{:S(2)}) async-start(), calls=%async_computation.6 | async-start | bytes 3145728 | tf_op jit(solution)/shard_map/all_gather | solution.py:34
  231.6 92.8 %collective-permute-start.4 = (bf16[2,1024,256]{2,1,0:T(8,128)(2,1)S(1)}, bf16[2,1024,256]{2,1,0:T(8,128)(2,1)S(1)}, u32[]{:S(2)}, u32[]{:S(2)}) collective-permute-start(bf16[2,1024,256]{2,1,0:T(8,128)(2,1)S(1)} %constant_dynamic-slice_fusion.1), channel_id=1, source_target_pairs={{0,48},{1,49},{2,50},{3,51},{4,52},{5,53},{6,54},{7,55},{8,56},{9,... | collective-permute-start | bytes 3145736 | tf_op jit(solution)/shard_map/ppermute | solution.py:17
  324.4 23.3 %collective-permute-start.5 = (bf16[2,1024,256]{2,1,0:T(8,128)(2,1)S(1)}, bf16[2,1024,256]{2,1,0:T(8,128)(2,1)}, u32[]{:S(2)}, u32[]{:S(2)}) collective-permute-start(bf16[2,1024,256]{2,1,0:T(8,128)(2,1)S(1)} %collective-permute-done.4), channel_id=1, source_target_pairs={{0,48},{1,49},{2,50},{3,51},{4,52},{5,53},{6,54},{7,55},{8,56},{9,... | collective-permute-start | bytes 3145736 | tf_op jit(solution)/shard_map/ppermute | solution.py:17
  347.7 157.1 %all-reduce.3.cloned.1.call-start = ((), (), s32[]{:S(2)}) async-start(), calls=%async_computation.8 | async-start | bytes 8388608 | tf_op jit(solution)/shard_map/psum | solution.py:159
  348.0 6.7 %copy-start.4 = (f32[1,256,2048]{2,1,0:T(8,128)S(1)}, f32[1,256,2048]{2,1,0:T(8,128)}, u32[]{:S(2)}) copy-start(f32[1,256,2048]{2,1,0:T(8,128)} %param.21) | copy-start | bytes 6291460
  348.0 6.7 %copy-start.5 = (bf16[1,256,2048]{2,1,0:T(8,128)(2,1)S(1)}, bf16[1,256,2048]{2,1,0:T(8,128)(2,1)}, u32[]{:S(2)}) copy-start(bf16[1,256,2048]{2,1,0:T(8,128)(2,1)} %all-gather.7.cloned.1.call-done) | copy-start | bytes 3145732
  348.0 6.7 %copy-start.8 = (f32[1536,256]{1,0:T(8,128)S(1)}, f32[1536,256]{1,0:T(8,128)}, u32[]{:S(2)}) copy-start(f32[1536,256]{1,0:T(8,128)} %fusion.29) | copy-start | bytes 4718596
  348.0 12.3 %slice-start = ((s8[6291456]{0:T(1024)(128)(4,1)}), s8[4194304]{0:T(1024)(128)(4,1)S(1)}, s32[]{:S(2)}) async-start(s8[6291456]{0:T(1024)(128)(4,1)} %bitcast.133), calls=%async_computation.9 | async-start | bytes 8388608
  354.7 5.6 %slice-start.1 = ((s8[6291456]{0:T(1024)(128)(4,1)}), s8[2097152]{0:T(1024)(128)(4,1)S(1)}, s32[]{:S(2)}) async-start(s8[6291456]{0:T(1024)(128)(4,1)} %bitcast.133), calls=%async_computation.10 | async-start | bytes 4194304
  369.4 164.6 %all-to-all-start.3 = ((bf16[64,24,2048]{2,1,0:T(8,128)(2,1)}), bf16[64,24,2048]{2,1,0:T(8,128)(2,1)}, u32[]{:S(2)}, u32[]{:S(2)}) async-start(bf16[64,24,2048]{2,1,0:T(8,128)(2,1)} %bitcast.128), calls=%async_computation.3 | async-start | bytes 12582912 | tf_op jit(solution)/shard_map/all_to_all | solution.py:155
  384.9 137.9 %all-gather.11.cloned.1.call-start = ((), (), s32[]{:S(2)}) async-start(), calls=%async_computation.7 | async-start | bytes 3145728 | tf_op jit(solution)/shard_map/all_gather | solution.py:34
  386.4 93.9 %collective-permute-start.6 = (bf16[2,128,2048]{2,1,0:T(8,128)(2,1)S(1)}, bf16[2,128,2048]{2,1,0:T(8,128)(2,1)S(1)}, u32[]{:S(2)}, u32[]{:S(2)}) collective-permute-start(bf16[2,128,2048]{2,1,0:T(8,128)(2,1)S(1)} %constant_dynamic-slice_fusion), channel_id=1, source_target_pairs={{0,48},{1,49},{2,50},{3,51},{4,52},{5,53},{6,54},{7,55},{8,56},{9,... | collective-permute-start | bytes 3145736 | tf_op jit(solution)/shard_map/ppermute | solution.py:17
  480.2 23.3 %collective-permute-start.7 = (bf16[2,128,2048]{2,1,0:T(8,128)(2,1)S(1)}, bf16[2,128,2048]{2,1,0:T(8,128)(2,1)}, u32[]{:S(2)}, u32[]{:S(2)}) collective-permute-start(bf16[2,128,2048]{2,1,0:T(8,128)(2,1)S(1)} %collective-permute-done.6), channel_id=1, source_target_pairs={{0,48},{1,49},{2,50},{3,51},{4,52},{5,53},{6,54},{7,55},{8,56},{9,... | collective-permute-start | bytes 3145736 | tf_op jit(solution)/shard_map/ppermute | solution.py:17
  534.0 4.6 copy-start.1
Sparse Core Ops, SparseCore 0:
  137.1 12.9 all-gather.4
  152.3 13.0 all-gather.6
  347.8 19.6 all-gather.8
  370.6 35.2 all-reduce.2
  503.7 19.1 all-gather.10

commit v9 on v6

--- a/solution.py
+++ b/solution.py
@@ -22,7 +22,13 @@
     step = lax.axis_size("expert") // 4
     here = lax.axis_index("dp")
     halves = tuple(
-        lax.dynamic_slice_in_dim(g, here * (g.shape[1] // ndp), g.shape[1] // ndp, 1)
+        jnp.stack(
+            [
+                lax.dynamic_slice_in_dim(a, here * (a.shape[0] // ndp), a.shape[0] // ndp, 0)
+                .astype(jnp.bfloat16)
+                for a in g
+            ]
+        )
         for g in groups
     )
     moved = relay(halves, step)
@@ -76,43 +82,33 @@
     position = jnp.sum((jnp.cumsum(onehot, 0) - 1) * onehot, 1)
     limit = jnp.sum(onehot * capacity[None, :], 1)
     kept = position < limit
-    npairs = count * topk
-    slot = jnp.where(kept, flat_routes * slots + position, experts * slots)
-    pair_of = (
-        jnp.full((experts * slots + 1,), npairs, jnp.int32)
-        .at[slot]
-        .set(jnp.arange(npairs, dtype=jnp.int32))[:-1]
-        .reshape(experts, slots)
-    )
     held = jnp.take(layout, partner, axis=0)
     target_expert = held // GROUP
-    send_pair = jnp.take(pair_of, target_expert, axis=0)
-    send_tok = jnp.where(send_pair < npairs, send_pair // topk, count)
-    gate_of = jnp.concatenate([gates.reshape(-1), jnp.zeros((1,), gates.dtype)])
-    pick = (send_tok[:, :, None] == jnp.arange(count, dtype=jnp.int32)[None, None, :]).astype(
-        jnp.bfloat16
-    )
-    pick = pick.reshape(nexp * slots, count)
+    row_expert = jnp.repeat(target_expert, slots)
+    row_pos = jnp.tile(jnp.arange(slots, dtype=jnp.int32), nexp)
+    owns = (
+        kept[:, None]
+        & (flat_routes[:, None] == row_expert[None, :])
+        & (position[:, None] == row_pos[None, :])
+    )
+    owns_tok = owns.reshape(count, topk, nexp * slots).any(axis=1).astype(jnp.bfloat16)
+    gate_row = jnp.sum(jnp.where(owns, gates.reshape(-1)[:, None], 0.0), axis=0)
+    pick_dims = (((0,), (0,)), ((), ()))
     send_x = (
-        jnp.dot(pick, tokens, preferred_element_type=jnp.float32)
+        lax.dot_general(owns_tok, tokens, pick_dims, preferred_element_type=jnp.float32)
         .astype(jnp.bfloat16)
         .reshape(nexp, slots, width)
     )
     send_g = (
-        jnp.take(gate_of, send_pair)[:, :, None]
-        * jnp.dot(pick, cotangent, preferred_element_type=jnp.float32)
+        gate_row.reshape(nexp, slots)[:, :, None]
+        * lax.dot_general(owns_tok, cotangent, pick_dims, preferred_element_type=jnp.float32)
         .astype(jnp.bfloat16)
         .astype(jnp.float32)
         .reshape(nexp, slots, width)
     ).astype(jnp.bfloat16)
     weight_in, weight_out = (w_in[0], w_out[0])
     first_in, second_in, first_out, second_out = (m_in[0], v_in[0], m_out[0], v_out[0])
-    halves = migrate(
-        (
-            jnp.stack([weight_in.astype(jnp.bfloat16), first_in, second_in]),
-            jnp.stack([weight_out.astype(jnp.bfloat16), first_out, second_out]),
-        )
-    )
+    halves = migrate(((weight_in, first_in, second_in), (weight_out, first_out, second_out)))
     send_x, send_g, halves = lax.optimization_barrier((send_x, send_g, halves))
     group_in, group_out = join(halves)
     other = (group_in[0], group_out[0], group_in[1], group_in[2], group_out[1], group_out[2])
@@ -160,15 +156,7 @@
     grad_in, grad_out = lax.psum((grad_in, grad_out), "dp")
     new_w_in, new_m_in, new_v_in = adamw(weight_in, first_in, second_in, grad_in)
     new_w_out, new_m_out, new_v_out = adamw(weight_out, first_out, second_out, grad_out)
-    row_expert = jnp.repeat(target_expert, slots)
-    row_pos = jnp.tile(jnp.arange(slots, dtype=jnp.int32), nexp)
-    owns = (
-        kept[:, None]
-        & (flat_routes[:, None] == row_expert[None, :])
-        & (position[:, None] == row_pos[None, :])
-    )
     owns_pair = owns.astype(jnp.bfloat16)
-    owns_tok = owns.reshape(count, topk, nexp * slots).any(axis=1).astype(jnp.bfloat16)
     out_vals = jnp.dot(
         owns_pair, back_part.reshape(-1, width), preferred_element_type=jnp.float32
     )

time: 473 us -> 472 us (level)
  waiting for transfers between devices: 318 us -> 329 us
  local copies, waits for them, and re-layouts: 15.9 us -> 8.81 us
  other arithmetic: 24.2 us -> 17.9 us
    ppermute x4, waiting for transfers between devices: 38.5 us -> 49.5 us  [relay(): return lax.ppermute(block, ('dp', 'expert'), route)]
    gather x3 -> x0, local copies, waits for them, and re-layouts: 10.2 us -> none  [the longest x2 9.56 us: body(): jnp.take(gate_of, send_pair)[:, :, None]]
  transfers between devices with their start and end apart: 11 -> 11, of which waited for: 9 -> 9; matrix products, arithmetic and copies ran while one was open for 17% -> 15% of each run, Pallas kernels for 0% -> 0%
where the time goes in v9:
time: 472 us; the launch traced here: 468 us
  waiting for transfers between devices  329 us (70%)
  matrix products  53.2 us (11%)
  starting transfers between devices  44.8 us (9%)
  other arithmetic  17.9 us (4%)
  between operations  14.8 us (3%)
  local copies, waits for them, and re-layouts  8.81 us (2%)
    all_to_all x1, waiting for transfers between devices, body(): lax.all_to_all(send_x, 'expert', split_axis=0, concat_axis=0, tiled=True)  82.6 us
    all_to_all x1, waiting for transfers between devices, body(): lax.all_to_all(xpart.reshape(nexp, slots, width), 'expert', split_axis=0,...  65.8 us
    all_to_all x1, waiting for transfers between devices, body(): lax.all_to_all(send_g, 'expert', split_axis=0, concat_axis=0, tiled=True)  61.1 us
    all_to_all x1, waiting for transfers between devices, body(): lax.all_to_all(part.reshape(nexp, slots, width), 'expert', split_axis=0,...  58 us
    ppermute x4, waiting for transfers between devices, relay(): return lax.ppermute(block, ('dp', 'expert'), route)  49.5 us
    all_to_all x1, starting transfers between devices, body(): lax.all_to_all(send_x, 'expert', split_axis=0, concat_axis=0, tiled=True)  11.1 us
    all_to_all x1, starting transfers between devices, body(): lax.all_to_all(xpart.reshape(nexp, slots, width), 'expert', split_axis=0,...  10.6 us
    all_gather x2, waiting for transfers between devices, join(): return tuple((lax.all_gather(m, 'dp', axis=1, tiled=True) for m in moved))  10.6 us
  transfers between devices with their start and end apart: 11, of which 9 were waited for; matrix products, arithmetic and copies ran while one was open for 15% of the time, Pallas kernels for 0%

profile of v9, /device:TPU:50, one launch (start us, length us, event | category | flops | bytes accessed | tf_op | source)
XLA Modules:
  0.0 468.4 jit_solution(18024756657501141119)
XLA Ops:
  7.2 1.1 constant_dynamic-slice_fusion.3
  8.3 1.5 dynamic-slice_convert_fusion.1
  9.8 1.3 pad_maximum_fusion
  11.1 1.3 collective-permute-start
  12.5 1.4 dynamic-slice_convert_fusion
  13.9 1.3 pad_maximum_fusion.1
  15.2 0.7 collective-permute-start.2
  16.2 0.1 eq.85
  16.3 0.6 reduce-window.6
  16.9 0.2 slice_reduce_fusion
  17.6 0.8 gather_fusion
  19.0 0.1 broadcast_in_dim.55
  19.1 0.6 select_reduce_fusion
  19.7 12.1 %collective-permute-done = bf16[3,1024,256]{2,1,0:T(8,128)(2,1)} collective-permute-done((bf16[3,1024,256]{2,1,0:T(8,128)(2,1)}, bf16[3,1024,256]{2,1,0:T(8,128)(2,1)}, u32[]{:S(2)}, u32[]{:S(2)}) %collective-permute-start) | collective-permute-done | bytes 1572896 | tf_op jit(solution)/shard_map/ppermute | solution.py:17
  31.9 1.3 collective-permute-start.1
  33.1 15.6 %collective-permute-done.2 = bf16[3,128,2048]{2,1,0:T(8,128)(2,1)} collective-permute-done((bf16[3,128,2048]{2,1,0:T(8,128)(2,1)}, bf16[3,128,2048]{2,1,0:T(8,128)(2,1)}, u32[]{:S(2)}, u32[]{:S(2)}) %collective-permute-start.2) | collective-permute-done | bytes 1572896 | tf_op jit(solution)/shard_map/ppermute | solution.py:17
  48.7 1.3 collective-permute-start.3
  50.0 0.5 fusion.33
  50.6 1.8 convolution_convert_fusion.2
  52.4 4.5 convolution_convert_fusion.3
  56.9 3.7 fusion
  60.6 4.8 %collective-permute-done.1 = bf16[3,1024,256]{2,1,0:T(8,128)(2,1)S(1)} collective-permute-done((bf16[3,1024,256]{2,1,0:T(8,128)(2,1)}, bf16[3,1024,256]{2,1,0:T(8,128)(2,1)S(1)}, u32[]{:S(2)}, u32[]{:S(2)}) %collective-permute-start.1) | collective-permute-done | bytes 1572896 | tf_op jit(solution)/shard_map/ppermute | solution.py:17
  65.5 17.0 %collective-permute-done.3 = bf16[3,128,2048]{2,1,0:T(8,128)(2,1)} collective-permute-done((bf16[3,128,2048]{2,1,0:T(8,128)(2,1)}, bf16[3,128,2048]{2,1,0:T(8,128)(2,1)}, u32[]{:S(2)}, u32[]{:S(2)}) %collective-permute-start.3) | collective-permute-done | bytes 1572896 | tf_op jit(solution)/shard_map/ppermute | solution.py:17
  82.4 11.1 %all-to-all-start = ((bf16[64,24,2048]{2,1,0:T(8,128)(2,1)}), bf16[64,24,2048]{2,1,0:T(8,128)(2,1)}, u32[]{:S(2)}, u32[]{:S(2)}) async-start(bf16[64,24,2048]{2,1,0:T(8,128)(2,1)} %bitcast.121), calls=%async_computation | async-start | bytes 12582912 | tf_op jit(solution)/shard_map/all_to_all | solution.py:124
  93.6 0.7 all-gather.3.cloned.1.call-update
  94.3 82.6 %all-to-all-done = bf16[64,24,2048]{2,1,0:T(8,128)(2,1)} async-done(((bf16[64,24,2048]{2,1,0:T(8,128)(2,1)}), bf16[64,24,2048]{2,1,0:T(8,128)(2,1)}, u32[]{:S(2)}, u32[]{:S(2)}) %all-to-all-start) | async-done | bytes 6291488 | tf_op jit(solution)/shard_map/all_to_all | solution.py:124
  176.9 8.7 %all-to-all-start.2 = ((bf16[64,24,2048]{2,1,0:T(8,128)(2,1)}), bf16[64,24,2048]{2,1,0:T(8,128)(2,1)}, u32[]{:S(2)}, u32[]{:S(2)}) async-start(bf16[64,24,2048]{2,1,0:T(8,128)(2,1)} %fusion), calls=%async_computation.2 | async-start | bytes 12582912 | tf_op jit(solution)/shard_map/all_to_all | solution.py:125
  185.6 0.2 all-gather.5.cloned.1.call-start
  185.8 0.5 all-gather.5.cloned.1.call-update
  186.3 0.6 dynamic-slice.8
  187.6 6.0 %fusion.29 = f32[1536,256]{1,0:T(8,128)} fusion(bf16[1536,2048]{1,0:T(8,128)(2,1)} %bitcast.3, f32[1,2048,256]{2,1,0:T(8,128)S(1)} %copy-done.3, bf16[3,2048,256]{2,1,0:T(8,128)(2,1)} %all-gather.3.cloned.1.call-done, pred[]{:T(512)S(6)} %ne.20), kind=kOutput, calls=%fused_computation.58 | convolution fusion | flops 1611661312 | bytes 11010049 | tf_op jit(solution)/shard_map/dot_general | solution.py:131
  193.6 10.6 %all-gather.5.cloned.1.call-done = bf16[3,256,2048]{2,1,0:T(8,128)(2,1)} async-done(((bf16[3,128,2048]{2,1,0:T(8,128)(2,1)}), bf16[3,256,2048]{2,1,0:T(8,128)(2,1)}) %all-gather.5.cloned.1.call-update) | async-done | bytes 3145744 | tf_op jit(solution)/shard_map/all_gather | solution.py:40
  204.2 6.3 %convolution_convert_fusion.1 = bf16[1536,2048]{1,0:T(8,128)(2,1)} fusion(f32[1,256,2048]{2,1,0:T(8,128)} %param.21, bf16[3,256,2048]{2,1,0:T(8,128)(2,1)} %all-gather.5.cloned.1.call-done, pred[]{:T(512)S(6)} %ne.20, f32[1536,256]{1,0:T(8,128)} %fusion.29), kind=kOutput, calls=%fused_computation.4 | convolution fusion | flops 1618345984 | bytes 11010049 | tf_op jit(solution)/shard_map/dot_general | solution.py:134
  210.5 61.1 %all-to-all-done.2 = bf16[64,24,2048]{2,1,0:T(8,128)(2,1)} async-done(((bf16[64,24,2048]{2,1,0:T(8,128)(2,1)}), bf16[64,24,2048]{2,1,0:T(8,128)(2,1)}, u32[]{:S(2)}, u32[]{:S(2)}) %all-to-all-start.2) | async-done | bytes 6291488 | tf_op jit(solution)/shard_map/all_to_all | solution.py:125
  271.6 9.5 %all-to-all-start.1 = ((bf16[64,24,2048]{2,1,0:T(8,128)(2,1)}), bf16[64,24,2048]{2,1,0:T(8,128)(2,1)}, u32[]{:S(2)}, u32[]{:S(2)}) async-start(bf16[64,24,2048]{2,1,0:T(8,128)(2,1)} %bitcast.120), calls=%async_computation.1 | async-start | bytes 12582912 | tf_op jit(solution)/shard_map/all_to_all | solution.py:149
  281.2 6.6 %fusion.42 = f32[256,2048]{1,0:T(8,128)} fusion(bf16[1536,2048]{1,0:T(8,128)(2,1)} %bitcast.11, f32[1536,256]{1,0:T(8,128)} %fusion.29), kind=kOutput, calls=%fused_computation.90 | convolution fusion | flops 1614151680 | bytes 9961472 | tf_op jit(solution)/shard_map/dot_general | solution.py:145
  287.9 5.7 %fusion.15 = bf16[1536,256]{1,0:T(8,128)(2,1)S(1)} fusion(f32[1536,256]{1,0:T(8,128)S(1)} %copy-done.7, bf16[1536,2048]{1,0:T(8,128)(2,1)} %bitcast.11, f32[1,256,2048]{2,1,0:T(8,128)S(1)} %copy-done.4, bf16[3,256,2048]{2,1,0:T(8,128)(2,1)} %all-gather.5.cloned.1.call-done, pred[]{:T(512)S(6)} %ne.20), kind=kOutput, calls=%fused_computation.37 | convolution fusion | flops 1619525632 | bytes 11796481 | tf_op jit(solution)/shard_map/dot_general | solution.py:135
  293.6 0.9 copy-done.13
  294.5 6.0 %fusion.43 = f32[2048,256]{1,0:T(8,128)} fusion(bf16[1536,2048]{1,0:T(8,128)(2,1)} %bitcast.3, bf16[1536,256]{1,0:T(8,128)(2,1)S(1)} %fusion.15), kind=kOutput, calls=%fused_computation.91 | convolution fusion | flops 1610612736 | bytes 9175040 | tf_op jit(solution)/shard_map/dot_general | solution.py:142
  300.5 5.9 %convolution_convert_fusion = bf16[1536,2048]{1,0:T(8,128)(2,1)} fusion(bf16[1536,256]{1,0:T(8,128)(2,1)} %copy-done.13, f32[1,2048,256]{2,1,0:T(8,128)S(1)} %copy-done.3, bf16[3,2048,256]{2,1,0:T(8,128)(2,1)} %all-gather.3.cloned.1.call-done, pred[]{:T(512)S(6)} %ne.20), kind=kOutput, calls=%fused_computation.3 | convolution fusion | flops 1614807040 | bytes 10223617 | tf_op jit(solution)/shard_map/dot_general | solution.py:139
  306.4 58.0 %all-to-all-done.1 = bf16[64,24,2048]{2,1,0:T(8,128)(2,1)} async-done(((bf16[64,24,2048]{2,1,0:T(8,128)(2,1)}), bf16[64,24,2048]{2,1,0:T(8,128)(2,1)}, u32[]{:S(2)}, u32[]{:S(2)}) %all-to-all-start.1) | async-done | bytes 6291488 | tf_op jit(solution)/shard_map/all_to_all | solution.py:149
  364.4 10.6 %all-to-all-start.3 = ((bf16[64,24,2048]{2,1,0:T(8,128)(2,1)}), bf16[64,24,2048]{2,1,0:T(8,128)(2,1)}, u32[]{:S(2)}, u32[]{:S(2)}) async-start(bf16[64,24,2048]{2,1,0:T(8,128)(2,1)} %bitcast.119), calls=%async_computation.3 | async-start | bytes 12582912 | tf_op jit(solution)/shard_map/all_to_all | solution.py:152
  375.1 5.9 %fusion.21 = (bf16[1,2048,256]{2,1,0:T(8,128)(2,1)}, f32[1,2048,256]{2,1,0:T(8,128)}, bf16[1,2048,256]{2,1,0:T(8,128)(2,1)}) fusion(f32[2048,256]{1,0:T(8,128)} %get-tuple-element.29, bf16[1,2048,256]{2,1,0:T(8,128)(2,1)} %param.23, bf16[3,2048,256]{2,1,0:T(8,128)(2,1)} %all-gather.3.cloned.1.call-done, pred[]{:T(512)S(6)} %ne.20, ...), kind=kLoop, calls=%fused_computation.48 | loop fusion | flops 12058624 | bytes 13631489 | tf_op jit(solution)/shard_map/broadcast_in_dim | solution.py:175
  381.0 0.9 copy-done.12
  381.9 3.8 fusion.22
  385.7 5.7 %fusion.16 = bf16[128,2048]{1,0:T(8,128)(2,1)} fusion(bf16[1536,2048,1]{1,0,2:T(8,128)(2,1)} %bitcast.10, f32[128,2]{0,1:T(2,128)S(1)} %copy-done.17, s32[1536]{0:T(1024)S(1)} %eq.94, s32[128,2]{0,1:T(2,128)S(1)} %copy.31, s32[1536]{0:T(1024)S(1)} %eq.90, s32[128,2]{0,1:T(2,128)S(1)} %copy-done.16, pred[128,2]{0,1:T(4,128)(4,1)S(1)} %copy.30), kind=kOutput, calls=%fused_computation.43 | convolution fusion | flops 1612972032 | bytes 6831360 | tf_op jit(solution)/shard_map/dot_general | solution.py:160
  391.4 65.8 %all-to-all-done.3 = bf16[64,24,2048]{2,1,0:T(8,128)(2,1)} async-done(((bf16[64,24,2048]{2,1,0:T(8,128)(2,1)}), bf16[64,24,2048]{2,1,0:T(8,128)(2,1)}, u32[]{:S(2)}, u32[]{:S(2)}) %all-to-all-start.3) | async-done | bytes 6291488 | tf_op jit(solution)/shard_map/all_to_all | solution.py:152
  457.2 4.6 convolution_convert_fusion.4
  (65 shorter events, 1.6 us)
Async XLA Ops:
  7.2 43.4 %copy-start = (bf16[128,2048]{1,0:T(8,128)(2,1)S(1)}, bf16[128,2048]{1,0:T(8,128)(2,1)}, u32[]{:S(2)}) copy-start(bf16[128,2048]{1,0:T(8,128)(2,1)} %param.14) | copy-start | bytes 1572868
  9.8 2.6 copy-start.10
  9.8 2.7 copy-start.8
  11.1 20.7 %collective-permute-start = (bf16[3,1024,256]{2,1,0:T(8,128)(2,1)}, bf16[3,1024,256]{2,1,0:T(8,128)(2,1)}, u32[]{:S(2)}, u32[]{:S(2)}) collective-permute-start(bf16[3,1024,256]{2,1,0:T(8,128)(2,1)} %pad_maximum_fusion), channel_id=1, source_target_pairs={{0,16},{1,17},{2,18},{3,19},{4,20},{5,21},{6,22},{7,23},{8,24},{9,... | collective-permute-start | bytes 4718600 | tf_op jit(solution)/shard_map/ppermute | solution.py:17
  13.8 2.1 copy-start.16
  13.8 3.3 copy-start.18
  13.9 3.7 copy-start.19
  13.9 3.7 copy-start.2
  13.9 4.9 %copy-start.17 = (f32[128,2]{0,1:T(2,128)S(1)}, f32[128,2]{0,1:T(2,128)}, u32[]{:S(2)}) copy-start(f32[128,2]{0,1:T(2,128)} %param.16) | copy-start | bytes 3076
  15.2 33.5 %collective-permute-start.2 = (bf16[3,128,2048]{2,1,0:T(8,128)(2,1)}, bf16[3,128,2048]{2,1,0:T(8,128)(2,1)}, u32[]{:S(2)}, u32[]{:S(2)}) collective-permute-start(bf16[3,128,2048]{2,1,0:T(8,128)(2,1)} %pad_maximum_fusion.1), channel_id=1, source_target_pairs={{0,16},{1,17},{2,18},{3,19},{4,20},{5,21},{6,22},{7,23},{8,24},{9,... | collective-permute-start | bytes 4718600 | tf_op jit(solution)/shard_map/ppermute | solution.py:17
  31.9 33.6 %collective-permute-start.1 = (bf16[3,1024,256]{2,1,0:T(8,128)(2,1)}, bf16[3,1024,256]{2,1,0:T(8,128)(2,1)S(1)}, u32[]{:S(2)}, u32[]{:S(2)}) collective-permute-start(bf16[3,1024,256]{2,1,0:T(8,128)(2,1)} %collective-permute-done), channel_id=1, source_target_pairs={{0,16},{1,17},{2,18},{3,19},{4,20},{5,21},{6,22},{7,23},{8,24},{9,... | collective-permute-start | bytes 4718600 | tf_op jit(solution)/shard_map/ppermute | solution.py:17
  48.7 33.7 %collective-permute-start.3 = (bf16[3,128,2048]{2,1,0:T(8,128)(2,1)}, bf16[3,128,2048]{2,1,0:T(8,128)(2,1)}, u32[]{:S(2)}, u32[]{:S(2)}) collective-permute-start(bf16[3,128,2048]{2,1,0:T(8,128)(2,1)} %collective-permute-done.2), channel_id=1, source_target_pairs={{0,16},{1,17},{2,18},{3,19},{4,20},{5,21},{6,22},{7,23},{8,24},{9,... | collective-permute-start | bytes 4718600 | tf_op jit(solution)/shard_map/ppermute | solution.py:17
  50.6 1.9 copy-start.15
  65.5 17.0 %copy-start.14 = (bf16[3,1024,256]{2,1,0:T(8,128)(2,1)}, bf16[3,1024,256]{2,1,0:T(8,128)(2,1)S(1)}, u32[]{:S(2)}) copy-start(bf16[3,1024,256]{2,1,0:T(8,128)(2,1)S(1)} %collective-permute-done.1) | copy-start | bytes 4718596
  82.4 94.5 %all-to-all-start = ((bf16[64,24,2048]{2,1,0:T(8,128)(2,1)}), bf16[64,24,2048]{2,1,0:T(8,128)(2,1)}, u32[]{:S(2)}, u32[]{:S(2)}) async-start(bf16[64,24,2048]{2,1,0:T(8,128)(2,1)} %bitcast.121), calls=%async_computation | async-start | bytes 12582912 | tf_op jit(solution)/shard_map/all_to_all | solution.py:124
  93.5 94.1 %all-gather.3.cloned.1.call-start = ((), (), s32[]{:S(2)}) async-start(), calls=%async_computation.4 | async-start | bytes 4718592 | tf_op jit(solution)/shard_map/all_gather | solution.py:40
  94.3 93.3 %copy-start.3 = (f32[1,2048,256]{2,1,0:T(8,128)S(1)}, f32[1,2048,256]{2,1,0:T(8,128)}, u32[]{:S(2)}) copy-start(f32[1,2048,256]{2,1,0:T(8,128)} %param.20) | copy-start | bytes 6291460
  176.9 94.7 %all-to-all-start.2 = ((bf16[64,24,2048]{2,1,0:T(8,128)(2,1)}), bf16[64,24,2048]{2,1,0:T(8,128)(2,1)}, u32[]{:S(2)}, u32[]{:S(2)}) async-start(bf16[64,24,2048]{2,1,0:T(8,128)(2,1)} %fusion), calls=%async_computation.2 | async-start | bytes 12582912 | tf_op jit(solution)/shard_map/all_to_all | solution.py:125
  185.6 18.6 %all-gather.5.cloned.1.call-start = ((), (), s32[]{:S(2)}) async-start(), calls=%async_computation.5 | async-start | bytes 4718592 | tf_op jit(solution)/shard_map/all_gather | solution.py:40
  271.6 92.8 %all-to-all-start.1 = ((bf16[64,24,2048]{2,1,0:T(8,128)(2,1)}), bf16[64,24,2048]{2,1,0:T(8,128)(2,1)}, u32[]{:S(2)}, u32[]{:S(2)}) async-start(bf16[64,24,2048]{2,1,0:T(8,128)(2,1)} %bitcast.120), calls=%async_computation.1 | async-start | bytes 12582912 | tf_op jit(solution)/shard_map/all_to_all | solution.py:149
  281.2 93.9 %all-reduce.3.cloned.1.call-start = ((), (), s32[]{:S(2)}) async-start(), calls=%async_computation.6 | async-start | bytes 8388608 | tf_op jit(solution)/shard_map/psum | solution.py:156
  281.2 6.6 %copy-start.4 = (f32[1,256,2048]{2,1,0:T(8,128)S(1)}, f32[1,256,2048]{2,1,0:T(8,128)}, u32[]{:S(2)}) copy-start(f32[1,256,2048]{2,1,0:T(8,128)} %param.21) | copy-start | bytes 6291460
  281.2 6.6 %copy-start.7 = (f32[1536,256]{1,0:T(8,128)S(1)}, f32[1536,256]{1,0:T(8,128)}, u32[]{:S(2)}) copy-start(f32[1536,256]{1,0:T(8,128)} %fusion.29) | copy-start | bytes 4718596
  293.6 0.9 copy-start.13
  364.4 92.8 %all-to-all-start.3 = ((bf16[64,24,2048]{2,1,0:T(8,128)(2,1)}), bf16[64,24,2048]{2,1,0:T(8,128)(2,1)}, u32[]{:S(2)}, u32[]{:S(2)}) async-start(bf16[64,24,2048]{2,1,0:T(8,128)(2,1)} %bitcast.119), calls=%async_computation.3 | async-start | bytes 12582912 | tf_op jit(solution)/shard_map/all_to_all | solution.py:152
  375.1 5.9 %copy-start.5 = (f32[1,256,2048]{2,1,0:T(8,128)S(1)}, f32[1,256,2048]{2,1,0:T(8,128)}, u32[]{:S(2)}) copy-start(f32[1,256,2048]{2,1,0:T(8,128)} %param.21) | copy-start | bytes 6291460
  375.1 5.9 %copy-start.6 = (bf16[3,256,2048]{2,1,0:T(8,128)(2,1)S(1)}, bf16[3,256,2048]{2,1,0:T(8,128)(2,1)}, u32[]{:S(2)}) copy-start(bf16[3,256,2048]{2,1,0:T(8,128)(2,1)} %all-gather.5.cloned.1.call-done) | copy-start | bytes 9437188
  375.1 5.9 %copy-start.9 = (bf16[1,256,2048]{2,1,0:T(8,128)(2,1)S(1)}, bf16[1,256,2048]{2,1,0:T(8,128)(2,1)}, u32[]{:S(2)}) copy-start(bf16[1,256,2048]{2,1,0:T(8,128)(2,1)} %param.25) | copy-start | bytes 3145732
  375.1 5.9 %copy-start.11 = (bf16[1,256,2048]{2,1,0:T(8,128)(2,1)S(1)}, bf16[1,256,2048]{2,1,0:T(8,128)(2,1)}, u32[]{:S(2)}) copy-start(bf16[1,256,2048]{2,1,0:T(8,128)(2,1)} %param.24) | copy-start | bytes 3145732
  375.1 6.8 %copy-start.12 = (f32[256,2048]{1,0:T(8,128)S(1)}, f32[256,2048]{1,0:T(8,128)}, u32[]{:S(2)}) copy-start(f32[256,2048]{1,0:T(8,128)} %get-tuple-element.30) | copy-start | bytes 6291460
  457.2 4.6 copy-start.1
Sparse Core Ops, SparseCore 0:
  96.6 16.0 all-gather.2
  188.1 16.0 all-gather.4
  300.6 35.1 all-reduce.2
